TPU v7x, 32 devices: a whole 2x2x4 slice. The times are simulated.
32 devices in a mesh: dp: 8 (over z, x), tensor: 4 (over y, core).
Axes of the slice: x: 2, y: 2, z: 4, core: 2. Of those that a mesh axis runs over, the one named last changes fastest.
Arguments:
- tokens: bfloat16 [16384, 768], P(('dp', 'tensor')), may hold values from -6 to 6
- w_query: bfloat16 [768, 768], P(None, 'tensor'), may hold values from -0.3125 to 0.3125
- w_key: bfloat16 [768, 768], P(None, 'tensor'), may hold values from -0.3125 to 0.3125
- w_value: bfloat16 [768, 768], P(None, 'tensor'), may hold values from -0.21875 to 0.21875
- b_query: bfloat16 [768], P('tensor'), may hold values from -3 to 3
- b_value: bfloat16 [768], P('tensor'), may hold values from -3 to 3
- w_output: bfloat16 [768, 768], P('tensor'), may hold values from -0.375 to 0.375
- b_output: bfloat16 [768], replicated, may hold values from -3 to 3
- first_gain: bfloat16 [768], replicated, may hold values from 0.5 to 1.5
- first_shift: bfloat16 [768], replicated, may hold values from -3 to 3
- w_up: bfloat16 [768, 3072], P(None, 'tensor'), may hold values from -0.21875 to 0.21875
- b_up: bfloat16 [3072], P('tensor'), may hold values from -3 to 3
- w_down: bfloat16 [3072, 768], P('tensor'), may hold values from -0.15625 to 0.15625
- b_down: bfloat16 [768], replicated, may hold values from -3 to 3
- second_gain: bfloat16 [768], replicated, may hold values from 0.5 to 1.5
- second_shift: bfloat16 [768], replicated, may hold values from -3 to 3
- cotangent: bfloat16 [16384, 768], P(('dp', 'tensor')), may hold values from -24 to 24, as said below
Outputs:
- layer_out: bfloat16 [16384, 768], P(('dp', 'tensor'))
- grad_tokens: bfloat16 [16384, 768], P(('dp', 'tensor'))
- grad_w_query: float32 [768, 768], P(None, 'tensor')
- grad_w_key: float32 [768, 768], P(None, 'tensor')
- grad_w_value: float32 [768, 768], P(None, 'tensor')
- grad_b_query: float32 [768], P('tensor')
- grad_b_value: float32 [768], P('tensor')
- grad_w_output: float32 [768, 768], P('tensor')
- grad_b_output: float32 [768], replicated
- grad_first_gain: float32 [768], replicated
- grad_first_shift: float32 [768], replicated
- grad_w_up: float32 [768, 3072], P(None, 'tensor')
- grad_b_up: float32 [3072], P('tensor')
- grad_w_down: float32 [3072, 768], P('tensor')
- grad_b_down: float32 [768], replicated
- grad_second_gain: float32 [768], replicated
- grad_second_shift: float32 [768], replicated
Inputs may be any that keep to these rules, and one draw needn't show every extreme that they name: cotangent of the layer's output.
All inputs are finite; a program needn't handle non-finite values.
Results may differ from a plain program's by a relative error of at most 0.013.
The roundings to bfloat16 on the way count: a program that leaves them out, or rounds other values in their place, can miss the bound.
Values may be sent and summed in bfloat16 or wider, within the bound.
No kernel may reach another device: no remote copies, remote signals or barrier semaphores. Data moves between devices by JAX's collectives and lax.ppermute only.
A program may use at most 128 MiB of HBM per device.

v0:
```python
import functools

import jax
import jax.numpy as jnp
from jax import lax
from jax.experimental import pallas as pl
from jax.experimental.pallas import tpu as pltpu
from jax.sharding import PartitionSpec as P

HEAD = 64
SEQ_LEN = 512
BIAS_ROWS = 16
BF = jnp.bfloat16
F32 = jnp.float32
ANY = pl.BlockSpec(memory_space=pl.ANY)
VMEM_BYTES = 26 << 20
BY_B, BY_A, NATURAL, FIRST, SECOND, THIRD, FOURTH, PLACES, SIDE, QUARTERS, SHARD = 0, 4, 8, 12, 16, 18, 22, 24, 28, 29, 33
ALL_VMEM_BYTES = 60 << 20
UNROLL = 1


def dot(left, right, left_dim, right_dim):
    return lax.dot_general(
        left, right, (((left_dim,), (right_dim,)), ((), ())), preferred_element_type=F32
    )


SMALL = pl.CostEstimate(flops=1000, bytes_accessed=1000, transcendentals=0)


def whole(shape):
    return pl.BlockSpec(shape, lambda *_: (0,) * len(shape))


def params(limit=VMEM_BYTES):
    return pltpu.CompilerParams(vmem_limit_bytes=limit)


def cost(flops, moved):
    return pl.CostEstimate(flops=int(20 * flops), bytes_accessed=int(20 * moved), transcendentals=0)


def run(kernel, name, outs, *ops, scratch=(), estimate=SMALL, plan=None):
    specs = [pl.BlockSpec(memory_space=pltpu.VMEM)] * len(ops)
    if plan is not None:
        ops = (plan, *ops)
        specs.insert(0, pl.BlockSpec(memory_space=pltpu.SMEM))
    return pl.pallas_call(
        kernel,
        in_specs=specs,
        out_specs=[pl.BlockSpec(memory_space=pltpu.VMEM)] * len(outs),
        out_shape=[jax.ShapeDtypeStruct(shape, dtype) for shape, dtype in outs],
        scratch_shapes=scratch,
        compiler_params=params(),
        cost_estimate=estimate,
        name=name,
    )(*ops)


def pack_kernel(plan, wq, wk, wv, wo, wu, wd, *refs):
    vectors, refs = refs[:9], refs[9:]
    out, near, up_far, down_far, table, packed, piece, lines, *lists, sem = refs
    local, width = wq.shape
    at = pl.multiple_of(plan[BY_B] * local, local)
    copies = [
        pltpu.make_async_copy(ref, packed.at[pl.ds(i * local, local)], sem.at[0])
        for i, ref in enumerate((wq, wk, wv, wo))
    ]
    copies += [
        pltpu.make_async_copy(ref, line, sem.at[0]) for ref, line in zip(vectors, lists)
    ]
    opposite = pl.multiple_of(plan[QUARTERS + 3] * local, local)
    pieces = [
        pltpu.make_async_copy(ref.at[pl.ds(rows, local)], piece.at[i], sem.at[1])
        for i, (ref, rows) in enumerate(((wu, at), (wu, opposite), (wd, at), (wd, opposite)))
    ]
    for copy in copies:
        copy.start()
    for copy in pieces:
        copy.start()
    packed[4 * local :, :] = jnp.zeros((BIAS_ROWS, width), BF)
    lines[...] = jnp.zeros_like(lines)
    for copy in copies:
        copy.wait()
    bq, bv, bu = lists[:3]
    packed[4 * local : 4 * local + 1, 0:local] = bq[...].reshape(1, local)
    packed[4 * local : 4 * local + 1, local : 2 * local] = bv[...].reshape(1, local)
    packed[4 * local + 1 : 4 * local + 2, :] = bu[...].reshape(1, width)
    outs = [
        pltpu.make_async_copy(
            packed.at[pl.ds(at, local)], near.at[pl.ds(0, local)], sem.at[2]
        ),
        pltpu.make_async_copy(
            packed.at[pl.ds(4 * local, BIAS_ROWS)], near.at[pl.ds(local, BIAS_ROWS)], sem.at[2]
        ),
        pltpu.make_async_copy(packed, out, sem.at[2]),
    ]
    for copy in outs:
        copy.start()
    for i, ref in enumerate(lists[3:]):
        lines[i : i + 1, :] = ref[...].astype(F32).reshape(1, width)
    outs.append(pltpu.make_async_copy(lines, table, sem.at[2]))
    outs[-1].start()
    for copy in pieces:
        copy.wait()
    for i, ref in enumerate((up_far, down_far)):
        for h in range(2):
            part = ref.at[pl.ds(h * local, local)]
            outs.append(pltpu.make_async_copy(piece.at[2 * i + h], part, sem.at[2]))
            outs[-1].start()
    for copy in outs:
        copy.wait()


def pack_weights(plan, w_query, w_key, w_value, w_output, w_up, w_down, vectors):
    local, width = w_output.shape
    shapes = [
        jax.ShapeDtypeStruct((4 * local + BIAS_ROWS, width), BF),
        jax.ShapeDtypeStruct((local + BIAS_ROWS, width), BF),
        *[jax.ShapeDtypeStruct((2 * local, width), BF)] * 2,
        jax.ShapeDtypeStruct((8, width), F32),
    ]
    return pl.pallas_call(
        pack_kernel,
        grid_spec=pltpu.PrefetchScalarGridSpec(
            num_scalar_prefetch=1,
            grid=(1,),
            in_specs=[ANY] * 15,
            out_specs=[ANY] * 5,
            scratch_shapes=[
                pltpu.VMEM(shapes[0].shape, BF),
                pltpu.VMEM((4, local, width), BF),
                pltpu.VMEM(shapes[4].shape, F32),
                *[pltpu.VMEM(v.shape, BF) for v in vectors],
                pltpu.SemaphoreType.DMA((3,)),
            ],
        ),
        out_shape=shapes,
        compiler_params=params(ALL_VMEM_BYTES),
        name="pack_weights",
    )(plan, w_query.T, w_key.T, w_value.T, w_output, w_up, w_down, *vectors)


def join_kernel(base, plan, *refs):
    *pieces, out = refs
    at = 0
    rows = pieces[0].shape[0]
    for ref in pieces:
        if at < 4:
            count = ref.shape[0] // rows
            for i in range(count):
                where = pl.multiple_of(plan[base + at + i] * rows, rows)
                copy_rows(out, where, ref, i * rows, rows)
            at += count
        else:
            out[4 * rows :, :] = ref[...]


def normalize(rows):
    center = rows - jnp.mean(rows, axis=-1, keepdims=True)
    scale = lax.rsqrt(jnp.mean(center * center, axis=-1, keepdims=True) + 1e-12)
    return center * scale, scale


def norm_back(grad, unit, scale):
    return scale * (
        grad
        - jnp.mean(grad, axis=-1, keepdims=True)
        - unit * jnp.mean(grad * unit, axis=-1, keepdims=True)
    )


def by_blocks(rows, body, block=64):
    def step(i, carry):
        body(pl.ds(pl.multiple_of(i * block, block), block))
        return carry

    lax.fori_loop(0, rows // block, step, 0)


def by_halves(rows, body):
    def step(i, carry):
        body(pl.ds(pl.multiple_of(i * (rows // 2), 128), rows // 2))
        return carry

    lax.fori_loop(0, 2, step, 0)


def head_rows(head, local, count):
    return [pl.ds(pl.multiple_of(i * local + head * HEAD, HEAD), HEAD) for i in range(count)]


def attention_kernel(first, last, small, *refs):
    tok, weights, *refs = refs
    if not first:
        part_in, *refs = refs
    if last:
        table, *refs = refs
        qkv, probs, att, bias_up, normed, normed_low, unit, scale, bias, part = refs
    else:
        qkv, probs, att, bias_up, part, bias = refs
    local = att.shape[0]
    body = 4 * local
    rows = weights[body : body + BIAS_ROWS, :].astype(F32)
    bias_up[...] = rows[1:2, :]
    column = jnp.transpose(rows)
    bias[...] = jnp.zeros_like(bias)
    bias[0:local, :] = column[0:local, 0:1]
    bias[2 * local : 3 * local, :] = column[local : 2 * local, 0:1]

    def project(i, carry):
        r = pl.ds(pl.multiple_of(i * local, local), local)
        rows = (dot(weights[r, :], tok[...], 1, 1) + bias[r, :]).astype(BF)
        qkv[r, :] = rows * jnp.where(i == 0, 0.125, 1.0).astype(BF)
        return carry

    lax.fori_loop(0, 3, project, 0, unroll=1 if small else 3)

    def one_head(head, carry):
        spans = head_rows(head, local, 3)
        queries, keys, values = (qkv[span, :] for span in spans)
        scores = dot(keys, queries, 0, 0)
        unnorm = jnp.exp(scores - jnp.max(scores, axis=0, keepdims=True))
        prob = (unnorm * (1.0 / jnp.sum(unnorm, axis=0, keepdims=True))).astype(BF)
        probs[head] = prob
        att[spans[0], :] = dot(values, prob, 1, 0).astype(BF)
        return carry

    lax.fori_loop(0, local // HEAD, one_head, 0, unroll=UNROLL)

    def out_rows(r):
        rows = dot(att[:, r], weights[3 * local : 4 * local, :], 0, 0)
        part[r, :] = rows if first else rows + part_in[r, :]

    by_halves(part.shape[0], out_rows)
    if last:

        def block(r):
            total = part[r, :] + table[0:1, :] + tok[r, :].astype(F32)
            unit_rows, scale_rows = normalize(total)
            unit[r, :] = unit_rows
            scale[r, :] = scale_rows
            rows = unit_rows * table[1:2, :] + table[2:3, :]
            normed[r, :] = rows
            normed_low[r, :] = rows.astype(BF)

        by_blocks(tok.shape[0], block)


def attention(tokens, pack, part=None, table=None, small=False):
    rows, width = tokens.shape
    local = (pack.shape[0] - BIAS_ROWS) // 4
    first, last = part is None, table is not None
    ops = [tokens, pack] + [x for x in (part, table) if x is not None]
    outs = [((3 * local, rows), BF), ((local // HEAD, rows, rows), BF), ((local, rows), BF)]
    outs += [((1, width), F32)]
    if last:
        outs += [((rows, width), F32), ((rows, width), BF), ((rows, width), F32), ((rows, 1), F32)]
    else:
        outs += [((rows, width), F32)]
    return run(
        functools.partial(attention_kernel, first, last, small),
        "attention_last" if last else "attention",
        outs,
        *ops,
        scratch=[pltpu.VMEM((3 * local, 1), F32)] + [pltpu.VMEM((rows, width), F32)] * last,
        estimate=cost(2.5e9, 4e6),
    )


def feed_kernel(last, *refs):
    low, up, down, bias, part_in, *refs = refs
    if last:
        table, cot, act, slope, layer_out, down_low, grad_second, small, part = refs
    else:
        act, slope, part = refs
    rows = dot(low[...], up[...], 1, 0) + bias[...]
    cdf = 0.5 * (1.0 + lax.erf(rows * 0.7071067811865476))
    active = (rows * cdf).astype(BF)
    act[...] = active
    slope[...] = (cdf + (rows * 0.3989422804014327) * jnp.exp(-0.5 * rows * rows)).astype(BF)
    part[...] = part_in[...] + dot(active, down[...], 1, 0)
    if last:
        small[...] = jnp.zeros_like(small)

        def block(r):
            unit2, scale2 = normalize(part[r, :] + table[3:4, :])
            layer_out[r, :] = unit2 * table[4:5, :] + table[5:6, :]
            cots = cot[r, :].astype(F32)
            grad = norm_back(cots * table[4:5, :], unit2, scale2)
            grad_second[r, :] = grad
            down_low[r, :] = grad.astype(BF)
            small[0:1, :] += jnp.sum(grad, axis=0, keepdims=True)
            small[1:2, :] += jnp.sum(cots * unit2, axis=0, keepdims=True)
            small[2:3, :] += jnp.sum(cots, axis=0, keepdims=True)

        by_blocks(low.shape[0], block)


def feed(low, up, down, bias, part, extra=None):
    rows, width = low.shape
    hidden = up.shape[1]
    last = extra is not None
    ops = [low, up, down, bias, part, *(extra or [])]
    outs = [((rows, hidden), BF)] * 2
    if last:
        outs += [((rows, width), F32), ((rows, width), BF), ((rows, width), F32), ((8, width), F32)]
    else:
        outs += [((rows, width), F32)]
    return run(
        functools.partial(feed_kernel, last),
        "feed_last" if last else "feed",
        outs,
        *ops,
        scratch=[pltpu.VMEM((rows, width), F32)] if last else [],
        estimate=cost(2.5e9 if last else 1.5e9, 4e6),
    )


def down_grad_kernel(*refs):
    count = len(refs) // 2
    low = refs[count]
    for act, out in zip(refs[:count], refs[count + 1 :]):

        out[...] = dot(act[...], low[...], 0, 0).astype(BF)


def down_grad(acts, low):
    return run(
        down_grad_kernel,
        "down_grad",
        [((acts[0].shape[1], low.shape[1]), BF)] * len(acts),
        *acts,
        low,
        estimate=cost(1.2e9, 4e6),
    )


def feed_back_kernel(last, *refs):
    slope, down_low, normed_low, grad_in, up, down, *refs = refs
    if last:
        unit, scale, table, grads, bias, grad_first, first_low, small, part = refs
    else:
        grads, bias, part = refs
    grad_up = (dot(down_low[...], down[...], 1, 1) * slope[...].astype(F32)).astype(BF)
    bias[...] = jnp.sum(grad_up.astype(F32), axis=0, keepdims=True)

    def grad_rows(r):
        grads[r, :] = dot(normed_low[:, r], grad_up, 0, 0).astype(BF)

    by_halves(grads.shape[0], grad_rows)
    part[...] = grad_in[...] + dot(grad_up, up[...], 1, 1)
    if last:
        small[...] = jnp.zeros_like(small)

        def block(r):
            grad = part[r, :]
            units = unit[r, :]
            first = norm_back(grad * table[1:2, :], units, scale[r, :])
            grad_first[r, :] = first
            first_low[r, :] = first.astype(BF)
            small[0:1, :] += jnp.sum(first, axis=0, keepdims=True)
            small[1:2, :] += jnp.sum(grad * units, axis=0, keepdims=True)
            small[2:3, :] += jnp.sum(grad, axis=0, keepdims=True)

        by_blocks(part.shape[0], block)


def feed_back(slope, down_low, normed_low, grad_in, up, down, extra=None):
    rows, width = down_low.shape
    hidden = up.shape[1]
    last = extra is not None
    outs = [((width, hidden), BF), ((1, hidden), F32), ((rows, width), F32)]
    if last:
        outs += [((rows, width), BF), ((8, width), F32)]
    return run(
        functools.partial(feed_back_kernel, last),
        "feed_back_last" if last else "feed_back",
        outs,
        slope,
        down_low,
        normed_low,
        grad_in,
        up,
        down,
        *(extra or []),
        scratch=[pltpu.VMEM((rows, width), F32)] if last else [],
        estimate=cost(2.5e9 if last else 2e9, 5e6),
    )


def attention_back_kernel(qkv, probs, first_low, tok, grad_in, weights, grads, bias, out, work):
    local = qkv.shape[0] // 3
    work[3 * local :, :] = dot(weights[3 * local : 4 * local, :], first_low[...], 1, 1).astype(BF)

    def one_head(head, carry):
        spans = head_rows(head, local, 4)
        queries, keys, values = (qkv[span, :] for span in spans[:3])
        grad_att = work[spans[3], :]
        prob = probs[head]
        grad_prob = dot(values, grad_att, 0, 0)
        wide = prob.astype(F32)
        inner = jnp.sum(wide * grad_prob, axis=0, keepdims=True)
        grad_score = (wide * (grad_prob - inner)).astype(BF)
        work[spans[0], :] = (dot(keys, grad_score, 1, 0) * 0.125).astype(BF)
        work[spans[1], :] = dot(queries, grad_score, 1, 1).astype(BF)
        work[spans[2], :] = dot(grad_att, prob, 1, 1).astype(BF)
        return carry

    lax.fori_loop(0, local // HEAD, one_head, 0, unroll=UNROLL)
    joined = work[0 : 3 * local, :]

    def grad_rows(i, carry):
        r = pl.ds(pl.multiple_of(i * local, local), local)
        grads[r, :] = dot(work[r, :], tok[...], 1, 0).astype(BF)
        return carry

    lax.fori_loop(0, 3, grad_rows, 0)
    bias[...] = dot(jnp.ones((8, joined.shape[1]), BF), joined, 1, 1)

    def out_rows(r):
        out[r, :] = grad_in[r, :] + dot(work[0 : 3 * local, r], weights[0 : 3 * local, :], 0, 0)

    by_halves(out.shape[0], out_rows)


def attention_back(saved, first_low, tokens, grad_in, pack):
    qkv, probs, _ = saved
    rows, width = tokens.shape
    joined = qkv.shape[0]
    return run(
        attention_back_kernel,
        "attention_back",
        [((joined, width), BF), ((8, joined), F32), ((rows, width), F32)],
        qkv,
        probs,
        first_low,
        tokens,
        grad_in,
        pack,
        scratch=[pltpu.VMEM((joined // 3 * 4, rows), BF)],
        estimate=cost(3.5e9, 6e6),
    )


def out_grad_kernel(a, b, c, d, low, send, keep):
    for ref, both in ((send, (a, c)), (keep, (b, d))):
        for i, att in enumerate(both):
            ref[i] = dot(att[...], low[...], 1, 0).astype(BF)


def out_grad(atts, low):
    shape = (2, atts[0].shape[0], low.shape[1])
    return run(
        out_grad_kernel, "out_grad", [(shape, BF)] * 2, *atts, low, estimate=cost(6e8, 3e6)
    )


def join(plan, base, *pieces):
    rows = sum(p.shape[0] for p in pieces)
    (out,) = run(
        functools.partial(join_kernel, base), "join", [((rows, pieces[0].shape[1]), BF)], *pieces,
        plan=plan,
    )
    return out


def add_rows(target, to, left, right, at, rows):
    block = next(b for b in (96, 64, 48, 32, 8) if rows % b == 0)

    def body(i, carry):
        here = pl.ds(pl.multiple_of(at + i * block, 8), block)
        there = pl.ds(pl.multiple_of(to + i * block, 8), block)
        total = left[here, :].astype(F32) + right[here, :].astype(F32)
        target[there, :] = total.astype(target.dtype)
        return carry

    lax.fori_loop(0, rows // block, body, 0)


def copy_rows(target, to, source, at, rows):
    block = next(b for b in (48, 40, 32, 24, 8) if rows % b == 0)

    def body(i, carry):
        here = pl.ds(pl.multiple_of(at + i * block, 8), block)
        there = pl.ds(pl.multiple_of(to + i * block, 8), block)
        target[there, :] = source[here, :].astype(target.dtype)
        return carry

    lax.fori_loop(0, rows // block, body, 0)


VECTORS = 16


def send_vectors(value, sent):
    high = value.astype(BF)
    low = (value - high.astype(F32)).astype(BF)
    at = sent.shape[0] - 2 * VECTORS
    sent[at : at + VECTORS, :] = high
    sent[at + VECTORS :, :] = low
    return high.astype(F32) + low.astype(F32)


def got_vectors(got):
    at = got.shape[0] - 2 * VECTORS
    return got[at : at + VECTORS, :].astype(F32) + got[at + VECTORS :, :].astype(F32)


def collect(plan, attn, up, second, first, rows):
    span = attn[0].shape[1]
    rows[...] = jnp.zeros_like(rows)
    for shard in range(4):
        wide, narrow = jnp.zeros((1, rows.shape[1]), F32), jnp.zeros((1, span), F32)
        for apart in range(4):
            here = plan[SHARD] == shard ^ apart
            narrow = jnp.where(here, attn[apart][0:1, :], narrow)
            wide = jnp.where(here, up[apart][...], wide)
        rows[shard : shard + 1, 0:span] = narrow
        rows[4 + shard : 5 + shard, :] = wide
    rows[8:11, :] = second[0:3, :]
    rows[11:14, :] = first[0:3, :]


def choose(total, plan, base, count, sent, keep):
    rows = keep.shape[0] // count
    for i in range(count):
        for ref, at in ((sent, base + i), (keep, base + count + i)):
            copy_rows(ref, i * rows, total, pl.multiple_of(plan[at] * rows, rows), rows)


def first_kernel(segments, vectors, plan, *refs):
    if vectors:
        *ops, sent, keep, kept_vectors, rows = refs
        parts = ops[-10:]
        collect(plan, parts[:4], parts[4:8], parts[8], parts[9], rows)
        kept_vectors[...] = send_vectors(rows[...], sent)
    else:
        *ops, sent, keep = refs
    half = keep.shape[0] // 2
    for slot in range(4):
        target = (sent, keep)[slot // 2]
        for block in ((0, 1), (1, 2, 3), (0, 1, 2), (2, 3))[slot]:

            @pl.when(plan[FIRST + slot] == block)
            def _(slot=slot, block=block, target=target):
                begin, end = (block % 2) * half, (block % 2 + 1) * half
                at = 0
                for left, right, size in segments[block // 2]:
                    low, high = max(begin, at), min(end, at + size)
                    if low < high:
                        to = (slot % 2) * half + low - begin
                        add_rows(target, to, ops[left[0]].at[left[1]], ops[right[0]].at[right[1]], low - at, high - low)
                    at += size


def first_stage(plan, parts, stacked, vectors):
    width = parts[0].shape[-1]
    size = parts[0].shape[0]
    ops = [p[None] for p in parts] + list(stacked)
    segments = [[((0, 0), (1, 0), size)], [((2, 0), (3, 0), size)]]
    rows = size
    if stacked:
        rows += stacked[0].shape[1]
        for i in range(2):
            segments[i].append(((4, i), (5, i), rows - size))
    outs = [((rows, width), BF), ((rows, width), F32)]
    if vectors:
        outs = [((rows + 2 * VECTORS, width), BF), outs[1], ((VECTORS, width), F32)]
    return run(
        functools.partial(first_kernel, segments, bool(vectors)),
        "first_stage",
        outs,
        *ops,
        *vectors,
        scratch=[pltpu.VMEM((VECTORS, width), F32)] if vectors else [],
        plan=plan,
    )


def next_kernel(base, count, plan, kept, got, *refs):
    rows = kept.shape[0]
    if len(refs) > 3:
        had, sent, keep, has, total = refs
        has[...] = send_vectors(had[...] + got_vectors(got), sent)
    else:
        sent, keep, total = refs
    total[...] = kept[...] + got[0:rows, :].astype(F32)
    choose(total, plan, base, count, sent, keep)


def next_stage(plan, base, count, kept, got, vectors=()):
    rows, width = kept.shape
    outs = [((rows // 2, width), BF), ((rows // 2, width), F32)]
    if vectors:
        outs = [((rows // 2 + 2 * VECTORS, width), BF), outs[1], ((VECTORS, width), F32)]
    return run(
        functools.partial(next_kernel, base, count),
        "next_stage",
        outs,
        kept,
        got,
        *vectors,
        scratch=[pltpu.VMEM((rows, width), F32)],
        plan=plan,
    )


def finish_kernel(sizes, plan, mine, theirs, *refs):
    outs, (sums, sem) = refs[:-2], refs[-2:]
    rows = mine.shape[0] // 4
    for h in range(2):
        for i in range(4):
            where = pl.ds(pl.multiple_of(plan[PLACES + i] * rows, rows), rows)
            at = (4 * h + i) * rows
            sums[at : at + rows, :] = jnp.where(
                plan[SIDE] == h, mine[where, :], theirs[where, :]
            ).astype(F32)
    copies, at = [], 0
    for ref, size in zip(outs, sizes):
        copies.append(pltpu.make_async_copy(sums.at[pl.ds(at, size)], ref, sem))
        copies[-1].start()
        at += size
    for copy in copies:
        copy.wait()


def finish(plan, mine, theirs, sizes):
    half, width = mine.shape
    return pl.pallas_call(
        functools.partial(finish_kernel, sizes),
        grid_spec=pltpu.PrefetchScalarGridSpec(
            num_scalar_prefetch=1,
            grid=(1,),
            in_specs=[whole((half, width))] * 2,
            out_specs=[ANY] * len(sizes),
            scratch_shapes=[pltpu.VMEM((2 * half, width), F32), pltpu.SemaphoreType.DMA(())],
        ),
        out_shape=[jax.ShapeDtypeStruct((size, width), F32) for size in sizes],
        compiler_params=params(),
        cost_estimate=SMALL,
        name="finish",
    )(plan, mine, theirs)


Y, X, Z_NEAR, Z_FAR = ("tensor", 2), ("dp", 1), ("dp", 2), ("dp", 4)


def tie(value, *others):
    return lax.optimization_barrier((value, others))[0]


def swap(value, even, odd=None):
    groups, width = lax.axis_size("dp"), lax.axis_size("tensor")
    pairs = []
    for group in range(groups):
        for t in range(width):
            axis, bit = even if odd is None or t % 2 == 0 else odd
            to = (group ^ bit, t) if axis == "dp" else (group, t ^ bit)
            pairs.append((group * width + t, to[0] * width + to[1]))
    return lax.ppermute(value, ("dp", "tensor"), pairs)


def partner(value):
    return swap(value, ("tensor", 1))


def make_plan():
    index, t = lax.axis_index("dp"), lax.axis_index("tensor")
    x, near, far, core = index % 2, index // 2 % 2, index // 4 % 2, t % 2
    quarter, place = x + 2 * near, near + 2 * far
    even = [quarter, quarter ^ 1, quarter ^ 2, quarter ^ 3]
    odd = [quarter, quarter ^ 2, quarter ^ 1, quarter ^ 3]
    even += odd + [0, 1, 2, 3]
    odd += even[:4] + [0, 1, 2, 3]
    even += [0, 1, 2, 3]
    odd += [1 - x, 3 - x, x, 2 + x]
    even += [1 - x, x]
    odd += [0, 1]
    even += [1 - near, 3 - near, near, 2 + near]
    odd += [2 - 2 * far, 3 - 2 * far, 2 * far, 2 * far + 1]
    even += [1 - far, far]
    odd += [1 - near, near]
    apart = [i ^ place for i in range(4)]
    even += [i // 2 + 2 * (i % 2) for i in apart]
    odd += apart
    quarters = [quarter ^ i for i in range(4)]
    even += [x, *quarters, t]
    odd += [x, *quarters, t]
    both = [jnp.stack([jnp.asarray(i, jnp.int32) for i in plan]) for plan in (even, odd)]
    return jnp.where(core == 0, *both)


class Gather:
    def __init__(self, plan, sent, tail=0):
        self.plan, self.tail = plan, tail
        self.got = swap(sent, Y)

    def after(self, *values):
        self.got = tie(self.got, *values)

    @classmethod
    def of_two(cls, plan, sent):
        return cls(plan, sent)

    def both(self):
        rows = self.got.shape[0] // 2
        self.held, self.far = self.got[:rows], self.got[rows:]
        self.got = [swap(self.held, X), swap(self.held, Z_NEAR)]

    def joined(self):
        return join(self.plan, QUARTERS, self.held, *self.got, self.far)

    def second(self):
        rows = self.got.shape[0] - self.tail
        self.rest = [self.got[rows:]] if self.tail else []
        self.held = self.got[:rows]
        self.got = swap(self.held, X, Z_NEAR)

    def third(self):
        self.held = jnp.concatenate([self.held, self.got], axis=0)
        self.got = swap(self.held, Z_NEAR, X)

    def result(self):
        rows = self.held.shape[0] // 2
        return join(
            self.plan, BY_B, self.held[:rows], self.held[rows:], self.got[:rows], self.got[rows:], *self.rest
        )


class Reduction:
    def __init__(self, plan):
        self.plan = plan

    def after(self, *values):
        self.got = tie(self.got, *values)

    def first(self, parts, stacked=(), vectors=()):
        self.sent, self.keep, *self.vectors = first_stage(self.plan, parts, stacked, vectors)
        self.got = swap(self.sent, Y, X)

    def next(self, base, count):
        self.sent, self.keep, *self.vectors = next_stage(
            self.plan, base, count, self.keep, self.got, self.vectors
        )

    def second(self):
        self.next(SECOND, 1)
        self.got = swap(self.sent, X, Y)

    def third(self):
        self.next(THIRD, 2)
        self.got = swap(self.sent, Z_NEAR, Z_FAR)

    def fourth(self):
        self.next(FOURTH, 1)
        self.got = swap(self.sent, Z_FAR, Z_NEAR)

    def fifth(self):
        rows = self.keep.shape[0]
        total = (self.keep + self.got[:rows].astype(F32)).astype(BF)
        if self.vectors:
            high, low = self.got[rows : rows + VECTORS], self.got[rows + VECTORS :]
            self.vectors = [self.vectors[0] + (high.astype(F32) + low.astype(F32))]
        bit = 8
        while bit < lax.axis_size("dp"):
            total = (total.astype(F32) + swap(total, ("dp", bit)).astype(F32)).astype(BF)
            self.vectors = [v + swap(v, ("dp", bit)) for v in self.vectors]
            bit *= 2
        self.sent = total
        self.got = swap(self.sent, Z_FAR, Z_NEAR)

    def sixth(self):
        self.sent = jnp.concatenate([self.sent, self.got], axis=0)
        self.got = swap(self.sent, Z_NEAR, Z_FAR)

    def seventh(self):
        self.sent = jnp.concatenate([self.sent, self.got], axis=0)
        self.got = swap(self.sent, X)

    def result(self, sizes):
        return finish(self.plan, self.sent, self.got, sizes)


def on_device(
    tokens,
    w_query,
    w_key,
    w_value,
    b_query,
    b_value,
    w_output,
    b_output,
    first_gain,
    first_shift,
    w_up,
    b_up,
    w_down,
    b_down,
    second_gain,
    second_shift,
    cotangent,
):
    rows, width = tokens.shape
    local = w_query.shape[1]
    assert rows == SEQ_LEN and width == 4 * local and w_up.shape == (width, width)
    plan = make_plan()
    pack_d, near, up_far, down_far, table = pack_weights(
        plan, w_query, w_key, w_value, w_output, w_up, w_down,
        (b_query, b_value, b_up, b_output, first_gain, first_shift, b_down, second_gain,
         second_shift),
    )

    far_pack = Gather(plan, near, BIAS_ROWS)
    up = Gather.of_two(plan, tie(up_far, near))
    pack_c = partner(tie(pack_d, near))
    down = Gather.of_two(plan, tie(down_far, far_pack.got))
    far_pack.second()
    *saved_d, bias_d, part = attention(tie(tokens, far_pack.held), pack_d, small=True)
    far_pack.after(part)
    far_pack.third()
    *saved_c, bias_c, part = attention(tokens, pack_c, tie(part, far_pack.held), small=True)
    far_pack.after(part)
    pack_b = far_pack.result()
    up.after(pack_b)
    up.both()
    pack_a = partner(pack_b)
    up_d, down_d = w_up, w_down
    up_c = partner(tie(w_up, pack_b))
    *saved_b, bias_b, part = attention(tokens, pack_b, tie(part, up.held))
    down.after(part)
    down.both()
    down_c = partner(tie(w_down, down.held))
    *saved_a, bias_a, normed, normed_low, unit, scale = attention(
        tokens, pack_a, tie(part, down.held), table
    )
    up.got, up.far = tie((up.got, up.far), normed)
    up_b = up.joined()
    up_a = partner(up_b)
    act_d, slope_d, part = feed(normed_low, up_d, down_d, bias_d, tie(normed, up_b))
    act_c, slope_c, part = feed(normed_low, up_c, down_c, bias_c, part)
    down.got, down.far = tie((down.got, down.far), part)
    down_b = down.joined()
    down_a = partner(down_b)
    act_b, slope_b, part = feed(normed_low, up_b, down_b, bias_b, part)
    act_a, slope_a, layer_out, down_low, grad_second, small_second = feed(
        normed_low, up_a, down_a, bias_a, part, [table, cotangent]
    )

    down, up, attn = Reduction(plan), Reduction(plan), Reduction(plan)
    grad_a, grad_b = down_grad([act_a, act_b], down_low)
    core_other = partner(grad_a)
    grad_c, grad_d = down_grad([act_c, act_d], tie(down_low, grad_a))
    core_own = partner(grad_c)
    up_grad_a, bias_up_a, part = feed_back(
        slope_a, down_low, normed_low, tie(grad_second, grad_c), up_a, down_a
    )
    core_up_other = partner(up_grad_a)
    down.first([grad_b, *tie((core_other,), up_grad_a), grad_d, core_own])
    up_grad_b, bias_up_b, part = feed_back(
        slope_b, down_low, normed_low, tie(part, down.sent), up_b, down_b
    )
    up_grad_c, bias_up_c, part = feed_back(
        slope_c, down_low, normed_low, tie(part, core_up_other), up_c, down_c
    )
    core_up_own = partner(up_grad_c)
    up_grad_d, bias_up_d, grad_first, first_low, small_first = feed_back(
        slope_d, down_low, normed_low, part, up_d, down_d, [unit, scale, table]
    )
    out_send, out_keep = out_grad([s[2] for s in (saved_a, saved_b, saved_c, saved_d)], first_low)
    core_out = partner(out_send)
    down.after(out_keep)
    down.second()
    grad_a, bias_a, part = attention_back(
        saved_a[:3], first_low, tokens, tie(grad_first, down.sent), pack_a
    )
    core_other = partner(grad_a)
    up.first([up_grad_b, core_up_other, up_grad_d, core_up_own], [out_keep, tie(core_out, grad_a)])
    down.after(up.sent)
    down.third()
    grad_b, bias_b, part = attention_back(
        saved_b, first_low, tokens, tie(part, down.sent), pack_b
    )
    grad_c, bias_c, part = attention_back(
        saved_c, first_low, tokens, tie(part, core_other), pack_c
    )
    core_own = partner(grad_c)
    down.after(grad_c)
    down.fourth()
    up.after(down.sent)
    up.second()
    grad_d, bias_d, grad_tokens = attention_back(
        saved_d, first_low, tokens, tie(part, up.sent), pack_d
    )
    down.after(grad_tokens)
    down.fifth()
    attn.first(
        [grad_b, core_other, grad_d, tie(core_own, down.sent, up.got)],
        vectors=[
            bias_d, bias_c, bias_b, bias_a, bias_up_d, bias_up_c, bias_up_b, bias_up_a,
            small_second, small_first,
        ],
    )

    up.after(attn.sent)
    up.third()
    down.after(up.sent)
    down.sixth()

    attn.after(down.sent)
    attn.second()
    up.after(attn.sent)
    up.fourth()
    down.after(up.sent)
    down.seventh()

    attn.after(down.sent)
    attn.third()
    up.after(attn.sent)
    up.fifth()

    attn.after(up.sent)
    attn.fourth()
    up.after(attn.sent)
    up.sixth()
    down.after(up.sent)
    (grad_w_down,) = down.result((width,))

    attn.after(grad_w_down)
    attn.fifth()
    (sums,) = attn.vectors
    others = partner(sums)
    up.after(attn.sent)
    up.seventh()

    attn.after(up.sent)
    attn.sixth()
    sums = sums + tie(others, attn.sent)
    shard = lax.axis_index("tensor")
    attn_vectors = lax.dynamic_index_in_dim(sums, shard, 0, keepdims=False)
    up_vector = lax.dynamic_index_in_dim(sums, 4 + shard, 0, keepdims=False)

    attn.after(attn_vectors, up_vector)
    attn.seventh()
    up.after(attn.sent)
    grad_w_up, grad_o = up.result((width, local))
    attn.after(grad_o)
    grad_q, grad_k, grad_v = attn.result((local,) * 3)

    return (
        tie(layer_out, attn.got).astype(BF),
        grad_tokens.astype(BF),
        grad_q.T,
        grad_k.T,
        grad_v.T,
        attn_vectors[:local],
        attn_vectors[2 * local : 3 * local],
        grad_o,
        sums[11],
        sums[12],
        sums[13],
        grad_w_up,
        up_vector,
        grad_w_down,
        sums[8],
        sums[9],
        sums[10],
    )


def solution(mesh):
    rows = P(("dp", "tensor"), None)
    col, row, vec, rep = P(None, "tensor"), P("tensor", None), P("tensor"), P()
    return jax.shard_map(
        on_device,
        mesh=mesh,
        in_specs=(
            rows, col, col, col, vec, vec, row, rep, rep, rep, col, vec, row, rep, rep, rep, rows,
        ),
        out_specs=(
            rows, rows, col, col, col, vec, vec, row, rep, rep, rep, col, vec, row, rep, rep, rep,
        ),
        check_vma=False,
    )
```

profile of v0, /device:TPU:0, one launch (start us, length us, event | category | flops | bytes accessed | tf_op | source)
XLA Modules:
  0.0 215.3 jit_solution(3881997843264915872)
XLA Ops:
  1.6 3.6 %pack_weights.1 = (bf16[784,768]{1,0:T(8,128)(2,1)}, bf16[208,768]{1,0:T(8,128)(2,1)}, bf16[384,768]{1,0:T(8,128)(2,1)}, bf16[384,768]{1,0:T(8,128)(2,1)}, f32[8,768]{1,0:T(8,128)}) custom-call(s32[34]{0:T(128)} %broadcast_select_fusion.plan, bf16[192,768]{1,0:T(8,128)(2,1)} %bitcast.59, bf16[192,768]{1,0:T(8,128)(2,1)} %bitcast.60, ...), custom_call_target="tpu_custom_call" | custom-call | tf_op jit(solution)/shard_map/pack_weights/pallas_call | solution.py:123
  5.2 3.0 %collective-permute-start = (bf16[208,768]{1,0:T(8,128)(2,1)}, bf16[208,768]{1,0:T(8,128)(2,1)S(1)}, u32[]{:S(2)}, u32[]{:S(2)}) collective-permute-start(bf16[208,768]{1,0:T(8,128)(2,1)} %get-tuple-element.179), channel_id=1, source_target_pairs={{0,2},{1,3},{2,0},{3,1},{4,6},{5,7},{6,4},{7,5},{8,10},{9,11},{10,... | collective-permute-start | bytes 958472 | tf_op jit(solution)/shard_map/ppermute | solution.py:661
  8.4 8.4 %collective-permute-done = bf16[208,768]{1,0:T(8,128)(2,1)S(1)} collective-permute-done((bf16[208,768]{1,0:T(8,128)(2,1)}, bf16[208,768]{1,0:T(8,128)(2,1)S(1)}, u32[]{:S(2)}, u32[]{:S(2)}) %collective-permute-start) | collective-permute-done | bytes 319520 | tf_op jit(solution)/shard_map/ppermute | solution.py:661
  16.9 2.1 collective-permute-start.1
  19.0 1.3 copy-done.11
  20.3 4.2 %attention.3 = (bf16[576,512]{1,0:T(8,128)(2,1)S(1)}, bf16[3,512,512]{2,1,0:T(8,128)(2,1)S(1)}, bf16[192,512]{1,0:T(8,128)(2,1)S(1)}, f32[1,768]{1,0:T(1,128)S(1)}, f32[512,768]{1,0:T(8,128)S(1)}) custom-call(bf16[512,768]{1,0:T(8,128)(2,1)S(1)} %copy-done.22, bf16[784,768]{1,0:T(8,128)(2,1)S(1)} %copy-done.11), custom_call_target="tpu_custom_call" | custom-call | flops 49999998976 | bytes 80000000 | tf_op jit(solution)/shard_map/attention/pallas_call | solution.py:48
  24.5 1.6 collective-permute-start.6
  26.2 1.6 collective-permute-start.2
  27.8 4.2 %attention.4 = (bf16[576,512]{1,0:T(8,128)(2,1)S(1)}, bf16[3,512,512]{2,1,0:T(8,128)(2,1)S(1)}, bf16[192,512]{1,0:T(8,128)(2,1)S(1)}, f32[1,768]{1,0:T(1,128)S(1)}, f32[512,768]{1,0:T(8,128)S(1)}) custom-call(bf16[512,768]{1,0:T(8,128)(2,1)S(1)} %copy-done.22, bf16[784,768]{1,0:T(8,128)(2,1)S(1)} %collective-permute-done.3.refs_1_.weights, ...), custom_call_target="tpu_custom_call" | custom-call | flops 49999998976 | bytes 80000000 | tf_op jit(solution)/shard_map/attention/pallas_call | solution.py:48
  32.1 4.0 %collective-permute-done.2 = bf16[384,768]{1,0:T(8,128)(2,1)S(1)} collective-permute-done((bf16[384,768]{1,0:T(8,128)(2,1)S(1)}, bf16[384,768]{1,0:T(8,128)(2,1)S(1)}, u32[]{:S(2)}, u32[]{:S(2)}) %collective-permute-start.2) | collective-permute-done | bytes 589856 | tf_op jit(solution)/shard_map/ppermute | solution.py:661
  37.6 1.6 collective-permute-start.8
  39.2 3.8 %attention.5 = (bf16[576,512]{1,0:T(8,128)(2,1)S(1)}, bf16[3,512,512]{2,1,0:T(8,128)(2,1)S(1)}, bf16[192,512]{1,0:T(8,128)(2,1)S(1)}, f32[1,768]{1,0:T(1,128)S(1)}, f32[512,768]{1,0:T(8,128)S(1)}) custom-call(bf16[512,768]{1,0:T(8,128)(2,1)S(1)} %copy-done.22, bf16[784,768]{1,0:T(8,128)(2,1)S(1)} %join.3.refs_1_.weights, ...), custom_call_target="tpu_custom_call" | custom-call | flops 49999998976 | bytes 80000000 | tf_op jit(solution)/shard_map/attention/pallas_call | solution.py:48
  43.1 1.6 collective-permute-start.10
  45.3 5.5 %attention_last.1 = (bf16[576,512]{1,0:T(8,128)(2,1)S(1)}, bf16[3,512,512]{2,1,0:T(8,128)(2,1)S(1)}, bf16[192,512]{1,0:T(8,128)(2,1)S(1)}, f32[1,768]{1,0:T(1,12...) custom-call(bf16[512,768]{1,0:T(8,128)(2,1)S(1)} %copy-done.22, ...), custom_call_target="tpu_custom_call" | custom-call | flops 49999998976 | bytes 80000000 | tf_op jit(solution)/shard_map/attention_last/pallas_call | solution.py:48
  52.2 1.8 feed.3
  54.1 1.8 feed.4
  57.2 1.8 feed.5
  59.7 4.6 %feed_last.1 = (bf16[512,768]{1,0:T(8,128)(2,1)S(1)}, bf16[512,768]{1,0:T(8,128)(2,1)S(1)}, f32[512,768]{1,0:T(8,128)S(1)}, bf16[512,768]{1,0:T(8,128)(2,1)S(1)}...) custom-call(bf16[512,768]{1,0:T(8,128)(2,1)S(1)} %get-tuple-element.198.refs_0_.refs_2_, ...), custom_call_target="tpu_custom_call" | custom-call | flops 49999998976 | bytes 80000000 | tf_op jit(solution)/shard_map/feed_last/pallas_call | solution.py:48
  64.2 1.4 down_grad.2
  66.1 1.4 down_grad.3
  67.7 2.7 %feed_back.3 = (bf16[768,768]{1,0:T(8,128)(2,1)S(1)}, f32[1,768]{1,0:T(1,128)S(1)}, f32[512,768]{1,0:T(8,128)S(1)}) custom-call(bf16[512,768]{1,0:T(8,128)(2,1)S(1)} %get-tuple-element.223.refs_0_, bf16[512,768]{1,0:T(8,128)(2,1)S(1)} %get-tuple-element.230.refs_2_.refs_1_, bf16[512,768]{1,0:T(8,128)(2,1)S(1)} %get-tuple-element.198.refs_0_.refs_2_, ...), custom_call_target="tpu_custom_call" | custom-call | flops 40000000000 | bytes 100000000 | tf_op jit(solution)/shard_map/feed_back/pallas_call | solution.py:48
  70.9 1.2 first_stage.3
  72.1 1.1 collective-permute-start.18
  73.2 2.7 %feed_back.4 = (bf16[768,768]{1,0:T(8,128)(2,1)S(1)}, f32[1,768]{1,0:T(1,128)S(1)}, f32[512,768]{1,0:T(8,128)S(1)}) custom-call(bf16[512,768]{1,0:T(8,128)(2,1)S(1)} %get-tuple-element.222.refs_0_, bf16[512,768]{1,0:T(8,128)(2,1)S(1)} %get-tuple-element.230.refs_2_.refs_1_, bf16[512,768]{1,0:T(8,128)(2,1)S(1)} %get-tuple-element.198.refs_0_.refs_2_, ...), custom_call_target="tpu_custom_call" | custom-call | flops 40000000000 | bytes 100000000 | tf_op jit(solution)/shard_map/feed_back/pallas_call | solution.py:48
  75.9 1.0 copy-done.7
  77.0 2.7 %feed_back.5 = (bf16[768,768]{1,0:T(8,128)(2,1)S(1)}, f32[1,768]{1,0:T(1,128)S(1)}, f32[512,768]{1,0:T(8,128)S(1)}) custom-call(bf16[512,768]{1,0:T(8,128)(2,1)S(1)} %get-tuple-element.221.refs_0_, bf16[512,768]{1,0:T(8,128)(2,1)S(1)} %get-tuple-element.230.refs_2_.refs_1_, bf16[512,768]{1,0:T(8,128)(2,1)S(1)} %get-tuple-element.198.refs_0_.refs_2_, ...), custom_call_target="tpu_custom_call" | custom-call | flops 40000000000 | bytes 100000000 | tf_op jit(solution)/shard_map/feed_back/pallas_call | solution.py:48
  79.8 4.1 %feed_back_last.1 = (bf16[768,768]{1,0:T(8,128)(2,1)S(1)}, f32[1,768]{1,0:T(1,128)S(1)}, f32[512,768]{1,0:T(8,128)S(1)}, bf16[512,768]{1,0:T(8,128)(2,1)S(1)}, f32[8,768]{1,0:T(8,128)S(1)}) custom-call(bf16[512,768]{1,0:T(8,128)(2,1)S(1)} %get-tuple-element.219.refs_0_, bf16[512,768]{1,0:T(8,128)(2,1)S(1)} %get-tuple-element.230.refs_2_.refs_1_, ...), custom_call_target="tpu_custom_call" | custom-call | flops 49999998976 | bytes 100000000 | tf_op jit(solution)/shard_map/feed_back_last/pallas_call | solution.py:48
  85.3 3.1 %collective-permute-done.18.got = bf16[768,768]{1,0:T(8,128)(2,1)S(1)} collective-permute-done((bf16[768,768]{1,0:T(8,128)(2,1)S(1)}, bf16[768,768]{1,0:T(8,128)(2,1)S(1)}, u32[]{:S(2)}, u32[]{:S(2)}) %collective-permute-start.18) | collective-permute-done | bytes 1179680 | tf_op jit(solution)/shard_map/ppermute | solution.py:661
  90.0 5.9 %attention_back.4 = (bf16[576,768]{1,0:T(8,128)(2,1)S(1)}, f32[8,576]{1,0:T(8,128)S(1)}, f32[512,768]{1,0:T(8,128)S(1)}) custom-call(bf16[576,512]{1,0:T(8,128)(2,1)S(1)} %copy-done.29, bf16[3,512,512]{2,1,0:T(8,128)(2,1)S(1)} %get-tuple-element.247.probs, bf16[512,768]{1,0:T(8,128)(2,1)S(1)} %get-tuple-element.245.low.first_low, ...), custom_call_target="tpu_custom_call" | custom-call | flops 70000001024 | bytes 120000000 | tf_op jit(solution)/shard_map/attention_back/pallas_call | solution.py:48
  96.1 1.4 first_stage.4
  97.4 1.1 collective-permute-start.23
  100.2 1.6 collective-permute-start.24
  101.9 5.9 %attention_back.5 = (bf16[576,768]{1,0:T(8,128)(2,1)S(1)}, f32[8,576]{1,0:T(8,128)S(1)}, f32[512,768]{1,0:T(8,128)S(1)}) custom-call(bf16[576,512]{1,0:T(8,128)(2,1)S(1)} %copy-done.33, bf16[3,512,512]{2,1,0:T(8,128)(2,1)S(1)} %get-tuple-element.218.probs, bf16[512,768]{1,0:T(8,128)(2,1)S(1)} %get-tuple-element.245.low.first_low, ...), custom_call_target="tpu_custom_call" | custom-call | flops 70000001024 | bytes 120000000 | tf_op jit(solution)/shard_map/attention_back/pallas_call | solution.py:48
  107.8 5.9 %attention_back.6 = (bf16[576,768]{1,0:T(8,128)(2,1)S(1)}, f32[8,576]{1,0:T(8,128)S(1)}, f32[512,768]{1,0:T(8,128)S(1)}) custom-call(bf16[576,512]{1,0:T(8,128)(2,1)S(1)} %copy-done.31, bf16[3,512,512]{2,1,0:T(8,128)(2,1)S(1)} %get-tuple-element.274.probs, bf16[512,768]{1,0:T(8,128)(2,1)S(1)} %get-tuple-element.245.low.first_low, ...), custom_call_target="tpu_custom_call" | custom-call | flops 70000001024 | bytes 120000000 | tf_op jit(solution)/shard_map/attention_back/pallas_call | solution.py:48
  115.0 2.1 collective-permute-start.26
  117.1 1.0 next_stage.12
  118.2 1.2 collective-permute-start.27
  119.4 5.9 %attention_back.7 = (bf16[576,768]{1,0:T(8,128)(2,1)S(1)}, f32[8,576]{1,0:T(8,128)S(1)}, f32[512,768]{1,0:T(8,128)S(1)}) custom-call(bf16[576,512]{1,0:T(8,128)(2,1)S(1)} %copy-done.35, bf16[3,512,512]{2,1,0:T(8,128)(2,1)S(1)} %copy-done.27, bf16[512,768]{1,0:T(8,128)(2,1)S(1)} %get-tuple-element.245.low.first_low, bf16[512,768]{1,0:T(8,128)(2,1)S(1)} %copy-done.23, ...), custom_call_target="tpu_custom_call" | custom-call | flops 70000001024 | bytes 120000000 | tf_op jit(solution)/shard_map/attention_back/pallas_call | solution.py:48
  125.3 1.1 copy-done
  126.5 3.2 %collective-permute-done.27.got = bf16[480,768]{1,0:T(8,128)(2,1)S(1)} collective-permute-done((bf16[480,768]{1,0:T(8,128)(2,1)S(1)}, bf16[480,768]{1,0:T(8,128)(2,1)S(1)}, u32[]{:S(2)}, u32[]{:S(2)}) %collective-permute-start.27) | collective-permute-done | bytes 737312 | tf_op jit(solution)/shard_map/ppermute | solution.py:661
  129.7 1.1 first_stage.5
  131.7 2.6 %collective-permute-start.29 = (bf16[96,768]{1,0:T(8,128)(2,1)S(1)}, bf16[96,768]{1,0:T(8,128)(2,1)S(1)}, u32[]{:S(2)}, u32[]{:S(2)}) collective-permute-start(bf16[96,768]{1,0:T(8,128)(2,1)S(1)} %add_convert_fusion.1), channel_id=1, source_target_pairs={{0,16},{1,9},{2,18},{3,11},{4,20},{5,13},{6,22},{7,15},{8,24},{9,1... | collective-permute-start | bytes 442376 | tf_op jit(solution)/shard_map/ppermute | solution.py:661
  135.1 1.1 collective-permute-start.32
  136.3 8.6 %collective-permute-done.29 = bf16[96,768]{1,0:T(8,128)(2,1)S(1)} collective-permute-done((bf16[96,768]{1,0:T(8,128)(2,1)S(1)}, bf16[96,768]{1,0:T(8,128)(2,1)S(1)}, u32[]{:S(2)}, u32[]{:S(2)}) %collective-permute-start.29) | collective-permute-done | bytes 147488 | tf_op jit(solution)/shard_map/ppermute | solution.py:661
  145.8 1.4 collective-permute-start.30
  148.9 2.5 %collective-permute-start.34 = (bf16[120,768]{1,0:T(8,128)(2,1)S(1)}, bf16[120,768]{1,0:T(8,128)(2,1)S(1)}, u32[]{:S(2)}, u32[]{:S(2)}) collective-permute-start(bf16[120,768]{1,0:T(8,128)(2,1)S(1)} %get-tuple-element.313), channel_id=1, source_target_pairs={{0,16},{1,9},{2,18},{3,11},{4,20},{5,13},{6,22},{7,15},{8,24},{9,1... | collective-permute-start | bytes 552968 | tf_op jit(solution)/shard_map/ppermute | solution.py:661
  151.5 10.7 %collective-permute-done.31 = bf16[192,768]{1,0:T(8,128)(2,1)S(1)} collective-permute-done((bf16[192,768]{1,0:T(8,128)(2,1)S(1)}, bf16[192,768]{1,0:T(8,128)(2,1)S(1)}, u32[]{:S(2)}, u32[]{:S(2)}) %collective-permute-start.31) | collective-permute-done | bytes 294944 | tf_op jit(solution)/shard_map/ppermute | solution.py:661
  163.3 1.5 collective-permute-start.37
  164.9 9.4 %collective-permute-done.33.got = bf16[176,768]{1,0:T(8,128)(2,1)S(1)} collective-permute-done((bf16[176,768]{1,0:T(8,128)(2,1)S(1)}, bf16[176,768]{1,0:T(8,128)(2,1)S(1)}, u32[]{:S(2)}, u32[]{:S(2)}) %collective-permute-start.33) | collective-permute-done | bytes 270368 | tf_op jit(solution)/shard_map/ppermute | solution.py:661
  175.1 2.1 collective-permute-start.39
  177.1 2.1 finish.3
  179.3 4.0 %collective-permute-done.35 = bf16[104,768]{1,0:T(8,128)(2,1)S(1)} collective-permute-done((bf16[104,768]{1,0:T(8,128)(2,1)S(1)}, bf16[104,768]{1,0:T(8,128)(2,1)S(1)}, u32[]{:S(2)}, u32[]{:S(2)}) %collective-permute-start.35) | collective-permute-done | bytes 159776 | tf_op jit(solution)/shard_map/ppermute | solution.py:661
  183.4 3.2 %collective-permute-done.39 = bf16[240,768]{1,0:T(8,128)(2,1)S(1)} collective-permute-done((bf16[240,768]{1,0:T(8,128)(2,1)S(1)}, bf16[240,768]{1,0:T(8,128)(2,1)S(1)}, u32[]{:S(2)}, u32[]{:S(2)}) %collective-permute-start.39) | collective-permute-done | bytes 368672 | tf_op jit(solution)/shard_map/ppermute | solution.py:661
  186.7 2.4 %collective-permute-start.43 = (bf16[480,768]{1,0:T(8,128)(2,1)S(1)}, bf16[480,768]{1,0:T(8,128)(2,1)S(1)}, u32[]{:S(2)}, u32[]{:S(2)}) collective-permute-start(bf16[480,768]{1,0:T(8,128)(2,1)S(1)} %pad_maximum_fusion.mine), channel_id=1, source_target_pairs={{0,4},{1,5},{2,6},{3,7},{4,0},{5,1},{6,2},{7,3},{8,12},{9,13},{10,... | collective-permute-start | bytes 2211848 | tf_op jit(solution)/shard_map/ppermute | solution.py:661
  189.1 3.8 %collective-permute-done.38 = bf16[72,768]{1,0:T(8,128)(2,1)S(1)} collective-permute-done((bf16[72,768]{1,0:T(8,128)(2,1)S(1)}, bf16[72,768]{1,0:T(8,128)(2,1)S(1)}, u32[]{:S(2)}, u32[]{:S(2)}) %collective-permute-start.38) | collective-permute-done | bytes 110624 | tf_op jit(solution)/shard_map/ppermute | solution.py:661
  193.6 1.4 collective-permute-done.41
  196.4 2.5 %collective-permute-done.40 = bf16[144,768]{1,0:T(8,128)(2,1)S(1)} collective-permute-done((bf16[144,768]{1,0:T(8,128)(2,1)S(1)}, bf16[144,768]{1,0:T(8,128)(2,1)S(1)}, u32[]{:S(2)}, u32[]{:S(2)}) %collective-permute-start.40) | collective-permute-done | bytes 221216 | tf_op jit(solution)/shard_map/ppermute | solution.py:661
  199.6 1.1 pad_maximum_fusion.3.mine
  200.7 1.3 collective-permute-start.42
  202.1 2.4 %convert_element_type.39 = bf16[512,768]{1,0:T(8,128)(2,1)} convert(f32[512,768]{1,0:T(8,128)} %copy-done) | non-fusion elementwise | flops 393216 | bytes 2359296 | tf_op jit(solution)/shard_map/convert_element_type | solution.py:952
  204.4 1.4 fusion.3
  205.8 2.3 %finish.4 = (f32[768,768]{1,0:T(8,128)}, f32[192,768]{1,0:T(8,128)}) custom-call(s32[34]{0:T(128)S(1)} %copy-done.10, bf16[480,768]{1,0:T(8,128)(2,1)S(1)} %pad_maximum_fusion.mine, bf16[480,768]{1,0:T(8,128)(2,1)S(1)} %collective-permute-done.43.theirs), custom_call_target="tpu_custom_call" | custom-call | flops 1000 | bytes 1000 | tf_op jit(solution)/shard_map/finish/pallas_call | solution.py:630
  208.1 3.4 %collective-permute-done.42.theirs = bf16[288,768]{1,0:T(8,128)(2,1)} collective-permute-done((bf16[288,768]{1,0:T(8,128)(2,1)S(1)}, bf16[288,768]{1,0:T(8,128)(2,1)}, u32[]{:S(2)}, u32[]{:S(2)}) %collective-permute-start.42) | collective-permute-done | bytes 442400 | tf_op jit(solution)/shard_map/ppermute | solution.py:661
  211.5 2.9 %finish.5 = (f32[192,768]{1,0:T(8,128)}, f32[192,768]{1,0:T(8,128)}, f32[192,768]{1,0:T(8,128)}) custom-call(s32[34]{0:T(128)S(1)} %copy-done.10, bf16[288,768]{1,0:T(8,128)(2,1)S(1)} %pad_maximum_fusion.3.mine, bf16[288,768]{1,0:T(8,128)(2,1)} %collective-permute-done.42.theirs), custom_call_target="tpu_custom_call" | custom-call | flops 1000 | bytes 1000 | tf_op jit(solution)/shard_map/finish/pallas_call | solution.py:630
  (168 shorter events, 23.7 us)
Async XLA Ops:
  1.6 17.4 %copy-start.22 = (bf16[512,768]{1,0:T(8,128)(2,1)S(1)}, bf16[512,768]{1,0:T(8,128)(2,1)}, u32[]{:S(2)}) copy-start(bf16[512,768]{1,0:T(8,128)(2,1)} %tok.7) | copy-start | bytes 2359300
  5.2 11.6 %collective-permute-start = (bf16[208,768]{1,0:T(8,128)(2,1)}, bf16[208,768]{1,0:T(8,128)(2,1)S(1)}, u32[]{:S(2)}, u32[]{:S(2)}) collective-permute-start(bf16[208,768]{1,0:T(8,128)(2,1)} %get-tuple-element.179), channel_id=1, source_target_pairs={{0,2},{1,3},{2,0},{3,1},{4,6},{5,7},{6,4},{7,5},{8,10},{9,11},{10,... | collective-permute-start | bytes 958472 | tf_op jit(solution)/shard_map/ppermute | solution.py:661
  8.3 19.5 %collective-permute-start.3 = (bf16[784,768]{1,0:T(8,128)(2,1)}, bf16[784,768]{1,0:T(8,128)(2,1)S(1)}, u32[]{:S(2)}, u32[]{:S(2)}) collective-permute-start(bf16[784,768]{1,0:T(8,128)(2,1)} %get-tuple-element.184.refs_1_.weights), channel_id=1, source_target_pairs={{0,1},{1,0},{2,3},{3,2},{4,5},{5,4},{6,7},{7,6},{8,9},{9,8},{10,11... | collective-permute-start | bytes 3612680 | tf_op jit(solution)/shard_map/ppermute | solution.py:661
  8.3 28.7 %collective-permute-start.5 = (bf16[384,768]{1,0:T(8,128)(2,1)}, bf16[384,768]{1,0:T(8,128)(2,1)S(1)}, u32[]{:S(2)}, u32[]{:S(2)}) collective-permute-start(bf16[384,768]{1,0:T(8,128)(2,1)} %get-tuple-element.189), channel_id=1, source_target_pairs={{0,2},{1,3},{2,0},{3,1},{4,6},{5,7},{6,4},{7,5},{8,10},{9,11},{10,... | collective-permute-start | bytes 1769480 | tf_op jit(solution)/shard_map/ppermute | solution.py:661
  16.9 9.2 %collective-permute-start.1 = (bf16[192,768]{1,0:T(8,128)(2,1)S(1)}, bf16[192,768]{1,0:T(8,128)(2,1)S(1)}, u32[]{:S(2)}, u32[]{:S(2)}) collective-permute-start(bf16[192,768]{1,0:T(8,128)(2,1)S(1)} %slice.84.refs_0_), channel_id=1, source_target_pairs={{0,4},{1,9},{2,6},{3,11},{4,0},{5,13},{6,2},{7,15},{8,12},{9,1},{1... | collective-permute-start | bytes 884744 | tf_op jit(solution)/shard_map/ppermute | solution.py:661
  20.3 4.3 %copy-start.40 = (bf16[384,768]{1,0:T(8,128)(2,1)S(1)}, bf16[384,768]{1,0:T(8,128)(2,1)}, u32[]{:S(2)}) copy-start(bf16[384,768]{1,0:T(8,128)(2,1)} %get-tuple-element.194) | copy-start | bytes 1769476
  24.5 7.6 %copy-start.26 = (bf16[3,512,512]{2,1,0:T(8,128)(2,1)}, bf16[3,512,512]{2,1,0:T(8,128)(2,1)S(1)}, u32[]{:S(2)}) copy-start(bf16[3,512,512]{2,1,0:T(8,128)(2,1)S(1)} %get-tuple-element.272.probs) | copy-start | bytes 4718596
  24.5 7.6 %copy-start.34 = (bf16[576,512]{1,0:T(8,128)(2,1)}, bf16[576,512]{1,0:T(8,128)(2,1)S(1)}, u32[]{:S(2)}) copy-start(bf16[576,512]{1,0:T(8,128)(2,1)S(1)} %get-tuple-element.271.qkv) | copy-start | bytes 1769476
  24.5 18.6 %collective-permute-start.6 = (bf16[384,768]{1,0:T(8,128)(2,1)S(1)}, bf16[384,768]{1,0:T(8,128)(2,1)S(1)}, u32[]{:S(2)}, u32[]{:S(2)}) collective-permute-start(bf16[384,768]{1,0:T(8,128)(2,1)S(1)} %copy-done.40), channel_id=1, source_target_pairs={{0,2},{1,3},{2,0},{3,1},{4,6},{5,7},{6,4},{7,5},{8,10},{9,11},{10,... | collective-permute-start | bytes 1769480 | tf_op jit(solution)/shard_map/ppermute | solution.py:661
  26.2 10.0 %copy-start.9 = (s32[34]{0:T(128)S(1)}, s32[34]{0:T(128)}, u32[]{:S(2)}) copy-start(s32[34]{0:T(128)} %broadcast_select_fusion.plan) | copy-start | bytes 412
  26.2 9.9 %collective-permute-start.2 = (bf16[384,768]{1,0:T(8,128)(2,1)S(1)}, bf16[384,768]{1,0:T(8,128)(2,1)S(1)}, u32[]{:S(2)}, u32[]{:S(2)}) collective-permute-start(bf16[384,768]{1,0:T(8,128)(2,1)S(1)} %pad_maximum_fusion.1), channel_id=1, source_target_pairs={{0,8},{1,5},{2,10},{3,7},{4,12},{5,1},{6,14},{7,3},{8,0},{9,13},{1... | collective-permute-start | bytes 1769480 | tf_op jit(solution)/shard_map/ppermute | solution.py:661
  27.8 4.3 %copy-start.13 = (bf16[784,768]{1,0:T(8,128)(2,1)}, bf16[784,768]{1,0:T(8,128)(2,1)S(1)}, u32[]{:S(2)}) copy-start(bf16[784,768]{1,0:T(8,128)(2,1)S(1)} %collective-permute-done.3.refs_1_.weights) | copy-start | bytes 3612676
  32.1 4.8 %copy-start.30 = (bf16[576,512]{1,0:T(8,128)(2,1)}, bf16[576,512]{1,0:T(8,128)(2,1)S(1)}, u32[]{:S(2)}) copy-start(bf16[576,512]{1,0:T(8,128)(2,1)S(1)} %get-tuple-element.273.qkv) | copy-start | bytes 1769476
  36.9 6.2 %copy-start.1 = (bf16[784,768]{1,0:T(8,128)(2,1)}, bf16[784,768]{1,0:T(8,128)(2,1)S(1)}, u32[]{:S(2)}) copy-start(bf16[784,768]{1,0:T(8,128)(2,1)S(1)} %join.3.refs_1_.weights) | copy-start | bytes 3612676
  36.9 8.3 %collective-permute-start.4 = (bf16[784,768]{1,0:T(8,128)(2,1)S(1)}, bf16[784,768]{1,0:T(8,128)(2,1)S(1)}, u32[]{:S(2)}, u32[]{:S(2)}) collective-permute-start(bf16[784,768]{1,0:T(8,128)(2,1)S(1)} %join.3.refs_1_.weights), channel_id=1, source_target_pairs={{0,1},{1,0},{2,3},{3,2},{4,5},{5,4},{6,7},{7,6},{8,9},{9,8},{10,11... | collective-permute-start | bytes 3612680 | tf_op jit(solution)/shard_map/ppermute | solution.py:661
  37.0 8.1 %copy-start.3 = (bf16[768,768]{1,0:T(8,128)(2,1)S(1)}, bf16[768,768]{1,0:T(8,128)(2,1)}, u32[]{:S(2)}) copy-start(bf16[768,768]{1,0:T(8,128)(2,1)} %refs_4_.3) | copy-start | bytes 3538948
  37.0 8.2 %copy-start.24 = (f32[8,768]{1,0:T(8,128)S(1)}, f32[8,768]{1,0:T(8,128)}, u32[]{:S(2)}) copy-start(f32[8,768]{1,0:T(8,128)} %get-tuple-element.197.refs_3_.refs_5_.refs_8_) | copy-start | bytes 73732
  37.1 13.8 %collective-permute-start.7 = (bf16[192,768]{1,0:T(8,128)(2,1)S(1)}, bf16[192,768]{1,0:T(8,128)(2,1)S(1)}, u32[]{:S(2)}, u32[]{:S(2)}) collective-permute-start(bf16[192,768]{1,0:T(8,128)(2,1)S(1)} %get-tuple-element.351.refs_0_), channel_id=1, source_target_pairs={{0,4},{1,5},{2,6},{3,7},{4,0},{5,1},{6,2},{7,3},{8,12},{9,13},{10,... | collective-permute-start | bytes 884744 | tf_op jit(solution)/shard_map/ppermute | solution.py:661
  37.6 13.8 %collective-permute-start.8 = (bf16[192,768]{1,0:T(8,128)(2,1)S(1)}, bf16[192,768]{1,0:T(8,128)(2,1)S(1)}, u32[]{:S(2)}, u32[]{:S(2)}) collective-permute-start(bf16[192,768]{1,0:T(8,128)(2,1)S(1)} %get-tuple-element.351.refs_0_), channel_id=1, source_target_pairs={{0,8},{1,9},{2,10},{3,11},{4,12},{5,13},{6,14},{7,15},{8,0},{9,1},... | collective-permute-start | bytes 884744 | tf_op jit(solution)/shard_map/ppermute | solution.py:661
  43.1 7.7 %copy-start.32 = (bf16[576,512]{1,0:T(8,128)(2,1)}, bf16[576,512]{1,0:T(8,128)(2,1)S(1)}, u32[]{:S(2)}) copy-start(bf16[576,512]{1,0:T(8,128)(2,1)S(1)} %get-tuple-element.217.qkv) | copy-start | bytes 1769476
  43.1 12.8 %collective-permute-start.10 = (bf16[192,768]{1,0:T(8,128)(2,1)S(1)}, bf16[192,768]{1,0:T(8,128)(2,1)S(1)}, u32[]{:S(2)}, u32[]{:S(2)}) collective-permute-start(bf16[192,768]{1,0:T(8,128)(2,1)S(1)} %get-tuple-element.349.refs_0_), channel_id=1, source_target_pairs={{0,4},{1,5},{2,6},{3,7},{4,0},{5,1},{6,2},{7,3},{8,12},{9,13},{10,... | collective-permute-start | bytes 884744 | tf_op jit(solution)/shard_map/ppermute | solution.py:661
  44.7 11.3 %collective-permute-start.11 = (bf16[192,768]{1,0:T(8,128)(2,1)S(1)}, bf16[192,768]{1,0:T(8,128)(2,1)S(1)}, u32[]{:S(2)}, u32[]{:S(2)}) collective-permute-start(bf16[192,768]{1,0:T(8,128)(2,1)S(1)} %get-tuple-element.349.refs_0_), channel_id=1, source_target_pairs={{0,8},{1,9},{2,10},{3,11},{4,12},{5,13},{6,14},{7,15},{8,0},{9,1},... | collective-permute-start | bytes 884744 | tf_op jit(solution)/shard_map/ppermute | solution.py:661
  45.2 5.7 %copy-start.15 = (bf16[784,768]{1,0:T(8,128)(2,1)}, bf16[784,768]{1,0:T(8,128)(2,1)S(1)}, u32[]{:S(2)}) copy-start(bf16[784,768]{1,0:T(8,128)(2,1)S(1)} %collective-permute-done.4.refs_1_.weights) | copy-start | bytes 3612676
  45.2 8.9 %collective-permute-start.12 = (bf16[768,768]{1,0:T(8,128)(2,1)S(1)}, bf16[768,768]{1,0:T(8,128)(2,1)S(1)}, u32[]{:S(2)}, u32[]{:S(2)}) collective-permute-start(bf16[768,768]{1,0:T(8,128)(2,1)S(1)} %copy-done.3), channel_id=1, source_target_pairs={{0,1},{1,0},{2,3},{3,2},{4,5},{5,4},{6,7},{7,6},{8,9},{9,8},{10,11... | collective-permute-start | bytes 3538952 | tf_op jit(solution)/shard_map/ppermute | solution.py:661
  45.2 5.6 %copy-start.5 = (bf16[768,768]{1,0:T(8,128)(2,1)S(1)}, bf16[768,768]{1,0:T(8,128)(2,1)}, u32[]{:S(2)}) copy-start(bf16[768,768]{1,0:T(8,128)(2,1)} %refs_5_.3) | copy-start | bytes 3538948
  50.9 3.2 %collective-permute-start.13 = (bf16[768,768]{1,0:T(8,128)(2,1)S(1)}, bf16[768,768]{1,0:T(8,128)(2,1)S(1)}, u32[]{:S(2)}, u32[]{:S(2)}) collective-permute-start(bf16[768,768]{1,0:T(8,128)(2,1)S(1)} %copy-done.5), channel_id=1, source_target_pairs={{0,1},{1,0},{2,3},{3,2},{4,5},{5,4},{6,7},{7,6},{8,9},{9,8},{10,11... | collective-permute-start | bytes 3538952 | tf_op jit(solution)/shard_map/ppermute | solution.py:661
  52.1 6.9 %collective-permute-start.9 = (bf16[768,768]{1,0:T(8,128)(2,1)S(1)}, bf16[768,768]{1,0:T(8,128)(2,1)S(1)}, u32[]{:S(2)}, u32[]{:S(2)}) collective-permute-start(bf16[768,768]{1,0:T(8,128)(2,1)S(1)} %join.4.refs_1_.refs_4_), channel_id=1, source_target_pairs={{0,1},{1,0},{2,3},{3,2},{4,5},{5,4},{6,7},{7,6},{8,9},{9,8},{10,11... | collective-permute-start | bytes 3538952 | tf_op jit(solution)/shard_map/ppermute | solution.py:661
  56.6 3.0 %collective-permute-start.14 = (bf16[768,768]{1,0:T(8,128)(2,1)S(1)}, bf16[768,768]{1,0:T(8,128)(2,1)S(1)}, u32[]{:S(2)}, u32[]{:S(2)}) collective-permute-start(bf16[768,768]{1,0:T(8,128)(2,1)S(1)} %join.5.refs_2_.refs_5_), channel_id=1, source_target_pairs={{0,1},{1,0},{2,3},{3,2},{4,5},{5,4},{6,7},{7,6},{8,9},{9,8},{10,11... | collective-permute-start | bytes 3538952 | tf_op jit(solution)/shard_map/ppermute | solution.py:661
  65.6 5.2 %collective-permute-start.15 = (bf16[768,768]{1,0:T(8,128)(2,1)S(1)}, bf16[768,768]{1,0:T(8,128)(2,1)S(1)}, u32[]{:S(2)}, u32[]{:S(2)}) collective-permute-start(bf16[768,768]{1,0:T(8,128)(2,1)S(1)} %get-tuple-element.229), channel_id=1, source_target_pairs={{0,1},{1,0},{2,3},{3,2},{4,5},{5,4},{6,7},{7,6},{8,9},{9,8},{10,11... | collective-permute-start | bytes 3538952 | tf_op jit(solution)/shard_map/ppermute | solution.py:661
  67.5 3.4 %collective-permute-start.16 = (bf16[768,768]{1,0:T(8,128)(2,1)S(1)}, bf16[768,768]{1,0:T(8,128)(2,1)S(1)}, u32[]{:S(2)}, u32[]{:S(2)}) collective-permute-start(bf16[768,768]{1,0:T(8,128)(2,1)S(1)} %get-tuple-element.231), channel_id=1, source_target_pairs={{0,1},{1,0},{2,3},{3,2},{4,5},{5,4},{6,7},{7,6},{8,9},{9,8},{10,11... | collective-permute-start | bytes 3538952 | tf_op jit(solution)/shard_map/ppermute | solution.py:661
  70.4 5.5 %collective-permute-start.17 = (bf16[768,768]{1,0:T(8,128)(2,1)S(1)}, bf16[768,768]{1,0:T(8,128)(2,1)S(1)}, u32[]{:S(2)}, u32[]{:S(2)}) collective-permute-start(bf16[768,768]{1,0:T(8,128)(2,1)S(1)} %get-tuple-element.235), channel_id=1, source_target_pairs={{0,1},{1,0},{2,3},{3,2},{4,5},{5,4},{6,7},{7,6},{8,9},{9,8},{10,11... | collective-permute-start | bytes 3538952 | tf_op jit(solution)/shard_map/ppermute | solution.py:661
  72.1 16.3 %collective-permute-start.18 = (bf16[768,768]{1,0:T(8,128)(2,1)S(1)}, bf16[768,768]{1,0:T(8,128)(2,1)S(1)}, u32[]{:S(2)}, u32[]{:S(2)}) collective-permute-start(bf16[768,768]{1,0:T(8,128)(2,1)S(1)} %get-tuple-element.238), channel_id=1, source_target_pairs={{0,2},{1,5},{2,0},{3,7},{4,6},{5,1},{6,4},{7,3},{8,10},{9,13},{10,... | collective-permute-start | bytes 3538952 | tf_op jit(solution)/shard_map/ppermute | solution.py:661
  73.2 3.8 %copy-start.20 = (bf16[768,768]{1,0:T(8,128)(2,1)S(1)}, bf16[768,768]{1,0:T(8,128)(2,1)}, u32[]{:S(2)}) copy-start(bf16[768,768]{1,0:T(8,128)(2,1)} %copy-done.19) | copy-start | bytes 3538948
  79.7 16.3 %collective-permute-start.20 = (bf16[768,768]{1,0:T(8,128)(2,1)S(1)}, bf16[768,768]{1,0:T(8,128)(2,1)S(1)}, u32[]{:S(2)}, u32[]{:S(2)}) collective-permute-start(bf16[768,768]{1,0:T(8,128)(2,1)S(1)} %get-tuple-element.262), channel_id=1, source_target_pairs={{0,1},{1,0},{2,3},{3,2},{4,5},{5,4},{6,7},{7,6},{8,9},{9,8},{10,11... | collective-permute-start | bytes 3538952 | tf_op jit(solution)/shard_map/ppermute | solution.py:661
  84.7 11.3 %collective-permute-start.21 = (bf16[2,192,768]{2,1,0:T(8,128)(2,1)S(1)}, bf16[2,192,768]{2,1,0:T(8,128)(2,1)S(1)}, u32[]{:S(2)}, u32[]{:S(2)}) collective-permute-start(bf16[2,192,768]{2,1,0:T(8,128)(2,1)S(1)} %get-tuple-element.263), channel_id=1, source_target_pairs={{0,1},{1,0},{2,3},{3,2},{4,5},{5,4},{6,7},{7,6},{8,9},{9,8},{10,11... | collective-permute-start | bytes 1769480 | tf_op jit(solution)/shard_map/ppermute | solution.py:661
  89.3 9.9 %collective-permute-start.19 = (bf16[384,768]{1,0:T(8,128)(2,1)S(1)}, bf16[384,768]{1,0:T(8,128)(2,1)S(1)}, u32[]{:S(2)}, u32[]{:S(2)}) collective-permute-start(bf16[384,768]{1,0:T(8,128)(2,1)S(1)} %get-tuple-element.256), channel_id=1, source_target_pairs={{0,4},{1,3},{2,6},{3,1},{4,0},{5,7},{6,2},{7,5},{8,12},{9,11},{10,... | collective-permute-start | bytes 1769480 | tf_op jit(solution)/shard_map/ppermute | solution.py:661
  90.0 6.0 %copy-start.8 = (bf16[768,768]{1,0:T(8,128)(2,1)S(1)}, bf16[768,768]{1,0:T(8,128)(2,1)}, u32[]{:S(2)}) copy-start(bf16[768,768]{1,0:T(8,128)(2,1)} %copy-done.7) | copy-start | bytes 3538948
  95.9 11.8 %collective-permute-start.22 = (bf16[576,768]{1,0:T(8,128)(2,1)S(1)}, bf16[576,768]{1,0:T(8,128)(2,1)S(1)}, u32[]{:S(2)}, u32[]{:S(2)}) collective-permute-start(bf16[576,768]{1,0:T(8,128)(2,1)S(1)} %get-tuple-element.264), channel_id=1, source_target_pairs={{0,1},{1,0},{2,3},{3,2},{4,5},{5,4},{6,7},{7,6},{8,9},{9,8},{10,11... | collective-permute-start | bytes 2654216 | tf_op jit(solution)/shard_map/ppermute | solution.py:661
  96.0 5.8 %copy-start.33 = (bf16[576,512]{1,0:T(8,128)(2,1)S(1)}, bf16[576,512]{1,0:T(8,128)(2,1)}, u32[]{:S(2)}) copy-start(bf16[576,512]{1,0:T(8,128)(2,1)} %copy-done.32) | copy-start | bytes 1769476
  97.4 4.4 %copy-start.2 = (bf16[784,768]{1,0:T(8,128)(2,1)S(1)}, bf16[784,768]{1,0:T(8,128)(2,1)}, u32[]{:S(2)}) copy-start(bf16[784,768]{1,0:T(8,128)(2,1)} %copy-done.1) | copy-start | bytes 3612676
  97.4 19.7 %collective-permute-start.23 = (bf16[960,768]{1,0:T(8,128)(2,1)S(1)}, bf16[960,768]{1,0:T(8,128)(2,1)S(1)}, u32[]{:S(2)}, u32[]{:S(2)}) collective-permute-start(bf16[960,768]{1,0:T(8,128)(2,1)S(1)} %get-tuple-element.266), channel_id=1, source_target_pairs={{0,2},{1,5},{2,0},{3,7},{4,6},{5,1},{6,4},{7,3},{8,10},{9,13},{10,... | collective-permute-start | bytes 4423688 | tf_op jit(solution)/shard_map/ppermute | solution.py:661
  100.2 14.1 %collective-permute-start.24 = (bf16[192,768]{1,0:T(8,128)(2,1)S(1)}, bf16[192,768]{1,0:T(8,128)(2,1)S(1)}, u32[]{:S(2)}, u32[]{:S(2)}) collective-permute-start(bf16[192,768]{1,0:T(8,128)(2,1)S(1)} %get-tuple-element.268), channel_id=1, source_target_pairs={{0,8},{1,17},{2,10},{3,19},{4,12},{5,21},{6,14},{7,23},{8,0},{9,25... | collective-permute-start | bytes 884744 | tf_op jit(solution)/shard_map/ppermute | solution.py:661
  101.9 5.9 %copy-start.14 = (bf16[784,768]{1,0:T(8,128)(2,1)S(1)}, bf16[784,768]{1,0:T(8,128)(2,1)}, u32[]{:S(2)}) copy-start(bf16[784,768]{1,0:T(8,128)(2,1)} %copy-done.13) | copy-start | bytes 3612676
  101.9 5.9 %copy-start.31 = (bf16[576,512]{1,0:T(8,128)(2,1)S(1)}, bf16[576,512]{1,0:T(8,128)(2,1)}, u32[]{:S(2)}) copy-start(bf16[576,512]{1,0:T(8,128)(2,1)} %copy-done.30) | copy-start | bytes 1769476
  113.7 12.8 %collective-permute-start.25 = (bf16[576,768]{1,0:T(8,128)(2,1)S(1)}, bf16[576,768]{1,0:T(8,128)(2,1)S(1)}, u32[]{:S(2)}, u32[]{:S(2)}) collective-permute-start(bf16[576,768]{1,0:T(8,128)(2,1)S(1)} %get-tuple-element.280), channel_id=1, source_target_pairs={{0,1},{1,0},{2,3},{3,2},{4,5},{5,4},{6,7},{7,6},{8,9},{9,8},{10,11... | collective-permute-start | bytes 2654216 | tf_op jit(solution)/shard_map/ppermute | solution.py:661
  115.0 11.5 %collective-permute-start.26 = (bf16[96,768]{1,0:T(8,128)(2,1)S(1)}, bf16[96,768]{1,0:T(8,128)(2,1)S(1)}, u32[]{:S(2)}, u32[]{:S(2)}) collective-permute-start(bf16[96,768]{1,0:T(8,128)(2,1)S(1)} %get-tuple-element.282), channel_id=1, source_target_pairs={{0,16},{1,9},{2,18},{3,11},{4,20},{5,13},{6,22},{7,15},{8,24},{9,1... | collective-permute-start | bytes 442376 | tf_op jit(solution)/shard_map/ppermute | solution.py:661
  118.2 11.5 %collective-permute-start.27 = (bf16[480,768]{1,0:T(8,128)(2,1)S(1)}, bf16[480,768]{1,0:T(8,128)(2,1)S(1)}, u32[]{:S(2)}, u32[]{:S(2)}) collective-permute-start(bf16[480,768]{1,0:T(8,128)(2,1)S(1)} %get-tuple-element.284), channel_id=1, source_target_pairs={{0,4},{1,3},{2,6},{3,1},{4,0},{5,7},{6,2},{7,5},{8,12},{9,11},{10,... | collective-permute-start | bytes 2211848 | tf_op jit(solution)/shard_map/ppermute | solution.py:661
  130.8 14.1 %collective-permute-start.28 = (bf16[608,768]{1,0:T(8,128)(2,1)S(1)}, bf16[608,768]{1,0:T(8,128)(2,1)S(1)}, u32[]{:S(2)}, u32[]{:S(2)}) collective-permute-start(bf16[608,768]{1,0:T(8,128)(2,1)S(1)} %get-tuple-element.302), channel_id=1, source_target_pairs={{0,2},{1,5},{2,0},{3,7},{4,6},{5,1},{6,4},{7,3},{8,10},{9,13},{10,... | collective-permute-start | bytes 2801672 | tf_op jit(solution)/shard_map/ppermute | solution.py:661
  131.7 13.2 %collective-permute-start.29 = (bf16[96,768]{1,0:T(8,128)(2,1)S(1)}, bf16[96,768]{1,0:T(8,128)(2,1)S(1)}, u32[]{:S(2)}, u32[]{:S(2)}) collective-permute-start(bf16[96,768]{1,0:T(8,128)(2,1)S(1)} %add_convert_fusion.1), channel_id=1, source_target_pairs={{0,16},{1,9},{2,18},{3,11},{4,20},{5,13},{6,22},{7,15},{8,24},{9,1... | collective-permute-start | bytes 442376 | tf_op jit(solution)/shard_map/ppermute | solution.py:661
  135.1 13.1 %collective-permute-start.32 = (bf16[240,768]{1,0:T(8,128)(2,1)S(1)}, bf16[240,768]{1,0:T(8,128)(2,1)S(1)}, u32[]{:S(2)}, u32[]{:S(2)}) collective-permute-start(bf16[240,768]{1,0:T(8,128)(2,1)S(1)} %get-tuple-element.305), channel_id=1, source_target_pairs={{0,8},{1,17},{2,10},{3,19},{4,12},{5,21},{6,14},{7,23},{8,0},{9,25... | collective-permute-start | bytes 1105928 | tf_op jit(solution)/shard_map/ppermute | solution.py:661
  145.8 16.7 %collective-permute-start.30 = (bf16[320,768]{1,0:T(8,128)(2,1)S(1)}, bf16[320,768]{1,0:T(8,128)(2,1)S(1)}, u32[]{:S(2)}, u32[]{:S(2)}) collective-permute-start(bf16[320,768]{1,0:T(8,128)(2,1)S(1)} %get-tuple-element.310), channel_id=1, source_target_pairs={{0,4},{1,3},{2,6},{3,1},{4,0},{5,7},{6,2},{7,5},{8,12},{9,11},{10,... | collective-permute-start | bytes 1474568 | tf_op jit(solution)/shard_map/ppermute | solution.py:661
  147.1 15.0 %collective-permute-start.31 = (bf16[192,768]{1,0:T(8,128)(2,1)S(1)}, bf16[192,768]{1,0:T(8,128)(2,1)S(1)}, u32[]{:S(2)}, u32[]{:S(2)}) collective-permute-start(bf16[192,768]{1,0:T(8,128)(2,1)S(1)} %pad_maximum_fusion.5), channel_id=1, source_target_pairs={{0,8},{1,17},{2,10},{3,19},{4,12},{5,21},{6,14},{7,23},{8,0},{9,25... | collective-permute-start | bytes 884744 | tf_op jit(solution)/shard_map/ppermute | solution.py:661
  148.9 14.4 %collective-permute-start.34 = (bf16[120,768]{1,0:T(8,128)(2,1)S(1)}, bf16[120,768]{1,0:T(8,128)(2,1)S(1)}, u32[]{:S(2)}, u32[]{:S(2)}) collective-permute-start(bf16[120,768]{1,0:T(8,128)(2,1)S(1)} %get-tuple-element.313), channel_id=1, source_target_pairs={{0,16},{1,9},{2,18},{3,11},{4,20},{5,13},{6,22},{7,15},{8,24},{9,1... | collective-permute-start | bytes 552968 | tf_op jit(solution)/shard_map/ppermute | solution.py:661
  162.2 15.0 %collective-permute-start.36 = (bf16[384,768]{1,0:T(8,128)(2,1)S(1)}, bf16[384,768]{1,0:T(8,128)(2,1)S(1)}, u32[]{:S(2)}, u32[]{:S(2)}) collective-permute-start(bf16[384,768]{1,0:T(8,128)(2,1)S(1)} %pad_maximum_fusion.2.mine), channel_id=1, source_target_pairs={{0,4},{1,5},{2,6},{3,7},{4,0},{5,1},{6,2},{7,3},{8,12},{9,13},{10,... | collective-permute-start | bytes 1769480 | tf_op jit(solution)/shard_map/ppermute | solution.py:661
  163.2 11.1 %collective-permute-start.33 = (bf16[176,768]{1,0:T(8,128)(2,1)S(1)}, bf16[176,768]{1,0:T(8,128)(2,1)S(1)}, u32[]{:S(2)}, u32[]{:S(2)}) collective-permute-start(bf16[176,768]{1,0:T(8,128)(2,1)S(1)} %get-tuple-element.318), channel_id=1, source_target_pairs={{0,8},{1,17},{2,10},{3,19},{4,12},{5,21},{6,14},{7,23},{8,0},{9,25... | collective-permute-start | bytes 811016 | tf_op jit(solution)/shard_map/ppermute | solution.py:661
  163.3 11.7 %collective-permute-start.37 = (bf16[120,768]{1,0:T(8,128)(2,1)S(1)}, bf16[120,768]{1,0:T(8,128)(2,1)S(1)}, u32[]{:S(2)}, u32[]{:S(2)}) collective-permute-start(bf16[120,768]{1,0:T(8,128)(2,1)S(1)} %add_convert_fusion), channel_id=1, source_target_pairs={{0,16},{1,9},{2,18},{3,11},{4,20},{5,13},{6,22},{7,15},{8,24},{9,1... | collective-permute-start | bytes 552968 | tf_op jit(solution)/shard_map/ppermute | solution.py:661
  175.0 8.3 %collective-permute-start.35 = (bf16[104,768]{1,0:T(8,128)(2,1)S(1)}, bf16[104,768]{1,0:T(8,128)(2,1)S(1)}, u32[]{:S(2)}, u32[]{:S(2)}) collective-permute-start(bf16[104,768]{1,0:T(8,128)(2,1)S(1)} %get-tuple-element.324), channel_id=1, source_target_pairs={{0,16},{1,9},{2,18},{3,11},{4,20},{5,13},{6,22},{7,15},{8,24},{9,1... | collective-permute-start | bytes 479240 | tf_op jit(solution)/shard_map/ppermute | solution.py:661
  175.1 11.5 %collective-permute-start.39 = (bf16[240,768]{1,0:T(8,128)(2,1)S(1)}, bf16[240,768]{1,0:T(8,128)(2,1)S(1)}, u32[]{:S(2)}, u32[]{:S(2)}) collective-permute-start(bf16[240,768]{1,0:T(8,128)(2,1)S(1)} %pad_maximum_fusion.4), channel_id=1, source_target_pairs={{0,8},{1,17},{2,10},{3,19},{4,12},{5,21},{6,14},{7,23},{8,0},{9,25... | collective-permute-start | bytes 1105928 | tf_op jit(solution)/shard_map/ppermute | solution.py:661
  183.3 9.7 %copy-start.36 = (bf16[72,768]{1,0:T(8,128)(2,1)}, bf16[72,768]{1,0:T(8,128)(2,1)S(1)}, u32[]{:S(2)}) copy-start(bf16[72,768]{1,0:T(8,128)(2,1)S(1)} %add_convert_fusion.2) | copy-start | bytes 331780
  183.3 9.6 %collective-permute-start.38 = (bf16[72,768]{1,0:T(8,128)(2,1)S(1)}, bf16[72,768]{1,0:T(8,128)(2,1)S(1)}, u32[]{:S(2)}, u32[]{:S(2)}) collective-permute-start(bf16[72,768]{1,0:T(8,128)(2,1)S(1)} %add_convert_fusion.2), channel_id=1, source_target_pairs={{0,16},{1,9},{2,18},{3,11},{4,20},{5,13},{6,22},{7,15},{8,24},{9,1... | collective-permute-start | bytes 331784 | tf_op jit(solution)/shard_map/ppermute | solution.py:661
  186.7 19.1 %collective-permute-start.43 = (bf16[480,768]{1,0:T(8,128)(2,1)S(1)}, bf16[480,768]{1,0:T(8,128)(2,1)S(1)}, u32[]{:S(2)}, u32[]{:S(2)}) collective-permute-start(bf16[480,768]{1,0:T(8,128)(2,1)S(1)} %pad_maximum_fusion.mine), channel_id=1, source_target_pairs={{0,4},{1,5},{2,6},{3,7},{4,0},{5,1},{6,2},{7,3},{8,12},{9,13},{10,... | collective-permute-start | bytes 2211848 | tf_op jit(solution)/shard_map/ppermute | solution.py:661
  193.0 6.0 %collective-permute-start.40 = (bf16[144,768]{1,0:T(8,128)(2,1)S(1)}, bf16[144,768]{1,0:T(8,128)(2,1)S(1)}, u32[]{:S(2)}, u32[]{:S(2)}) collective-permute-start(bf16[144,768]{1,0:T(8,128)(2,1)S(1)} %pad_maximum_fusion.6), channel_id=1, source_target_pairs={{0,8},{1,17},{2,10},{3,19},{4,12},{5,21},{6,14},{7,23},{8,0},{9,25... | collective-permute-start | bytes 663560 | tf_op jit(solution)/shard_map/ppermute | solution.py:661
  193.6 1.4 collective-permute-start.41
  200.7 10.8 %collective-permute-start.42 = (bf16[288,768]{1,0:T(8,128)(2,1)S(1)}, bf16[288,768]{1,0:T(8,128)(2,1)}, u32[]{:S(2)}, u32[]{:S(2)}) collective-permute-start(bf16[288,768]{1,0:T(8,128)(2,1)S(1)} %pad_maximum_fusion.3.mine), channel_id=1, source_target_pairs={{0,4},{1,5},{2,6},{3,7},{4,0},{5,1},{6,2},{7,3},{8,12},{9,13},{10,... | collective-permute-start | bytes 1327112 | tf_op jit(solution)/shard_map/ppermute | solution.py:661
  (21 other events, 44.3 us)
where the time goes:
time: 216 us; the launch traced here: 215 us
  Pallas kernels  91.3 us (42%)
  waiting for transfers between devices  67.3 us (31%)
  starting transfers between devices  41.6 us (19%)
  local copies, waits for them, and re-layouts  7.31 us (3%)
  other arithmetic  6.03 us (3%)
    pallas_call x34, Pallas kernels, run(): pl.pallas_call(kernel, in_specs=specs, out_specs=[pl.BlockSpec(memory_spa...  80.3 us
    ppermute x44, waiting for transfers between devices, swap(): return lax.ppermute(value, ('dp', 'tensor'), pairs)  67.3 us
    ppermute x44, starting transfers between devices, swap(): return lax.ppermute(value, ('dp', 'tensor'), pairs)  41.6 us
    pallas_call x3, Pallas kernels, finish(): pl.pallas_call(functools.partial(finish_kernel, sizes), grid_spec=pltpu.P...  7.33 us
    unnamed x82, local copies, waits for them, and re-layouts  4.93 us
  transfers between devices with their start and end apart: 44, of which 16 were waited for; matrix products, arithmetic and copies ran while one was open for 3% of the time, Pallas kernels for 36%

commit v1 on v0

--- a/solution.py
+++ b/solution.py
@@ -57,50 +57,75 @@
     )(*ops)
 
 
-def pack_kernel(plan, wq, wk, wv, wo, wu, wd, *refs):
-    vectors, refs = refs[:9], refs[9:]
-    out, near, up_far, down_far, table, packed, piece, lines, *lists, sem = refs
+def near_kernel(plan, wq, wk, wv, wo, bq, bv, bu, out, *lines):
+    sem = lines[-1]
+    local, width = wq.shape
+    for i, ref in enumerate((wq, wk, wv, wo)):
+
+        @pl.when(plan[BY_B] == i)
+        def _(ref=ref):
+            pltpu.make_async_copy(ref, out.at[pl.ds(0, local)], sem.at[0]).start()
+
+    copies = [
+        pltpu.make_async_copy(ref, line, sem.at[1]) for ref, line in zip((bq, bv, bu), lines)
+    ]
+    for copy in copies:
+        copy.start()
+    out[local:, :] = jnp.zeros((BIAS_ROWS, width), BF)
+    for copy in copies:
+        copy.wait()
+    q, v, u = lines[:3]
+    out[local : local + 1, 0:local] = q[...].reshape(1, local)
+    out[local : local + 1, local : 2 * local] = v[...].reshape(1, local)
+    out[local + 1 : local + 2, :] = u[...].reshape(1, width)
+    pltpu.make_async_copy(wq, out.at[pl.ds(0, local)], sem.at[0]).wait()
+
+
+def pack_near(plan, w_query, w_key, w_value, w_output, biases):
+    local, width = w_output.shape
+    (out,) = pl.pallas_call(
+        near_kernel,
+        in_specs=[pl.BlockSpec(memory_space=pltpu.SMEM)] + [ANY] * 7,
+        out_specs=[pl.BlockSpec(memory_space=pltpu.VMEM)],
+        out_shape=[jax.ShapeDtypeStruct((local + BIAS_ROWS, width), BF)],
+        scratch_shapes=[
+            *[pltpu.VMEM(v.shape, BF) for v in biases],
+            pltpu.SemaphoreType.DMA((2,)),
+        ],
+        compiler_params=params(ALL_VMEM_BYTES),
+        name="pack_near",
+    )(plan, w_query.T, w_key.T, w_value.T, w_output, *biases)
+    return out
+
+
+def pack_kernel(plan, wq, wk, wv, wo, wu, wd, near, *refs):
+    vectors, refs = refs[:6], refs[6:]
+    out, up_far, down_far, table, packed, piece, lines, *lists, sem = refs
     local, width = wq.shape
     at = pl.multiple_of(plan[BY_B] * local, local)
-    copies = [
-        pltpu.make_async_copy(ref, packed.at[pl.ds(i * local, local)], sem.at[0])
-        for i, ref in enumerate((wq, wk, wv, wo))
-    ]
-    copies += [
-        pltpu.make_async_copy(ref, line, sem.at[0]) for ref, line in zip(vectors, lists)
-    ]
     opposite = pl.multiple_of(plan[QUARTERS + 3] * local, local)
     pieces = [
         pltpu.make_async_copy(ref.at[pl.ds(rows, local)], piece.at[i], sem.at[1])
         for i, (ref, rows) in enumerate(((wu, at), (wu, opposite), (wd, at), (wd, opposite)))
     ]
+    copies = [
+        pltpu.make_async_copy(ref, packed.at[pl.ds(i * local, local)], sem.at[0])
+        for i, ref in enumerate((wq, wk, wv, wo))
+    ]
+    copies.append(
+        pltpu.make_async_copy(
+            near.at[pl.ds(local, BIAS_ROWS)], packed.at[pl.ds(4 * local, BIAS_ROWS)], sem.at[0]
+        )
+    )
+    copies += [
+        pltpu.make_async_copy(ref, line, sem.at[0]) for ref, line in zip(vectors, lists)
+    ]
+    for copy in pieces:
+        copy.start()
     for copy in copies:
         copy.start()
-    for copy in pieces:
-        copy.start()
-    packed[4 * local :, :] = jnp.zeros((BIAS_ROWS, width), BF)
     lines[...] = jnp.zeros_like(lines)
-    for copy in copies:
-        copy.wait()
-    bq, bv, bu = lists[:3]
-    packed[4 * local : 4 * local + 1, 0:local] = bq[...].reshape(1, local)
-    packed[4 * local : 4 * local + 1, local : 2 * local] = bv[...].reshape(1, local)
-    packed[4 * local + 1 : 4 * local + 2, :] = bu[...].reshape(1, width)
-    outs = [
-        pltpu.make_async_copy(
-            packed.at[pl.ds(at, local)], near.at[pl.ds(0, local)], sem.at[2]
-        ),
-        pltpu.make_async_copy(
-            packed.at[pl.ds(4 * local, BIAS_ROWS)], near.at[pl.ds(local, BIAS_ROWS)], sem.at[2]
-        ),
-        pltpu.make_async_copy(packed, out, sem.at[2]),
-    ]
-    for copy in outs:
-        copy.start()
-    for i, ref in enumerate(lists[3:]):
-        lines[i : i + 1, :] = ref[...].astype(F32).reshape(1, width)
-    outs.append(pltpu.make_async_copy(lines, table, sem.at[2]))
-    outs[-1].start()
+    outs = []
     for copy in pieces:
         copy.wait()
     for i, ref in enumerate((up_far, down_far)):
@@ -108,15 +133,22 @@
             part = ref.at[pl.ds(h * local, local)]
             outs.append(pltpu.make_async_copy(piece.at[2 * i + h], part, sem.at[2]))
             outs[-1].start()
+    for copy in copies:
+        copy.wait()
+    outs.append(pltpu.make_async_copy(packed, out, sem.at[2]))
+    outs[-1].start()
+    for i, ref in enumerate(lists):
+        lines[i : i + 1, :] = ref[...].astype(F32).reshape(1, width)
+    outs.append(pltpu.make_async_copy(lines, table, sem.at[2]))
+    outs[-1].start()
     for copy in outs:
         copy.wait()
 
 
-def pack_weights(plan, w_query, w_key, w_value, w_output, w_up, w_down, vectors):
+def pack_weights(plan, w_query, w_key, w_value, w_output, w_up, w_down, near, vectors):
     local, width = w_output.shape
     shapes = [
         jax.ShapeDtypeStruct((4 * local + BIAS_ROWS, width), BF),
-        jax.ShapeDtypeStruct((local + BIAS_ROWS, width), BF),
         *[jax.ShapeDtypeStruct((2 * local, width), BF)] * 2,
         jax.ShapeDtypeStruct((8, width), F32),
     ]
@@ -125,12 +157,12 @@
         grid_spec=pltpu.PrefetchScalarGridSpec(
             num_scalar_prefetch=1,
             grid=(1,),
-            in_specs=[ANY] * 15,
-            out_specs=[ANY] * 5,
+            in_specs=[ANY] * 13,
+            out_specs=[ANY] * 4,
             scratch_shapes=[
                 pltpu.VMEM(shapes[0].shape, BF),
                 pltpu.VMEM((4, local, width), BF),
-                pltpu.VMEM(shapes[4].shape, F32),
+                pltpu.VMEM(shapes[3].shape, F32),
                 *[pltpu.VMEM(v.shape, BF) for v in vectors],
                 pltpu.SemaphoreType.DMA((3,)),
             ],
@@ -138,7 +170,7 @@
         out_shape=shapes,
         compiler_params=params(ALL_VMEM_BYTES),
         name="pack_weights",
-    )(plan, w_query.T, w_key.T, w_value.T, w_output, w_up, w_down, *vectors)
+    )(plan, w_query.T, w_key.T, w_value.T, w_output, w_up, w_down, near, *vectors)
 
 
 def join_kernel(base, plan, *refs):
@@ -170,7 +202,7 @@
     )
 
 
-def by_blocks(rows, body, block=64):
+def by_blocks(rows, body, block=128):
     def step(i, carry):
         body(pl.ds(pl.multiple_of(i * block, block), block))
         return carry
@@ -409,13 +441,7 @@
 
     lax.fori_loop(0, local // HEAD, one_head, 0, unroll=UNROLL)
     joined = work[0 : 3 * local, :]
-
-    def grad_rows(i, carry):
-        r = pl.ds(pl.multiple_of(i * local, local), local)
-        grads[r, :] = dot(work[r, :], tok[...], 1, 0).astype(BF)
-        return carry
-
-    lax.fori_loop(0, 3, grad_rows, 0)
+    grads[...] = dot(joined, tok[...], 1, 0).astype(BF)
     bias[...] = dot(jnp.ones((8, joined.shape[1]), BF), joined, 1, 1)
 
     def out_rows(r):
@@ -466,7 +492,7 @@
 
 
 def add_rows(target, to, left, right, at, rows):
-    block = next(b for b in (96, 64, 48, 32, 8) if rows % b == 0)
+    block = next(b for b in (32, 24, 8) if rows % b == 0)
 
     def body(i, carry):
         here = pl.ds(pl.multiple_of(at + i * block, 8), block)
@@ -479,7 +505,7 @@
 
 
 def copy_rows(target, to, source, at, rows):
-    block = next(b for b in (48, 40, 32, 24, 8) if rows % b == 0)
+    block = next(b for b in (32, 24, 16, 8) if rows % b == 0)
 
     def body(i, carry):
         here = pl.ds(pl.multiple_of(at + i * block, 8), block)
@@ -609,18 +635,21 @@
 def finish_kernel(sizes, plan, mine, theirs, *refs):
     outs, (sums, sem) = refs[:-2], refs[-2:]
     rows = mine.shape[0] // 4
-    for h in range(2):
-        for i in range(4):
-            where = pl.ds(pl.multiple_of(plan[PLACES + i] * rows, rows), rows)
-            at = (4 * h + i) * rows
-            sums[at : at + rows, :] = jnp.where(
-                plan[SIDE] == h, mine[where, :], theirs[where, :]
-            ).astype(F32)
-    copies, at = [], 0
-    for ref, size in zip(outs, sizes):
-        copies.append(pltpu.make_async_copy(sums.at[pl.ds(at, size)], ref, sem))
-        copies[-1].start()
-        at += size
+    copies = []
+    for i in range(8):
+        where = pl.ds(pl.multiple_of(plan[PLACES + i % 4] * rows, rows), rows)
+        begin, end = i * rows, (i + 1) * rows
+        sums[begin:end, :] = jnp.where(
+            plan[SIDE] == i // 4, mine[where, :], theirs[where, :]
+        ).astype(F32)
+        at = 0
+        for ref, size in zip(outs, sizes):
+            low, high = max(begin, at), min(end, at + size)
+            if low < high:
+                source, target = sums.at[pl.ds(low, high - low)], ref.at[pl.ds(low - at, high - low)]
+                copies.append(pltpu.make_async_copy(source, target, sem))
+                copies[-1].start()
+            at += size
     for copy in copies:
         copy.wait()
 
@@ -805,10 +834,10 @@
     local = w_query.shape[1]
     assert rows == SEQ_LEN and width == 4 * local and w_up.shape == (width, width)
     plan = make_plan()
-    pack_d, near, up_far, down_far, table = pack_weights(
-        plan, w_query, w_key, w_value, w_output, w_up, w_down,
-        (b_query, b_value, b_up, b_output, first_gain, first_shift, b_down, second_gain,
-         second_shift),
+    near = pack_near(plan, w_query, w_key, w_value, w_output, (b_query, b_value, b_up))
+    pack_d, up_far, down_far, table = pack_weights(
+        tie(plan, near), w_query, w_key, w_value, w_output, w_up, w_down, near,
+        (b_output, first_gain, first_shift, b_down, second_gain, second_shift),
     )
 
     far_pack = Gather(plan, near, BIAS_ROWS)
@@ -948,8 +977,8 @@
     grad_q, grad_k, grad_v = attn.result((local,) * 3)
 
     return (
-        tie(layer_out, attn.got).astype(BF),
-        grad_tokens.astype(BF),
+        tie(layer_out, attn.sent).astype(BF),
+        tie(grad_tokens, attn.sent).astype(BF),
         grad_q.T,
         grad_k.T,
         grad_v.T,

time: 216 us -> 213 us (0.986)
  waiting for transfers between devices: 67.3 us -> 64.8 us
    pallas_call x34, Pallas kernels: 80.3 us -> 76.9 us  [run(): pl.pallas_call(kernel, in_specs=specs, out_specs=[pl.BlockSpec(memory_spa...]
    ppermute x44, waiting for transfers between devices: 67.3 us -> 64.8 us  [swap(): return lax.ppermute(value, ('dp', 'tensor'), pairs)]
    pallas_call x0 -> x1, Pallas kernels: none -> 2.36 us  [pack_near(): pl.pallas_call(near_kernel, in_specs=[pl.BlockSpec(memory_space=pltpu.SME...]
    unnamed x82 -> x78, local copies, waits for them, and re-layouts: 4.93 us -> 5.55 us
  transfers between devices with their start and end apart: 44 -> 44, of which waited for: 16 -> 17; matrix products, arithmetic and copies ran while one was open for 3% -> 3% of each run, Pallas kernels for 36% -> 37%
where the time goes in v1:
time: 213 us
  Pallas kernels  89.5 us (42%)
  waiting for transfers between devices  64.8 us (30%)
  starting transfers between devices  43.6 us (20%)
  local copies, waits for them, and re-layouts  8.04 us (4%)
  other arithmetic  4.64 us (2%)
    pallas_call x34, Pallas kernels, run(): pl.pallas_call(kernel, in_specs=specs, out_specs=[pl.BlockSpec(memory_spa...  76.9 us
    ppermute x44, waiting for transfers between devices, swap(): return lax.ppermute(value, ('dp', 'tensor'), pairs)  64.8 us
    ppermute x44, starting transfers between devices, swap(): return lax.ppermute(value, ('dp', 'tensor'), pairs)  43.6 us
    pallas_call x3, Pallas kernels, finish(): pl.pallas_call(functools.partial(finish_kernel, sizes), grid_spec=pltpu.P...  6.9 us
    unnamed x78, local copies, waits for them, and re-layouts  5.55 us
  transfers between devices with their start and end apart: 44, of which 17 were waited for; matrix products, arithmetic and copies ran while one was open for 3% of the time, Pallas kernels for 37%

profile of v1, /device:TPU:0, one launch (start us, length us, event | category | flops | bytes accessed | tf_op | source)
XLA Modules:
  0.0 212.5 jit_solution(10588764577512982087)
XLA Ops:
  1.6 2.4 %pack_near.1.near = bf16[208,768]{1,0:T(8,128)(2,1)} custom-call(s32[34]{0:T(128)} %broadcast_select_fusion.plan, bf16[192,768]{1,0:T(8,128)(2,1)} %bitcast.59, bf16[192,768]{1,0:T(8,128)(2,1)} %bitcast.61, bf16[192,768]{1,0:T(8,128)(2,1)} %bitcast.63, bf16[192,768]{1,0:T(8,128)(2,1)} %wo.3, bf16[192]{0:T(256)(128)(2,1)} %bq.1, bf16[192]{0:T(256)(128)(2,1)} %bv.1, ...), custom_call_target="tpu_custom_call" | custom-call | tf_op jit(solution)/shard_map/pack_near/pallas_call | solution.py:86
  4.0 3.0 %collective-permute-start = (bf16[208,768]{1,0:T(8,128)(2,1)}, bf16[208,768]{1,0:T(8,128)(2,1)S(1)}, u32[]{:S(2)}, u32[]{:S(2)}) collective-permute-start(bf16[208,768]{1,0:T(8,128)(2,1)} %pack_near.1.near), channel_id=1, source_target_pairs={{0,2},{1,3},{2,0},{3,1},{4,6},{5,7},{6,4},{7,5},{8,10},{9,11},{10,... | collective-permute-start | bytes 958472 | tf_op jit(solution)/shard_map/ppermute | solution.py:690
  7.0 3.3 %pack_weights.1 = (bf16[784,768]{1,0:T(8,128)(2,1)}, bf16[384,768]{1,0:T(8,128)(2,1)}, bf16[384,768]{1,0:T(8,128)(2,1)}, f32[8,768]{1,0:T(8,128)}) custom-call(s32[34]{0:T(128)} %broadcast_select_fusion.plan, bf16[192,768]{1,0:T(8,128)(2,1)} %bitcast.60, bf16[192,768]{1,0:T(8,128)(2,1)} %bitcast.62, bf16[192,768]{1,0:T(8,128)(2,1)} %bitcast.64, ...), custom_call_target="tpu_custom_call" | custom-call | tf_op jit(solution)/shard_map/pack_weights/pallas_call | solution.py:155
  10.7 4.9 %collective-permute-done = bf16[208,768]{1,0:T(8,128)(2,1)S(1)} collective-permute-done((bf16[208,768]{1,0:T(8,128)(2,1)}, bf16[208,768]{1,0:T(8,128)(2,1)S(1)}, u32[]{:S(2)}, u32[]{:S(2)}) %collective-permute-start) | collective-permute-done | bytes 319520 | tf_op jit(solution)/shard_map/ppermute | solution.py:690
  15.6 2.1 collective-permute-start.1
  17.7 1.3 copy-done.12
  19.0 4.2 %attention.3 = (bf16[576,512]{1,0:T(8,128)(2,1)S(1)}, bf16[3,512,512]{2,1,0:T(8,128)(2,1)S(1)}, bf16[192,512]{1,0:T(8,128)(2,1)S(1)}, f32[1,768]{1,0:T(1,128)S(1)}, f32[512,768]{1,0:T(8,128)S(1)}) custom-call(bf16[512,768]{1,0:T(8,128)(2,1)S(1)} %copy-done.23, bf16[784,768]{1,0:T(8,128)(2,1)S(1)} %copy-done.12), custom_call_target="tpu_custom_call" | custom-call | flops 49999998976 | bytes 80000000 | tf_op jit(solution)/shard_map/attention/pallas_call | solution.py:48
  23.2 1.1 copy-done.26
  24.4 1.5 collective-permute-start.6
  26.0 1.6 collective-permute-start.2
  27.6 4.2 %attention.4 = (bf16[576,512]{1,0:T(8,128)(2,1)S(1)}, bf16[3,512,512]{2,1,0:T(8,128)(2,1)S(1)}, bf16[192,512]{1,0:T(8,128)(2,1)S(1)}, f32[1,768]{1,0:T(1,128)S(1)}, f32[512,768]{1,0:T(8,128)S(1)}) custom-call(bf16[512,768]{1,0:T(8,128)(2,1)S(1)} %copy-done.23, bf16[784,768]{1,0:T(8,128)(2,1)S(1)} %collective-permute-done.3.refs_1_.weights, ...), custom_call_target="tpu_custom_call" | custom-call | flops 49999998976 | bytes 80000000 | tf_op jit(solution)/shard_map/attention/pallas_call | solution.py:48
  31.9 4.0 %collective-permute-done.2 = bf16[384,768]{1,0:T(8,128)(2,1)S(1)} collective-permute-done((bf16[384,768]{1,0:T(8,128)(2,1)S(1)}, bf16[384,768]{1,0:T(8,128)(2,1)S(1)}, u32[]{:S(2)}, u32[]{:S(2)}) %collective-permute-start.2) | collective-permute-done | bytes 589856 | tf_op jit(solution)/shard_map/ppermute | solution.py:690
  37.5 1.6 collective-permute-start.8
  39.0 3.8 %attention.5 = (bf16[576,512]{1,0:T(8,128)(2,1)S(1)}, bf16[3,512,512]{2,1,0:T(8,128)(2,1)S(1)}, bf16[192,512]{1,0:T(8,128)(2,1)S(1)}, f32[1,768]{1,0:T(1,128)S(1)}, f32[512,768]{1,0:T(8,128)S(1)}) custom-call(bf16[512,768]{1,0:T(8,128)(2,1)S(1)} %copy-done.23, bf16[784,768]{1,0:T(8,128)(2,1)S(1)} %join.3.refs_1_.weights, ...), custom_call_target="tpu_custom_call" | custom-call | flops 49999998976 | bytes 80000000 | tf_op jit(solution)/shard_map/attention/pallas_call | solution.py:48
  43.7 1.5 collective-permute-start.10
  45.7 4.8 %attention_last.1 = (bf16[576,512]{1,0:T(8,128)(2,1)S(1)}, bf16[3,512,512]{2,1,0:T(8,128)(2,1)S(1)}, bf16[192,512]{1,0:T(8,128)(2,1)S(1)}, f32[1,768]{1,0:T(1,12...) custom-call(bf16[512,768]{1,0:T(8,128)(2,1)S(1)} %copy-done.23, ...), custom_call_target="tpu_custom_call" | custom-call | flops 49999998976 | bytes 80000000 | tf_op jit(solution)/shard_map/attention_last/pallas_call | solution.py:48
  52.0 1.8 feed.3
  53.8 1.8 feed.4
  56.9 1.8 feed.5
  59.4 3.6 %feed_last.1 = (bf16[512,768]{1,0:T(8,128)(2,1)S(1)}, bf16[512,768]{1,0:T(8,128)(2,1)S(1)}, f32[512,768]{1,0:T(8,128)S(1)}, bf16[512,768]{1,0:T(8,128)(2,1)S(1)}...) custom-call(bf16[512,768]{1,0:T(8,128)(2,1)S(1)} %get-tuple-element.199.refs_0_.refs_2_, ...), custom_call_target="tpu_custom_call" | custom-call | flops 49999998976 | bytes 80000000 | tf_op jit(solution)/shard_map/feed_last/pallas_call | solution.py:48
  63.0 1.4 down_grad.2
  64.9 1.4 down_grad.3
  66.5 2.7 %feed_back.3 = (bf16[768,768]{1,0:T(8,128)(2,1)S(1)}, f32[1,768]{1,0:T(1,128)S(1)}, f32[512,768]{1,0:T(8,128)S(1)}) custom-call(bf16[512,768]{1,0:T(8,128)(2,1)S(1)} %get-tuple-element.224.refs_0_, bf16[512,768]{1,0:T(8,128)(2,1)S(1)} %get-tuple-element.231.refs_2_.refs_1_, bf16[512,768]{1,0:T(8,128)(2,1)S(1)} %get-tuple-element.199.refs_0_.refs_2_, ...), custom_call_target="tpu_custom_call" | custom-call | flops 40000000000 | bytes 100000000 | tf_op jit(solution)/shard_map/feed_back/pallas_call | solution.py:48
  69.6 1.4 first_stage.3
  71.6 2.7 %feed_back.4 = (bf16[768,768]{1,0:T(8,128)(2,1)S(1)}, f32[1,768]{1,0:T(1,128)S(1)}, f32[512,768]{1,0:T(8,128)S(1)}) custom-call(bf16[512,768]{1,0:T(8,128)(2,1)S(1)} %get-tuple-element.223.refs_0_, bf16[512,768]{1,0:T(8,128)(2,1)S(1)} %get-tuple-element.231.refs_2_.refs_1_, bf16[512,768]{1,0:T(8,128)(2,1)S(1)} %get-tuple-element.199.refs_0_.refs_2_, ...), custom_call_target="tpu_custom_call" | custom-call | flops 40000000000 | bytes 100000000 | tf_op jit(solution)/shard_map/feed_back/pallas_call | solution.py:48
  75.4 2.7 %feed_back.5 = (bf16[768,768]{1,0:T(8,128)(2,1)S(1)}, f32[1,768]{1,0:T(1,128)S(1)}, f32[512,768]{1,0:T(8,128)S(1)}) custom-call(bf16[512,768]{1,0:T(8,128)(2,1)S(1)} %get-tuple-element.222.refs_0_, bf16[512,768]{1,0:T(8,128)(2,1)S(1)} %get-tuple-element.231.refs_2_.refs_1_, bf16[512,768]{1,0:T(8,128)(2,1)S(1)} %get-tuple-element.199.refs_0_.refs_2_, ...), custom_call_target="tpu_custom_call" | custom-call | flops 40000000000 | bytes 100000000 | tf_op jit(solution)/shard_map/feed_back/pallas_call | solution.py:48
  78.2 3.7 %feed_back_last.1 = (bf16[768,768]{1,0:T(8,128)(2,1)S(1)}, f32[1,768]{1,0:T(1,128)S(1)}, f32[512,768]{1,0:T(8,128)S(1)}, bf16[512,768]{1,0:T(8,128)(2,1)S(1)}, f32[8,768]{1,0:T(8,128)S(1)}) custom-call(bf16[512,768]{1,0:T(8,128)(2,1)S(1)} %get-tuple-element.220.refs_0_, bf16[512,768]{1,0:T(8,128)(2,1)S(1)} %get-tuple-element.231.refs_2_.refs_1_, ...), custom_call_target="tpu_custom_call" | custom-call | flops 49999998976 | bytes 100000000 | tf_op jit(solution)/shard_map/feed_back_last/pallas_call | solution.py:48
  83.2 4.1 %collective-permute-done.18.got = bf16[768,768]{1,0:T(8,128)(2,1)S(1)} collective-permute-done((bf16[768,768]{1,0:T(8,128)(2,1)S(1)}, bf16[768,768]{1,0:T(8,128)(2,1)S(1)}, u32[]{:S(2)}, u32[]{:S(2)}) %collective-permute-start.18) | collective-permute-done | bytes 1179680 | tf_op jit(solution)/shard_map/ppermute | solution.py:690
  88.9 5.4 %attention_back.4 = (bf16[576,768]{1,0:T(8,128)(2,1)S(1)}, f32[8,576]{1,0:T(8,128)S(1)}, f32[512,768]{1,0:T(8,128)S(1)}) custom-call(bf16[576,512]{1,0:T(8,128)(2,1)S(1)} %get-tuple-element.247.qkv, bf16[3,512,512]{2,1,0:T(8,128)(2,1)S(1)} %get-tuple-element.248.probs, bf16[512,768]{1,0:T(8,128)(2,1)S(1)} %get-tuple-element.246.low.first_low, ...), custom_call_target="tpu_custom_call" | custom-call | flops 70000001024 | bytes 120000000 | tf_op jit(solution)/shard_map/attention_back/pallas_call | solution.py:48
  94.4 1.6 first_stage.4
  96.5 1.7 collective-permute-done.19.got
  99.2 1.6 collective-permute-start.24
  100.9 5.4 %attention_back.5 = (bf16[576,768]{1,0:T(8,128)(2,1)S(1)}, f32[8,576]{1,0:T(8,128)S(1)}, f32[512,768]{1,0:T(8,128)S(1)}) custom-call(bf16[576,512]{1,0:T(8,128)(2,1)S(1)} %copy-done.31, bf16[3,512,512]{2,1,0:T(8,128)(2,1)S(1)} %get-tuple-element.219.probs, bf16[512,768]{1,0:T(8,128)(2,1)S(1)} %get-tuple-element.246.low.first_low, ...), custom_call_target="tpu_custom_call" | custom-call | flops 70000001024 | bytes 120000000 | tf_op jit(solution)/shard_map/attention_back/pallas_call | solution.py:48
  106.3 5.4 %attention_back.6 = (bf16[576,768]{1,0:T(8,128)(2,1)S(1)}, f32[8,576]{1,0:T(8,128)S(1)}, f32[512,768]{1,0:T(8,128)S(1)}) custom-call(bf16[576,512]{1,0:T(8,128)(2,1)S(1)} %copy-done.29, bf16[3,512,512]{2,1,0:T(8,128)(2,1)S(1)} %get-tuple-element.275.probs, bf16[512,768]{1,0:T(8,128)(2,1)S(1)} %get-tuple-element.246.low.first_low, ...), custom_call_target="tpu_custom_call" | custom-call | flops 70000001024 | bytes 120000000 | tf_op jit(solution)/shard_map/attention_back/pallas_call | solution.py:48
  112.7 2.4 %collective-permute-start.26 = (bf16[96,768]{1,0:T(8,128)(2,1)S(1)}, bf16[96,768]{1,0:T(8,128)(2,1)S(1)}, u32[]{:S(2)}, u32[]{:S(2)}) collective-permute-start(bf16[96,768]{1,0:T(8,128)(2,1)S(1)} %get-tuple-element.283), channel_id=1, source_target_pairs={{0,16},{1,9},{2,18},{3,11},{4,20},{5,13},{6,22},{7,15},{8,24},{9,1... | collective-permute-start | bytes 442376 | tf_op jit(solution)/shard_map/ppermute | solution.py:690
  115.4 1.1 next_stage.12
  116.5 1.6 collective-permute-start.27
  118.1 5.4 %attention_back.7 = (bf16[576,768]{1,0:T(8,128)(2,1)S(1)}, f32[8,576]{1,0:T(8,128)S(1)}, f32[512,768]{1,0:T(8,128)S(1)}) custom-call(bf16[576,512]{1,0:T(8,128)(2,1)S(1)} %copy-done.33, bf16[3,512,512]{2,1,0:T(8,128)(2,1)S(1)} %copy-done.27, bf16[512,768]{1,0:T(8,128)(2,1)S(1)} %get-tuple-element.246.low.first_low, bf16[512,768]{1,0:T(8,128)(2,1)S(1)} %copy-done.23, ...), custom_call_target="tpu_custom_call" | custom-call | flops 70000001024 | bytes 120000000 | tf_op jit(solution)/shard_map/attention_back/pallas_call | solution.py:48
  123.5 4.5 %collective-permute-done.27.got = bf16[480,768]{1,0:T(8,128)(2,1)S(1)} collective-permute-done((bf16[480,768]{1,0:T(8,128)(2,1)S(1)}, bf16[480,768]{1,0:T(8,128)(2,1)S(1)}, u32[]{:S(2)}, u32[]{:S(2)}) %collective-permute-start.27) | collective-permute-done | bytes 737312 | tf_op jit(solution)/shard_map/ppermute | solution.py:690
  128.0 1.2 first_stage.5
  129.8 2.6 %collective-permute-start.29 = (bf16[96,768]{1,0:T(8,128)(2,1)S(1)}, bf16[96,768]{1,0:T(8,128)(2,1)S(1)}, u32[]{:S(2)}, u32[]{:S(2)}) collective-permute-start(bf16[96,768]{1,0:T(8,128)(2,1)S(1)} %add_convert_fusion.1), channel_id=1, source_target_pairs={{0,16},{1,9},{2,18},{3,11},{4,20},{5,13},{6,22},{7,15},{8,24},{9,1... | collective-permute-start | bytes 442376 | tf_op jit(solution)/shard_map/ppermute | solution.py:690
  133.4 1.6 collective-permute-start.32
  135.0 5.8 %collective-permute-done.29 = bf16[96,768]{1,0:T(8,128)(2,1)S(1)} collective-permute-done((bf16[96,768]{1,0:T(8,128)(2,1)S(1)}, bf16[96,768]{1,0:T(8,128)(2,1)S(1)}, u32[]{:S(2)}, u32[]{:S(2)}) %collective-permute-start.29) | collective-permute-done | bytes 147488 | tf_op jit(solution)/shard_map/ppermute | solution.py:690
  140.8 2.1 %collective-permute-done.28.got = bf16[608,768]{1,0:T(8,128)(2,1)S(1)} collective-permute-done((bf16[608,768]{1,0:T(8,128)(2,1)S(1)}, bf16[608,768]{1,0:T(8,128)(2,1)S(1)}, u32[]{:S(2)}, u32[]{:S(2)}) %collective-permute-start.28) | collective-permute-done | bytes 933920 | tf_op jit(solution)/shard_map/ppermute | solution.py:690
  143.8 1.8 collective-permute-start.30
  145.6 1.4 collective-permute-start.31
  147.7 2.7 %collective-permute-start.34 = (bf16[120,768]{1,0:T(8,128)(2,1)S(1)}, bf16[120,768]{1,0:T(8,128)(2,1)S(1)}, u32[]{:S(2)}, u32[]{:S(2)}) collective-permute-start(bf16[120,768]{1,0:T(8,128)(2,1)S(1)} %get-tuple-element.314), channel_id=1, source_target_pairs={{0,16},{1,9},{2,18},{3,11},{4,20},{5,13},{6,22},{7,15},{8,24},{9,1... | collective-permute-start | bytes 552968 | tf_op jit(solution)/shard_map/ppermute | solution.py:690
  150.3 10.0 %collective-permute-done.31 = bf16[192,768]{1,0:T(8,128)(2,1)S(1)} collective-permute-done((bf16[192,768]{1,0:T(8,128)(2,1)S(1)}, bf16[192,768]{1,0:T(8,128)(2,1)S(1)}, u32[]{:S(2)}, u32[]{:S(2)}) %collective-permute-start.31) | collective-permute-done | bytes 294944 | tf_op jit(solution)/shard_map/ppermute | solution.py:690
  161.7 2.5 %collective-permute-start.37 = (bf16[120,768]{1,0:T(8,128)(2,1)S(1)}, bf16[120,768]{1,0:T(8,128)(2,1)S(1)}, u32[]{:S(2)}, u32[]{:S(2)}) collective-permute-start(bf16[120,768]{1,0:T(8,128)(2,1)S(1)} %add_convert_fusion), channel_id=1, source_target_pairs={{0,16},{1,9},{2,18},{3,11},{4,20},{5,13},{6,22},{7,15},{8,24},{9,1... | collective-permute-start | bytes 552968 | tf_op jit(solution)/shard_map/ppermute | solution.py:690
  164.1 9.1 %collective-permute-done.33.got = bf16[176,768]{1,0:T(8,128)(2,1)S(1)} collective-permute-done((bf16[176,768]{1,0:T(8,128)(2,1)S(1)}, bf16[176,768]{1,0:T(8,128)(2,1)S(1)}, u32[]{:S(2)}, u32[]{:S(2)}) %collective-permute-start.33) | collective-permute-done | bytes 270368 | tf_op jit(solution)/shard_map/ppermute | solution.py:690
  174.0 1.7 collective-permute-start.39
  175.8 2.0 finish.3
  177.7 3.9 %collective-permute-done.35 = bf16[104,768]{1,0:T(8,128)(2,1)S(1)} collective-permute-done((bf16[104,768]{1,0:T(8,128)(2,1)S(1)}, bf16[104,768]{1,0:T(8,128)(2,1)S(1)}, u32[]{:S(2)}, u32[]{:S(2)}) %collective-permute-start.35) | collective-permute-done | bytes 159776 | tf_op jit(solution)/shard_map/ppermute | solution.py:690
  181.7 3.2 %collective-permute-done.39 = bf16[240,768]{1,0:T(8,128)(2,1)S(1)} collective-permute-done((bf16[240,768]{1,0:T(8,128)(2,1)S(1)}, bf16[240,768]{1,0:T(8,128)(2,1)S(1)}, u32[]{:S(2)}, u32[]{:S(2)}) %collective-permute-start.39) | collective-permute-done | bytes 368672 | tf_op jit(solution)/shard_map/ppermute | solution.py:690
  185.0 3.4 %collective-permute-start.43 = (bf16[480,768]{1,0:T(8,128)(2,1)S(1)}, bf16[480,768]{1,0:T(8,128)(2,1)S(1)}, u32[]{:S(2)}, u32[]{:S(2)}) collective-permute-start(bf16[480,768]{1,0:T(8,128)(2,1)S(1)} %pad_maximum_fusion.mine), channel_id=1, source_target_pairs={{0,4},{1,5},{2,6},{3,7},{4,0},{5,1},{6,2},{7,3},{8,12},{9,13},{10,... | collective-permute-start | bytes 2211848 | tf_op jit(solution)/shard_map/ppermute | solution.py:690
  188.4 3.5 %collective-permute-done.38 = bf16[72,768]{1,0:T(8,128)(2,1)S(1)} collective-permute-done((bf16[72,768]{1,0:T(8,128)(2,1)S(1)}, bf16[72,768]{1,0:T(8,128)(2,1)S(1)}, u32[]{:S(2)}, u32[]{:S(2)}) %collective-permute-start.38) | collective-permute-done | bytes 110624 | tf_op jit(solution)/shard_map/ppermute | solution.py:690
  192.6 1.4 collective-permute-done.41
  195.4 2.5 %collective-permute-done.40 = bf16[144,768]{1,0:T(8,128)(2,1)S(1)} collective-permute-done((bf16[144,768]{1,0:T(8,128)(2,1)S(1)}, bf16[144,768]{1,0:T(8,128)(2,1)S(1)}, u32[]{:S(2)}, u32[]{:S(2)}) %collective-permute-start.40) | collective-permute-done | bytes 221216 | tf_op jit(solution)/shard_map/ppermute | solution.py:690
  198.6 1.1 pad_maximum_fusion.3.mine
  199.7 1.3 collective-permute-start.42
  201.0 1.5 fusion.3
  204.4 2.2 %finish.4 = (f32[768,768]{1,0:T(8,128)}, f32[192,768]{1,0:T(8,128)}) custom-call(s32[34]{0:T(128)S(1)} %copy-done.11, bf16[480,768]{1,0:T(8,128)(2,1)S(1)} %pad_maximum_fusion.mine, bf16[480,768]{1,0:T(8,128)(2,1)S(1)} %collective-permute-done.43.theirs), custom_call_target="tpu_custom_call" | custom-call | flops 1000 | bytes 1000 | tf_op jit(solution)/shard_map/finish/pallas_call | solution.py:659
  206.6 3.0 %collective-permute-done.42.theirs = bf16[288,768]{1,0:T(8,128)(2,1)} collective-permute-done((bf16[288,768]{1,0:T(8,128)(2,1)S(1)}, bf16[288,768]{1,0:T(8,128)(2,1)}, u32[]{:S(2)}, u32[]{:S(2)}) %collective-permute-start.42) | collective-permute-done | bytes 442400 | tf_op jit(solution)/shard_map/ppermute | solution.py:690
  209.6 2.8 %finish.5 = (f32[192,768]{1,0:T(8,128)}, f32[192,768]{1,0:T(8,128)}, f32[192,768]{1,0:T(8,128)}) custom-call(s32[34]{0:T(128)S(1)} %copy-done.11, bf16[288,768]{1,0:T(8,128)(2,1)S(1)} %pad_maximum_fusion.3.mine, bf16[288,768]{1,0:T(8,128)(2,1)} %collective-permute-done.42.theirs), custom_call_target="tpu_custom_call" | custom-call | flops 1000 | bytes 1000 | tf_op jit(solution)/shard_map/finish/pallas_call | solution.py:659
  (165 shorter events, 25.9 us)
Async XLA Ops:
  4.0 13.7 %copy-start.23 = (bf16[512,768]{1,0:T(8,128)(2,1)S(1)}, bf16[512,768]{1,0:T(8,128)(2,1)}, u32[]{:S(2)}) copy-start(bf16[512,768]{1,0:T(8,128)(2,1)} %tok.7) | copy-start | bytes 2359300
  4.0 11.6 %collective-permute-start = (bf16[208,768]{1,0:T(8,128)(2,1)}, bf16[208,768]{1,0:T(8,128)(2,1)S(1)}, u32[]{:S(2)}, u32[]{:S(2)}) collective-permute-start(bf16[208,768]{1,0:T(8,128)(2,1)} %pack_near.1.near), channel_id=1, source_target_pairs={{0,2},{1,3},{2,0},{3,1},{4,6},{5,7},{6,4},{7,5},{8,10},{9,11},{10,... | collective-permute-start | bytes 958472 | tf_op jit(solution)/shard_map/ppermute | solution.py:690
  10.3 17.3 %collective-permute-start.3 = (bf16[784,768]{1,0:T(8,128)(2,1)}, bf16[784,768]{1,0:T(8,128)(2,1)S(1)}, u32[]{:S(2)}, u32[]{:S(2)}) collective-permute-start(bf16[784,768]{1,0:T(8,128)(2,1)} %get-tuple-element.185.refs_1_.weights), channel_id=1, source_target_pairs={{0,1},{1,0},{2,3},{3,2},{4,5},{5,4},{6,7},{7,6},{8,9},{9,8},{10,11... | collective-permute-start | bytes 3612680 | tf_op jit(solution)/shard_map/ppermute | solution.py:690
  10.4 26.4 %collective-permute-start.5 = (bf16[384,768]{1,0:T(8,128)(2,1)}, bf16[384,768]{1,0:T(8,128)(2,1)S(1)}, u32[]{:S(2)}, u32[]{:S(2)}) collective-permute-start(bf16[384,768]{1,0:T(8,128)(2,1)} %get-tuple-element.190), channel_id=1, source_target_pairs={{0,2},{1,3},{2,0},{3,1},{4,6},{5,7},{6,4},{7,5},{8,10},{9,11},{10,... | collective-permute-start | bytes 1769480 | tf_op jit(solution)/shard_map/ppermute | solution.py:690
  15.6 10.3 %collective-permute-start.1 = (bf16[192,768]{1,0:T(8,128)(2,1)S(1)}, bf16[192,768]{1,0:T(8,128)(2,1)S(1)}, u32[]{:S(2)}, u32[]{:S(2)}) collective-permute-start(bf16[192,768]{1,0:T(8,128)(2,1)S(1)} %slice.84.refs_0_), channel_id=1, source_target_pairs={{0,4},{1,9},{2,6},{3,11},{4,0},{5,13},{6,2},{7,15},{8,12},{9,1},{1... | collective-permute-start | bytes 884744 | tf_op jit(solution)/shard_map/ppermute | solution.py:690
  19.0 5.4 %copy-start.38 = (bf16[384,768]{1,0:T(8,128)(2,1)S(1)}, bf16[384,768]{1,0:T(8,128)(2,1)}, u32[]{:S(2)}) copy-start(bf16[384,768]{1,0:T(8,128)(2,1)} %get-tuple-element.195) | copy-start | bytes 1769476
  24.4 3.2 %copy-start.32 = (bf16[576,512]{1,0:T(8,128)(2,1)}, bf16[576,512]{1,0:T(8,128)(2,1)S(1)}, u32[]{:S(2)}) copy-start(bf16[576,512]{1,0:T(8,128)(2,1)S(1)} %get-tuple-element.272.qkv) | copy-start | bytes 1769476
  24.4 18.5 %collective-permute-start.6 = (bf16[384,768]{1,0:T(8,128)(2,1)S(1)}, bf16[384,768]{1,0:T(8,128)(2,1)S(1)}, u32[]{:S(2)}, u32[]{:S(2)}) collective-permute-start(bf16[384,768]{1,0:T(8,128)(2,1)S(1)} %copy-done.38), channel_id=1, source_target_pairs={{0,2},{1,3},{2,0},{3,1},{4,6},{5,7},{6,4},{7,5},{8,10},{9,11},{10,... | collective-permute-start | bytes 1769480 | tf_op jit(solution)/shard_map/ppermute | solution.py:690
  25.9 10.0 %copy-start.10 = (s32[34]{0:T(128)S(1)}, s32[34]{0:T(128)}, u32[]{:S(2)}) copy-start(s32[34]{0:T(128)} %broadcast_select_fusion.plan) | copy-start | bytes 412
  26.0 9.9 %collective-permute-start.2 = (bf16[384,768]{1,0:T(8,128)(2,1)S(1)}, bf16[384,768]{1,0:T(8,128)(2,1)S(1)}, u32[]{:S(2)}, u32[]{:S(2)}) collective-permute-start(bf16[384,768]{1,0:T(8,128)(2,1)S(1)} %pad_maximum_fusion.1), channel_id=1, source_target_pairs={{0,8},{1,5},{2,10},{3,7},{4,12},{5,1},{6,14},{7,3},{8,0},{9,13},{1... | collective-permute-start | bytes 1769480 | tf_op jit(solution)/shard_map/ppermute | solution.py:690
  27.6 4.2 %copy-start.14 = (bf16[784,768]{1,0:T(8,128)(2,1)}, bf16[784,768]{1,0:T(8,128)(2,1)S(1)}, u32[]{:S(2)}) copy-start(bf16[784,768]{1,0:T(8,128)(2,1)S(1)} %collective-permute-done.3.refs_1_.weights) | copy-start | bytes 3612676
  31.9 4.8 %copy-start.28 = (bf16[576,512]{1,0:T(8,128)(2,1)}, bf16[576,512]{1,0:T(8,128)(2,1)S(1)}, u32[]{:S(2)}) copy-start(bf16[576,512]{1,0:T(8,128)(2,1)S(1)} %get-tuple-element.274.qkv) | copy-start | bytes 1769476
  36.7 6.2 %copy-start.2 = (bf16[784,768]{1,0:T(8,128)(2,1)}, bf16[784,768]{1,0:T(8,128)(2,1)S(1)}, u32[]{:S(2)}) copy-start(bf16[784,768]{1,0:T(8,128)(2,1)S(1)} %join.3.refs_1_.weights) | copy-start | bytes 3612676
  36.7 8.9 %collective-permute-start.4 = (bf16[784,768]{1,0:T(8,128)(2,1)S(1)}, bf16[784,768]{1,0:T(8,128)(2,1)S(1)}, u32[]{:S(2)}, u32[]{:S(2)}) collective-permute-start(bf16[784,768]{1,0:T(8,128)(2,1)S(1)} %join.3.refs_1_.weights), channel_id=1, source_target_pairs={{0,1},{1,0},{2,3},{3,2},{4,5},{5,4},{6,7},{7,6},{8,9},{9,8},{10,11... | collective-permute-start | bytes 3612680 | tf_op jit(solution)/shard_map/ppermute | solution.py:690
  36.8 8.8 %copy-start.4 = (bf16[768,768]{1,0:T(8,128)(2,1)S(1)}, bf16[768,768]{1,0:T(8,128)(2,1)}, u32[]{:S(2)}) copy-start(bf16[768,768]{1,0:T(8,128)(2,1)} %refs_4_.3) | copy-start | bytes 3538948
  36.8 8.9 %copy-start.24 = (f32[8,768]{1,0:T(8,128)S(1)}, f32[8,768]{1,0:T(8,128)}, u32[]{:S(2)}) copy-start(f32[8,768]{1,0:T(8,128)} %get-tuple-element.198.refs_3_.refs_5_.refs_8_) | copy-start | bytes 73732
  36.9 13.7 %collective-permute-start.7 = (bf16[192,768]{1,0:T(8,128)(2,1)S(1)}, bf16[192,768]{1,0:T(8,128)(2,1)S(1)}, u32[]{:S(2)}, u32[]{:S(2)}) collective-permute-start(bf16[192,768]{1,0:T(8,128)(2,1)S(1)} %get-tuple-element.353.refs_0_), channel_id=1, source_target_pairs={{0,4},{1,5},{2,6},{3,7},{4,0},{5,1},{6,2},{7,3},{8,12},{9,13},{10,... | collective-permute-start | bytes 884744 | tf_op jit(solution)/shard_map/ppermute | solution.py:690
  37.5 13.7 %collective-permute-start.8 = (bf16[192,768]{1,0:T(8,128)(2,1)S(1)}, bf16[192,768]{1,0:T(8,128)(2,1)S(1)}, u32[]{:S(2)}, u32[]{:S(2)}) collective-permute-start(bf16[192,768]{1,0:T(8,128)(2,1)S(1)} %get-tuple-element.353.refs_0_), channel_id=1, source_target_pairs={{0,8},{1,9},{2,10},{3,11},{4,12},{5,13},{6,14},{7,15},{8,0},{9,1},... | collective-permute-start | bytes 884744 | tf_op jit(solution)/shard_map/ppermute | solution.py:690
  43.7 12.0 %collective-permute-start.10 = (bf16[192,768]{1,0:T(8,128)(2,1)S(1)}, bf16[192,768]{1,0:T(8,128)(2,1)S(1)}, u32[]{:S(2)}, u32[]{:S(2)}) collective-permute-start(bf16[192,768]{1,0:T(8,128)(2,1)S(1)} %get-tuple-element.351.refs_0_), channel_id=1, source_target_pairs={{0,4},{1,5},{2,6},{3,7},{4,0},{5,1},{6,2},{7,3},{8,12},{9,13},{10,... | collective-permute-start | bytes 884744 | tf_op jit(solution)/shard_map/ppermute | solution.py:690
  45.2 10.5 %collective-permute-start.11 = (bf16[192,768]{1,0:T(8,128)(2,1)S(1)}, bf16[192,768]{1,0:T(8,128)(2,1)S(1)}, u32[]{:S(2)}, u32[]{:S(2)}) collective-permute-start(bf16[192,768]{1,0:T(8,128)(2,1)S(1)} %get-tuple-element.351.refs_0_), channel_id=1, source_target_pairs={{0,8},{1,9},{2,10},{3,11},{4,12},{5,13},{6,14},{7,15},{8,0},{9,1},... | collective-permute-start | bytes 884744 | tf_op jit(solution)/shard_map/ppermute | solution.py:690
  45.6 4.9 %copy-start.16 = (bf16[784,768]{1,0:T(8,128)(2,1)}, bf16[784,768]{1,0:T(8,128)(2,1)S(1)}, u32[]{:S(2)}) copy-start(bf16[784,768]{1,0:T(8,128)(2,1)S(1)} %collective-permute-done.4.refs_1_.weights) | copy-start | bytes 3612676
  45.6 8.1 %collective-permute-start.12 = (bf16[768,768]{1,0:T(8,128)(2,1)S(1)}, bf16[768,768]{1,0:T(8,128)(2,1)S(1)}, u32[]{:S(2)}, u32[]{:S(2)}) collective-permute-start(bf16[768,768]{1,0:T(8,128)(2,1)S(1)} %copy-done.4), channel_id=1, source_target_pairs={{0,1},{1,0},{2,3},{3,2},{4,5},{5,4},{6,7},{7,6},{8,9},{9,8},{10,11... | collective-permute-start | bytes 3538952 | tf_op jit(solution)/shard_map/ppermute | solution.py:690
  45.7 4.9 %copy-start.6 = (bf16[768,768]{1,0:T(8,128)(2,1)S(1)}, bf16[768,768]{1,0:T(8,128)(2,1)}, u32[]{:S(2)}) copy-start(bf16[768,768]{1,0:T(8,128)(2,1)} %refs_5_.3) | copy-start | bytes 3538948
  50.6 3.2 %collective-permute-start.13 = (bf16[768,768]{1,0:T(8,128)(2,1)S(1)}, bf16[768,768]{1,0:T(8,128)(2,1)S(1)}, u32[]{:S(2)}, u32[]{:S(2)}) collective-permute-start(bf16[768,768]{1,0:T(8,128)(2,1)S(1)} %copy-done.6), channel_id=1, source_target_pairs={{0,1},{1,0},{2,3},{3,2},{4,5},{5,4},{6,7},{7,6},{8,9},{9,8},{10,11... | collective-permute-start | bytes 3538952 | tf_op jit(solution)/shard_map/ppermute | solution.py:690
  51.9 6.9 %collective-permute-start.9 = (bf16[768,768]{1,0:T(8,128)(2,1)S(1)}, bf16[768,768]{1,0:T(8,128)(2,1)S(1)}, u32[]{:S(2)}, u32[]{:S(2)}) collective-permute-start(bf16[768,768]{1,0:T(8,128)(2,1)S(1)} %join.4.refs_1_.refs_4_), channel_id=1, source_target_pairs={{0,1},{1,0},{2,3},{3,2},{4,5},{5,4},{6,7},{7,6},{8,9},{9,8},{10,11... | collective-permute-start | bytes 3538952 | tf_op jit(solution)/shard_map/ppermute | solution.py:690
  56.4 3.0 %collective-permute-start.14 = (bf16[768,768]{1,0:T(8,128)(2,1)S(1)}, bf16[768,768]{1,0:T(8,128)(2,1)S(1)}, u32[]{:S(2)}, u32[]{:S(2)}) collective-permute-start(bf16[768,768]{1,0:T(8,128)(2,1)S(1)} %join.5.refs_2_.refs_5_), channel_id=1, source_target_pairs={{0,1},{1,0},{2,3},{3,2},{4,5},{5,4},{6,7},{7,6},{8,9},{9,8},{10,11... | collective-permute-start | bytes 3538952 | tf_op jit(solution)/shard_map/ppermute | solution.py:690
  64.4 5.2 %collective-permute-start.15 = (bf16[768,768]{1,0:T(8,128)(2,1)S(1)}, bf16[768,768]{1,0:T(8,128)(2,1)S(1)}, u32[]{:S(2)}, u32[]{:S(2)}) collective-permute-start(bf16[768,768]{1,0:T(8,128)(2,1)S(1)} %get-tuple-element.230), channel_id=1, source_target_pairs={{0,1},{1,0},{2,3},{3,2},{4,5},{5,4},{6,7},{7,6},{8,9},{9,8},{10,11... | collective-permute-start | bytes 3538952 | tf_op jit(solution)/shard_map/ppermute | solution.py:690
  66.3 3.3 %collective-permute-start.16 = (bf16[768,768]{1,0:T(8,128)(2,1)S(1)}, bf16[768,768]{1,0:T(8,128)(2,1)S(1)}, u32[]{:S(2)}, u32[]{:S(2)}) collective-permute-start(bf16[768,768]{1,0:T(8,128)(2,1)S(1)} %get-tuple-element.232), channel_id=1, source_target_pairs={{0,1},{1,0},{2,3},{3,2},{4,5},{5,4},{6,7},{7,6},{8,9},{9,8},{10,11... | collective-permute-start | bytes 3538952 | tf_op jit(solution)/shard_map/ppermute | solution.py:690
  69.2 5.1 %collective-permute-start.17 = (bf16[768,768]{1,0:T(8,128)(2,1)S(1)}, bf16[768,768]{1,0:T(8,128)(2,1)S(1)}, u32[]{:S(2)}, u32[]{:S(2)}) collective-permute-start(bf16[768,768]{1,0:T(8,128)(2,1)S(1)} %get-tuple-element.236), channel_id=1, source_target_pairs={{0,1},{1,0},{2,3},{3,2},{4,5},{5,4},{6,7},{7,6},{8,9},{9,8},{10,11... | collective-permute-start | bytes 3538952 | tf_op jit(solution)/shard_map/ppermute | solution.py:690
  71.0 16.3 %collective-permute-start.18 = (bf16[768,768]{1,0:T(8,128)(2,1)S(1)}, bf16[768,768]{1,0:T(8,128)(2,1)S(1)}, u32[]{:S(2)}, u32[]{:S(2)}) collective-permute-start(bf16[768,768]{1,0:T(8,128)(2,1)S(1)} %get-tuple-element.239), channel_id=1, source_target_pairs={{0,2},{1,5},{2,0},{3,7},{4,6},{5,1},{6,4},{7,3},{8,10},{9,13},{10,... | collective-permute-start | bytes 3538952 | tf_op jit(solution)/shard_map/ppermute | solution.py:690
  71.6 3.7 %copy-start.19 = (bf16[768,768]{1,0:T(8,128)(2,1)S(1)}, bf16[768,768]{1,0:T(8,128)(2,1)}, u32[]{:S(2)}) copy-start(bf16[768,768]{1,0:T(8,128)(2,1)} %copy-done.18) | copy-start | bytes 3538948
  71.6 3.7 %copy-start.21 = (bf16[768,768]{1,0:T(8,128)(2,1)S(1)}, bf16[768,768]{1,0:T(8,128)(2,1)}, u32[]{:S(2)}) copy-start(bf16[768,768]{1,0:T(8,128)(2,1)} %copy-done.20) | copy-start | bytes 3538948
  78.1 16.3 %collective-permute-start.20 = (bf16[768,768]{1,0:T(8,128)(2,1)S(1)}, bf16[768,768]{1,0:T(8,128)(2,1)S(1)}, u32[]{:S(2)}, u32[]{:S(2)}) collective-permute-start(bf16[768,768]{1,0:T(8,128)(2,1)S(1)} %get-tuple-element.263), channel_id=1, source_target_pairs={{0,1},{1,0},{2,3},{3,2},{4,5},{5,4},{6,7},{7,6},{8,9},{9,8},{10,11... | collective-permute-start | bytes 3538952 | tf_op jit(solution)/shard_map/ppermute | solution.py:690
  82.7 11.7 %collective-permute-start.21 = (bf16[2,192,768]{2,1,0:T(8,128)(2,1)S(1)}, bf16[2,192,768]{2,1,0:T(8,128)(2,1)S(1)}, u32[]{:S(2)}, u32[]{:S(2)}) collective-permute-start(bf16[2,192,768]{2,1,0:T(8,128)(2,1)S(1)} %get-tuple-element.264), channel_id=1, source_target_pairs={{0,1},{1,0},{2,3},{3,2},{4,5},{5,4},{6,7},{7,6},{8,9},{9,8},{10,11... | collective-permute-start | bytes 1769480 | tf_op jit(solution)/shard_map/ppermute | solution.py:690
  88.3 9.9 %collective-permute-start.19 = (bf16[384,768]{1,0:T(8,128)(2,1)S(1)}, bf16[384,768]{1,0:T(8,128)(2,1)S(1)}, u32[]{:S(2)}, u32[]{:S(2)}) collective-permute-start(bf16[384,768]{1,0:T(8,128)(2,1)S(1)} %get-tuple-element.257), channel_id=1, source_target_pairs={{0,4},{1,3},{2,6},{3,1},{4,0},{5,7},{6,2},{7,5},{8,12},{9,11},{10,... | collective-permute-start | bytes 1769480 | tf_op jit(solution)/shard_map/ppermute | solution.py:690
  88.9 5.5 %copy-start.9 = (bf16[768,768]{1,0:T(8,128)(2,1)S(1)}, bf16[768,768]{1,0:T(8,128)(2,1)}, u32[]{:S(2)}) copy-start(bf16[768,768]{1,0:T(8,128)(2,1)} %copy-done.8) | copy-start | bytes 3538948
  94.3 12.0 %collective-permute-start.22 = (bf16[576,768]{1,0:T(8,128)(2,1)S(1)}, bf16[576,768]{1,0:T(8,128)(2,1)S(1)}, u32[]{:S(2)}, u32[]{:S(2)}) collective-permute-start(bf16[576,768]{1,0:T(8,128)(2,1)S(1)} %get-tuple-element.265), channel_id=1, source_target_pairs={{0,1},{1,0},{2,3},{3,2},{4,5},{5,4},{6,7},{7,6},{8,9},{9,8},{10,11... | collective-permute-start | bytes 2654216 | tf_op jit(solution)/shard_map/ppermute | solution.py:690
  94.4 6.5 %copy-start.31 = (bf16[576,512]{1,0:T(8,128)(2,1)S(1)}, bf16[576,512]{1,0:T(8,128)(2,1)}, u32[]{:S(2)}) copy-start(bf16[576,512]{1,0:T(8,128)(2,1)} %copy-done.30) | copy-start | bytes 1769476
  96.0 4.9 %copy-start.3 = (bf16[784,768]{1,0:T(8,128)(2,1)S(1)}, bf16[784,768]{1,0:T(8,128)(2,1)}, u32[]{:S(2)}) copy-start(bf16[784,768]{1,0:T(8,128)(2,1)} %copy-done.2) | copy-start | bytes 3612676
  96.0 19.4 %collective-permute-start.23 = (bf16[960,768]{1,0:T(8,128)(2,1)S(1)}, bf16[960,768]{1,0:T(8,128)(2,1)S(1)}, u32[]{:S(2)}, u32[]{:S(2)}) collective-permute-start(bf16[960,768]{1,0:T(8,128)(2,1)S(1)} %get-tuple-element.267), channel_id=1, source_target_pairs={{0,2},{1,5},{2,0},{3,7},{4,6},{5,1},{6,4},{7,3},{8,10},{9,13},{10,... | collective-permute-start | bytes 4423688 | tf_op jit(solution)/shard_map/ppermute | solution.py:690
  99.2 12.8 %collective-permute-start.24 = (bf16[192,768]{1,0:T(8,128)(2,1)S(1)}, bf16[192,768]{1,0:T(8,128)(2,1)S(1)}, u32[]{:S(2)}, u32[]{:S(2)}) collective-permute-start(bf16[192,768]{1,0:T(8,128)(2,1)S(1)} %get-tuple-element.269), channel_id=1, source_target_pairs={{0,8},{1,17},{2,10},{3,19},{4,12},{5,21},{6,14},{7,23},{8,0},{9,25... | collective-permute-start | bytes 884744 | tf_op jit(solution)/shard_map/ppermute | solution.py:690
  100.8 5.4 %copy-start.15 = (bf16[784,768]{1,0:T(8,128)(2,1)S(1)}, bf16[784,768]{1,0:T(8,128)(2,1)}, u32[]{:S(2)}) copy-start(bf16[784,768]{1,0:T(8,128)(2,1)} %copy-done.14) | copy-start | bytes 3612676
  100.8 5.4 %copy-start.29 = (bf16[576,512]{1,0:T(8,128)(2,1)S(1)}, bf16[576,512]{1,0:T(8,128)(2,1)}, u32[]{:S(2)}) copy-start(bf16[576,512]{1,0:T(8,128)(2,1)} %copy-done.28) | copy-start | bytes 1769476
  111.7 11.9 %collective-permute-start.25 = (bf16[576,768]{1,0:T(8,128)(2,1)S(1)}, bf16[576,768]{1,0:T(8,128)(2,1)S(1)}, u32[]{:S(2)}, u32[]{:S(2)}) collective-permute-start(bf16[576,768]{1,0:T(8,128)(2,1)S(1)} %get-tuple-element.281), channel_id=1, source_target_pairs={{0,1},{1,0},{2,3},{3,2},{4,5},{5,4},{6,7},{7,6},{8,9},{9,8},{10,11... | collective-permute-start | bytes 2654216 | tf_op jit(solution)/shard_map/ppermute | solution.py:690
  112.7 10.8 %collective-permute-start.26 = (bf16[96,768]{1,0:T(8,128)(2,1)S(1)}, bf16[96,768]{1,0:T(8,128)(2,1)S(1)}, u32[]{:S(2)}, u32[]{:S(2)}) collective-permute-start(bf16[96,768]{1,0:T(8,128)(2,1)S(1)} %get-tuple-element.283), channel_id=1, source_target_pairs={{0,16},{1,9},{2,18},{3,11},{4,20},{5,13},{6,22},{7,15},{8,24},{9,1... | collective-permute-start | bytes 442376 | tf_op jit(solution)/shard_map/ppermute | solution.py:690
  116.5 11.5 %collective-permute-start.27 = (bf16[480,768]{1,0:T(8,128)(2,1)S(1)}, bf16[480,768]{1,0:T(8,128)(2,1)S(1)}, u32[]{:S(2)}, u32[]{:S(2)}) collective-permute-start(bf16[480,768]{1,0:T(8,128)(2,1)S(1)} %get-tuple-element.285), channel_id=1, source_target_pairs={{0,4},{1,3},{2,6},{3,1},{4,0},{5,7},{6,2},{7,5},{8,12},{9,11},{10,... | collective-permute-start | bytes 2211848 | tf_op jit(solution)/shard_map/ppermute | solution.py:690
  123.5 5.8 %copy-start = (f32[512,768]{1,0:T(8,128)}, f32[512,768]{1,0:T(8,128)S(1)}, u32[]{:S(2)}) copy-start(f32[512,768]{1,0:T(8,128)S(1)} %get-tuple-element.335) | copy-start | bytes 4718596
  129.3 13.6 %collective-permute-start.28 = (bf16[608,768]{1,0:T(8,128)(2,1)S(1)}, bf16[608,768]{1,0:T(8,128)(2,1)S(1)}, u32[]{:S(2)}, u32[]{:S(2)}) collective-permute-start(bf16[608,768]{1,0:T(8,128)(2,1)S(1)} %get-tuple-element.303), channel_id=1, source_target_pairs={{0,2},{1,5},{2,0},{3,7},{4,6},{5,1},{6,4},{7,3},{8,10},{9,13},{10,... | collective-permute-start | bytes 2801672 | tf_op jit(solution)/shard_map/ppermute | solution.py:690
  129.8 10.9 %collective-permute-start.29 = (bf16[96,768]{1,0:T(8,128)(2,1)S(1)}, bf16[96,768]{1,0:T(8,128)(2,1)S(1)}, u32[]{:S(2)}, u32[]{:S(2)}) collective-permute-start(bf16[96,768]{1,0:T(8,128)(2,1)S(1)} %add_convert_fusion.1), channel_id=1, source_target_pairs={{0,16},{1,9},{2,18},{3,11},{4,20},{5,13},{6,22},{7,15},{8,24},{9,1... | collective-permute-start | bytes 442376 | tf_op jit(solution)/shard_map/ppermute | solution.py:690
  133.4 13.6 %collective-permute-start.32 = (bf16[240,768]{1,0:T(8,128)(2,1)S(1)}, bf16[240,768]{1,0:T(8,128)(2,1)S(1)}, u32[]{:S(2)}, u32[]{:S(2)}) collective-permute-start(bf16[240,768]{1,0:T(8,128)(2,1)S(1)} %get-tuple-element.306), channel_id=1, source_target_pairs={{0,8},{1,17},{2,10},{3,19},{4,12},{5,21},{6,14},{7,23},{8,0},{9,25... | collective-permute-start | bytes 1105928 | tf_op jit(solution)/shard_map/ppermute | solution.py:690
  143.8 17.0 %collective-permute-start.30 = (bf16[320,768]{1,0:T(8,128)(2,1)S(1)}, bf16[320,768]{1,0:T(8,128)(2,1)S(1)}, u32[]{:S(2)}, u32[]{:S(2)}) collective-permute-start(bf16[320,768]{1,0:T(8,128)(2,1)S(1)} %get-tuple-element.311), channel_id=1, source_target_pairs={{0,4},{1,3},{2,6},{3,1},{4,0},{5,7},{6,2},{7,5},{8,12},{9,11},{10,... | collective-permute-start | bytes 1474568 | tf_op jit(solution)/shard_map/ppermute | solution.py:690
  145.6 14.7 %collective-permute-start.31 = (bf16[192,768]{1,0:T(8,128)(2,1)S(1)}, bf16[192,768]{1,0:T(8,128)(2,1)S(1)}, u32[]{:S(2)}, u32[]{:S(2)}) collective-permute-start(bf16[192,768]{1,0:T(8,128)(2,1)S(1)} %pad_maximum_fusion.5), channel_id=1, source_target_pairs={{0,8},{1,17},{2,10},{3,19},{4,12},{5,21},{6,14},{7,23},{8,0},{9,25... | collective-permute-start | bytes 884744 | tf_op jit(solution)/shard_map/ppermute | solution.py:690
  147.7 13.9 %collective-permute-start.34 = (bf16[120,768]{1,0:T(8,128)(2,1)S(1)}, bf16[120,768]{1,0:T(8,128)(2,1)S(1)}, u32[]{:S(2)}, u32[]{:S(2)}) collective-permute-start(bf16[120,768]{1,0:T(8,128)(2,1)S(1)} %get-tuple-element.314), channel_id=1, source_target_pairs={{0,16},{1,9},{2,18},{3,11},{4,20},{5,13},{6,22},{7,15},{8,24},{9,1... | collective-permute-start | bytes 552968 | tf_op jit(solution)/shard_map/ppermute | solution.py:690
  160.4 15.4 %collective-permute-start.36 = (bf16[384,768]{1,0:T(8,128)(2,1)S(1)}, bf16[384,768]{1,0:T(8,128)(2,1)S(1)}, u32[]{:S(2)}, u32[]{:S(2)}) collective-permute-start(bf16[384,768]{1,0:T(8,128)(2,1)S(1)} %pad_maximum_fusion.2.mine), channel_id=1, source_target_pairs={{0,4},{1,5},{2,6},{3,7},{4,0},{5,1},{6,2},{7,3},{8,12},{9,13},{10,... | collective-permute-start | bytes 1769480 | tf_op jit(solution)/shard_map/ppermute | solution.py:690
  161.5 11.7 %collective-permute-start.33 = (bf16[176,768]{1,0:T(8,128)(2,1)S(1)}, bf16[176,768]{1,0:T(8,128)(2,1)S(1)}, u32[]{:S(2)}, u32[]{:S(2)}) collective-permute-start(bf16[176,768]{1,0:T(8,128)(2,1)S(1)} %get-tuple-element.319), channel_id=1, source_target_pairs={{0,8},{1,17},{2,10},{3,19},{4,12},{5,21},{6,14},{7,23},{8,0},{9,25... | collective-permute-start | bytes 811016 | tf_op jit(solution)/shard_map/ppermute | solution.py:690
  161.7 12.3 %collective-permute-start.37 = (bf16[120,768]{1,0:T(8,128)(2,1)S(1)}, bf16[120,768]{1,0:T(8,128)(2,1)S(1)}, u32[]{:S(2)}, u32[]{:S(2)}) collective-permute-start(bf16[120,768]{1,0:T(8,128)(2,1)S(1)} %add_convert_fusion), channel_id=1, source_target_pairs={{0,16},{1,9},{2,18},{3,11},{4,20},{5,13},{6,22},{7,15},{8,24},{9,1... | collective-permute-start | bytes 552968 | tf_op jit(solution)/shard_map/ppermute | solution.py:690
  173.9 7.7 %collective-permute-start.35 = (bf16[104,768]{1,0:T(8,128)(2,1)S(1)}, bf16[104,768]{1,0:T(8,128)(2,1)S(1)}, u32[]{:S(2)}, u32[]{:S(2)}) collective-permute-start(bf16[104,768]{1,0:T(8,128)(2,1)S(1)} %get-tuple-element.325), channel_id=1, source_target_pairs={{0,16},{1,9},{2,18},{3,11},{4,20},{5,13},{6,22},{7,15},{8,24},{9,1... | collective-permute-start | bytes 479240 | tf_op jit(solution)/shard_map/ppermute | solution.py:690
  174.0 10.9 %collective-permute-start.39 = (bf16[240,768]{1,0:T(8,128)(2,1)S(1)}, bf16[240,768]{1,0:T(8,128)(2,1)S(1)}, u32[]{:S(2)}, u32[]{:S(2)}) collective-permute-start(bf16[240,768]{1,0:T(8,128)(2,1)S(1)} %pad_maximum_fusion.4), channel_id=1, source_target_pairs={{0,8},{1,17},{2,10},{3,19},{4,12},{5,21},{6,14},{7,23},{8,0},{9,25... | collective-permute-start | bytes 1105928 | tf_op jit(solution)/shard_map/ppermute | solution.py:690
  181.6 10.4 %copy-start.34 = (bf16[72,768]{1,0:T(8,128)(2,1)}, bf16[72,768]{1,0:T(8,128)(2,1)S(1)}, u32[]{:S(2)}) copy-start(bf16[72,768]{1,0:T(8,128)(2,1)S(1)} %add_convert_fusion.2) | copy-start | bytes 331780
  181.6 10.3 %collective-permute-start.38 = (bf16[72,768]{1,0:T(8,128)(2,1)S(1)}, bf16[72,768]{1,0:T(8,128)(2,1)S(1)}, u32[]{:S(2)}, u32[]{:S(2)}) collective-permute-start(bf16[72,768]{1,0:T(8,128)(2,1)S(1)} %add_convert_fusion.2), channel_id=1, source_target_pairs={{0,16},{1,9},{2,18},{3,11},{4,20},{5,13},{6,22},{7,15},{8,24},{9,1... | collective-permute-start | bytes 331784 | tf_op jit(solution)/shard_map/ppermute | solution.py:690
  185.0 19.5 %collective-permute-start.43 = (bf16[480,768]{1,0:T(8,128)(2,1)S(1)}, bf16[480,768]{1,0:T(8,128)(2,1)S(1)}, u32[]{:S(2)}, u32[]{:S(2)}) collective-permute-start(bf16[480,768]{1,0:T(8,128)(2,1)S(1)} %pad_maximum_fusion.mine), channel_id=1, source_target_pairs={{0,4},{1,5},{2,6},{3,7},{4,0},{5,1},{6,2},{7,3},{8,12},{9,13},{10,... | collective-permute-start | bytes 2211848 | tf_op jit(solution)/shard_map/ppermute | solution.py:690
  191.9 6.0 %collective-permute-start.40 = (bf16[144,768]{1,0:T(8,128)(2,1)S(1)}, bf16[144,768]{1,0:T(8,128)(2,1)S(1)}, u32[]{:S(2)}, u32[]{:S(2)}) collective-permute-start(bf16[144,768]{1,0:T(8,128)(2,1)S(1)} %pad_maximum_fusion.6), channel_id=1, source_target_pairs={{0,8},{1,17},{2,10},{3,19},{4,12},{5,21},{6,14},{7,23},{8,0},{9,25... | collective-permute-start | bytes 663560 | tf_op jit(solution)/shard_map/ppermute | solution.py:690
  192.6 1.4 collective-permute-start.41
  199.7 9.9 %collective-permute-start.42 = (bf16[288,768]{1,0:T(8,128)(2,1)S(1)}, bf16[288,768]{1,0:T(8,128)(2,1)}, u32[]{:S(2)}, u32[]{:S(2)}) collective-permute-start(bf16[288,768]{1,0:T(8,128)(2,1)S(1)} %pad_maximum_fusion.3.mine), channel_id=1, source_target_pairs={{0,4},{1,5},{2,6},{3,7},{4,0},{5,1},{6,2},{7,3},{8,12},{9,13},{10,... | collective-permute-start | bytes 1327112 | tf_op jit(solution)/shard_map/ppermute | solution.py:690
  (19 other events, 38.5 us)

commit v2 on v1

--- a/solution.py
+++ b/solution.py
@@ -843,11 +843,11 @@
     far_pack = Gather(plan, near, BIAS_ROWS)
     up = Gather.of_two(plan, tie(up_far, near))
     pack_c = partner(tie(pack_d, near))
-    down = Gather.of_two(plan, tie(down_far, far_pack.got))
     far_pack.second()
     *saved_d, bias_d, part = attention(tie(tokens, far_pack.held), pack_d, small=True)
     far_pack.after(part)
     far_pack.third()
+    down = Gather.of_two(plan, tie(down_far, far_pack.held))
     *saved_c, bias_c, part = attention(tokens, pack_c, tie(part, far_pack.held), small=True)
     far_pack.after(part)
     pack_b = far_pack.result()
@@ -914,12 +914,12 @@
         saved_c, first_low, tokens, tie(part, core_other), pack_c
     )
     core_own = partner(grad_c)
-    down.after(grad_c)
+    up.after(grad_c)
+    up.second()
+    down.after(up.sent)
     down.fourth()
-    up.after(down.sent)
-    up.second()
     grad_d, bias_d, grad_tokens = attention_back(
-        saved_d, first_low, tokens, tie(part, up.sent), pack_d
+        saved_d, first_low, tokens, tie(part, down.sent), pack_d
     )
     down.after(grad_tokens)
     down.fifth()
@@ -935,40 +935,34 @@
     up.third()
     down.after(up.sent)
     down.sixth()
-
     attn.after(down.sent)
     attn.second()
     up.after(attn.sent)
     up.fourth()
     down.after(up.sent)
     down.seventh()
-
     attn.after(down.sent)
     attn.third()
     up.after(attn.sent)
     up.fifth()
-
     attn.after(up.sent)
     attn.fourth()
     up.after(attn.sent)
     up.sixth()
-    down.after(up.sent)
-    (grad_w_down,) = down.result((width,))
-
-    attn.after(grad_w_down)
+    attn.after(up.sent)
     attn.fifth()
     (sums,) = attn.vectors
     others = partner(sums)
     up.after(attn.sent)
     up.seventh()
-
-    attn.after(up.sent)
+    down.after(up.sent)
+    (grad_w_down,) = down.result((width,))
+    attn.after(grad_w_down)
     attn.sixth()
     sums = sums + tie(others, attn.sent)
     shard = lax.axis_index("tensor")
     attn_vectors = lax.dynamic_index_in_dim(sums, shard, 0, keepdims=False)
     up_vector = lax.dynamic_index_in_dim(sums, 4 + shard, 0, keepdims=False)
-
     attn.after(attn_vectors, up_vector)
     attn.seventh()
     up.after(attn.sent)

time: 213 us -> 212 us (level)
  starting transfers between devices: 43.6 us -> 40.1 us
  waiting for transfers between devices: 64.8 us -> 67.5 us
    ppermute x44, starting transfers between devices: 43.6 us -> 40.1 us  [swap(): return lax.ppermute(value, ('dp', 'tensor'), pairs)]
    ppermute x44, waiting for transfers between devices: 64.8 us -> 67.5 us  [swap(): return lax.ppermute(value, ('dp', 'tensor'), pairs)]
where the time goes in v2:
time: 212 us
  Pallas kernels  89.4 us (42%)
  waiting for transfers between devices  67.5 us (32%)
  starting transfers between devices  40.1 us (19%)
  local copies, waits for them, and re-layouts  8.18 us (4%)
  other arithmetic  4.64 us (2%)
    pallas_call x34, Pallas kernels, run(): pl.pallas_call(kernel, in_specs=specs, out_specs=[pl.BlockSpec(memory_spa...  76.8 us
    ppermute x44, waiting for transfers between devices, swap(): return lax.ppermute(value, ('dp', 'tensor'), pairs)  67.5 us
    ppermute x44, starting transfers between devices, swap(): return lax.ppermute(value, ('dp', 'tensor'), pairs)  40.1 us
    pallas_call x3, Pallas kernels, finish(): pl.pallas_call(functools.partial(finish_kernel, sizes), grid_spec=pltpu.P...  6.9 us
    unnamed x78, local copies, waits for them, and re-layouts  5.68 us
  transfers between devices with their start and end apart: 44, of which 17 were waited for; matrix products, arithmetic and copies ran while one was open for 3% of the time, Pallas kernels for 37%

profile of v2, /device:TPU:0, one launch (start us, length us, event | category | flops | bytes accessed | tf_op | source)
XLA Modules:
  0.0 211.7 jit_solution(1289440642927569053)
XLA Ops:
  1.6 2.4 %pack_near.1.near = bf16[208,768]{1,0:T(8,128)(2,1)} custom-call(s32[34]{0:T(128)} %broadcast_select_fusion.plan, bf16[192,768]{1,0:T(8,128)(2,1)} %bitcast.59, bf16[192,768]{1,0:T(8,128)(2,1)} %bitcast.61, bf16[192,768]{1,0:T(8,128)(2,1)} %bitcast.63, bf16[192,768]{1,0:T(8,128)(2,1)} %wo.3, bf16[192]{0:T(256)(128)(2,1)} %bq.1, bf16[192]{0:T(256)(128)(2,1)} %bv.1, ...), custom_call_target="tpu_custom_call" | custom-call | tf_op jit(solution)/shard_map/pack_near/pallas_call | solution.py:86
  4.0 3.0 %collective-permute-start = (bf16[208,768]{1,0:T(8,128)(2,1)}, bf16[208,768]{1,0:T(8,128)(2,1)S(1)}, u32[]{:S(2)}, u32[]{:S(2)}) collective-permute-start(bf16[208,768]{1,0:T(8,128)(2,1)} %pack_near.1.near), channel_id=1, source_target_pairs={{0,2},{1,3},{2,0},{3,1},{4,6},{5,7},{6,4},{7,5},{8,10},{9,11},{10,... | collective-permute-start | bytes 958472 | tf_op jit(solution)/shard_map/ppermute | solution.py:690
  7.0 3.3 %pack_weights.1 = (bf16[784,768]{1,0:T(8,128)(2,1)}, bf16[384,768]{1,0:T(8,128)(2,1)}, bf16[384,768]{1,0:T(8,128)(2,1)}, f32[8,768]{1,0:T(8,128)}) custom-call(s32[34]{0:T(128)} %broadcast_select_fusion.plan, bf16[192,768]{1,0:T(8,128)(2,1)} %bitcast.60, bf16[192,768]{1,0:T(8,128)(2,1)} %bitcast.62, bf16[192,768]{1,0:T(8,128)(2,1)} %bitcast.64, ...), custom_call_target="tpu_custom_call" | custom-call | tf_op jit(solution)/shard_map/pack_weights/pallas_call | solution.py:155
  10.7 4.9 %collective-permute-done = bf16[208,768]{1,0:T(8,128)(2,1)S(1)} collective-permute-done((bf16[208,768]{1,0:T(8,128)(2,1)}, bf16[208,768]{1,0:T(8,128)(2,1)S(1)}, u32[]{:S(2)}, u32[]{:S(2)}) %collective-permute-start) | collective-permute-done | bytes 319520 | tf_op jit(solution)/shard_map/ppermute | solution.py:690
  15.6 2.1 collective-permute-start.1
  17.7 1.3 copy-done.12
  19.0 4.2 %attention.3 = (bf16[576,512]{1,0:T(8,128)(2,1)S(1)}, bf16[3,512,512]{2,1,0:T(8,128)(2,1)S(1)}, bf16[192,512]{1,0:T(8,128)(2,1)S(1)}, f32[1,768]{1,0:T(1,128)S(1)}, f32[512,768]{1,0:T(8,128)S(1)}) custom-call(bf16[512,768]{1,0:T(8,128)(2,1)S(1)} %copy-done.23, bf16[784,768]{1,0:T(8,128)(2,1)S(1)} %copy-done.12), custom_call_target="tpu_custom_call" | custom-call | flops 49999998976 | bytes 80000000 | tf_op jit(solution)/shard_map/attention/pallas_call | solution.py:48
  23.2 1.1 copy-done.26
  24.4 1.6 collective-permute-start.2
  26.1 1.5 collective-permute-start.6
  27.6 4.2 %attention.4 = (bf16[576,512]{1,0:T(8,128)(2,1)S(1)}, bf16[3,512,512]{2,1,0:T(8,128)(2,1)S(1)}, bf16[192,512]{1,0:T(8,128)(2,1)S(1)}, f32[1,768]{1,0:T(1,128)S(1)}, f32[512,768]{1,0:T(8,128)S(1)}) custom-call(bf16[512,768]{1,0:T(8,128)(2,1)S(1)} %copy-done.23, bf16[784,768]{1,0:T(8,128)(2,1)S(1)} %collective-permute-done.3.refs_1_.weights, ...), custom_call_target="tpu_custom_call" | custom-call | flops 49999998976 | bytes 80000000 | tf_op jit(solution)/shard_map/attention/pallas_call | solution.py:48
  31.9 2.5 %collective-permute-done.2 = bf16[384,768]{1,0:T(8,128)(2,1)S(1)} collective-permute-done((bf16[384,768]{1,0:T(8,128)(2,1)S(1)}, bf16[384,768]{1,0:T(8,128)(2,1)S(1)}, u32[]{:S(2)}, u32[]{:S(2)}) %collective-permute-start.2) | collective-permute-done | bytes 589856 | tf_op jit(solution)/shard_map/ppermute | solution.py:690
  35.5 2.0 collective-permute-start.8
  37.5 3.8 %attention.5 = (bf16[576,512]{1,0:T(8,128)(2,1)S(1)}, bf16[3,512,512]{2,1,0:T(8,128)(2,1)S(1)}, bf16[192,512]{1,0:T(8,128)(2,1)S(1)}, f32[1,768]{1,0:T(1,128)S(1)}, f32[512,768]{1,0:T(8,128)S(1)}) custom-call(bf16[512,768]{1,0:T(8,128)(2,1)S(1)} %copy-done.23, bf16[784,768]{1,0:T(8,128)(2,1)S(1)} %join.3.refs_1_.weights, ...), custom_call_target="tpu_custom_call" | custom-call | flops 49999998976 | bytes 80000000 | tf_op jit(solution)/shard_map/attention/pallas_call | solution.py:48
  42.2 1.5 collective-permute-start.10
  44.2 4.8 %attention_last.1 = (bf16[576,512]{1,0:T(8,128)(2,1)S(1)}, bf16[3,512,512]{2,1,0:T(8,128)(2,1)S(1)}, bf16[192,512]{1,0:T(8,128)(2,1)S(1)}, f32[1,768]{1,0:T(1,12...) custom-call(bf16[512,768]{1,0:T(8,128)(2,1)S(1)} %copy-done.23, ...), custom_call_target="tpu_custom_call" | custom-call | flops 49999998976 | bytes 80000000 | tf_op jit(solution)/shard_map/attention_last/pallas_call | solution.py:48
  50.5 1.8 feed.3
  52.3 1.8 feed.4
  55.4 1.8 feed.5
  57.9 3.6 %feed_last.1 = (bf16[512,768]{1,0:T(8,128)(2,1)S(1)}, bf16[512,768]{1,0:T(8,128)(2,1)S(1)}, f32[512,768]{1,0:T(8,128)S(1)}, bf16[512,768]{1,0:T(8,128)(2,1)S(1)}...) custom-call(bf16[512,768]{1,0:T(8,128)(2,1)S(1)} %get-tuple-element.199.refs_0_.refs_2_, ...), custom_call_target="tpu_custom_call" | custom-call | flops 49999998976 | bytes 80000000 | tf_op jit(solution)/shard_map/feed_last/pallas_call | solution.py:48
  61.5 1.4 down_grad.2
  63.3 1.4 down_grad.3
  65.0 2.7 %feed_back.3 = (bf16[768,768]{1,0:T(8,128)(2,1)S(1)}, f32[1,768]{1,0:T(1,128)S(1)}, f32[512,768]{1,0:T(8,128)S(1)}) custom-call(bf16[512,768]{1,0:T(8,128)(2,1)S(1)} %get-tuple-element.224.refs_0_, bf16[512,768]{1,0:T(8,128)(2,1)S(1)} %get-tuple-element.231.refs_2_.refs_1_, bf16[512,768]{1,0:T(8,128)(2,1)S(1)} %get-tuple-element.199.refs_0_.refs_2_, ...), custom_call_target="tpu_custom_call" | custom-call | flops 40000000000 | bytes 100000000 | tf_op jit(solution)/shard_map/feed_back/pallas_call | solution.py:48
  68.1 1.4 first_stage.3
  69.5 1.6 collective-permute-start.18
  71.1 2.7 %feed_back.4 = (bf16[768,768]{1,0:T(8,128)(2,1)S(1)}, f32[1,768]{1,0:T(1,128)S(1)}, f32[512,768]{1,0:T(8,128)S(1)}) custom-call(bf16[512,768]{1,0:T(8,128)(2,1)S(1)} %get-tuple-element.223.refs_0_, bf16[512,768]{1,0:T(8,128)(2,1)S(1)} %get-tuple-element.231.refs_2_.refs_1_, bf16[512,768]{1,0:T(8,128)(2,1)S(1)} %get-tuple-element.199.refs_0_.refs_2_, ...), custom_call_target="tpu_custom_call" | custom-call | flops 40000000000 | bytes 100000000 | tf_op jit(solution)/shard_map/feed_back/pallas_call | solution.py:48
  73.8 1.0 copy-done.8
  74.8 2.7 %feed_back.5 = (bf16[768,768]{1,0:T(8,128)(2,1)S(1)}, f32[1,768]{1,0:T(1,128)S(1)}, f32[512,768]{1,0:T(8,128)S(1)}) custom-call(bf16[512,768]{1,0:T(8,128)(2,1)S(1)} %get-tuple-element.222.refs_0_, bf16[512,768]{1,0:T(8,128)(2,1)S(1)} %get-tuple-element.231.refs_2_.refs_1_, bf16[512,768]{1,0:T(8,128)(2,1)S(1)} %get-tuple-element.199.refs_0_.refs_2_, ...), custom_call_target="tpu_custom_call" | custom-call | flops 40000000000 | bytes 100000000 | tf_op jit(solution)/shard_map/feed_back/pallas_call | solution.py:48
  77.7 3.7 %feed_back_last.1 = (bf16[768,768]{1,0:T(8,128)(2,1)S(1)}, f32[1,768]{1,0:T(1,128)S(1)}, f32[512,768]{1,0:T(8,128)S(1)}, bf16[512,768]{1,0:T(8,128)(2,1)S(1)}, f32[8,768]{1,0:T(8,128)S(1)}) custom-call(bf16[512,768]{1,0:T(8,128)(2,1)S(1)} %get-tuple-element.220.refs_0_, bf16[512,768]{1,0:T(8,128)(2,1)S(1)} %get-tuple-element.231.refs_2_.refs_1_, ...), custom_call_target="tpu_custom_call" | custom-call | flops 49999998976 | bytes 100000000 | tf_op jit(solution)/shard_map/feed_back_last/pallas_call | solution.py:48
  82.7 3.1 %collective-permute-done.18.got = bf16[768,768]{1,0:T(8,128)(2,1)S(1)} collective-permute-done((bf16[768,768]{1,0:T(8,128)(2,1)S(1)}, bf16[768,768]{1,0:T(8,128)(2,1)S(1)}, u32[]{:S(2)}, u32[]{:S(2)}) %collective-permute-start.18) | collective-permute-done | bytes 1179680 | tf_op jit(solution)/shard_map/ppermute | solution.py:690
  87.0 5.4 %attention_back.4 = (bf16[576,768]{1,0:T(8,128)(2,1)S(1)}, f32[8,576]{1,0:T(8,128)S(1)}, f32[512,768]{1,0:T(8,128)S(1)}) custom-call(bf16[576,512]{1,0:T(8,128)(2,1)S(1)} %get-tuple-element.247.qkv, bf16[3,512,512]{2,1,0:T(8,128)(2,1)S(1)} %get-tuple-element.248.probs, bf16[512,768]{1,0:T(8,128)(2,1)S(1)} %get-tuple-element.246.low.first_low, ...), custom_call_target="tpu_custom_call" | custom-call | flops 70000001024 | bytes 120000000 | tf_op jit(solution)/shard_map/attention_back/pallas_call | solution.py:48
  92.8 1.6 first_stage.4
  94.4 1.6 collective-permute-start.24
  97.7 1.6 collective-permute-start.23
  99.3 5.4 %attention_back.5 = (bf16[576,768]{1,0:T(8,128)(2,1)S(1)}, f32[8,576]{1,0:T(8,128)S(1)}, f32[512,768]{1,0:T(8,128)S(1)}) custom-call(bf16[576,512]{1,0:T(8,128)(2,1)S(1)} %copy-done.31, bf16[3,512,512]{2,1,0:T(8,128)(2,1)S(1)} %get-tuple-element.219.probs, bf16[512,768]{1,0:T(8,128)(2,1)S(1)} %get-tuple-element.246.low.first_low, ...), custom_call_target="tpu_custom_call" | custom-call | flops 70000001024 | bytes 120000000 | tf_op jit(solution)/shard_map/attention_back/pallas_call | solution.py:48
  104.8 5.4 %attention_back.6 = (bf16[576,768]{1,0:T(8,128)(2,1)S(1)}, f32[8,576]{1,0:T(8,128)S(1)}, f32[512,768]{1,0:T(8,128)S(1)}) custom-call(bf16[576,512]{1,0:T(8,128)(2,1)S(1)} %copy-done.29, bf16[3,512,512]{2,1,0:T(8,128)(2,1)S(1)} %get-tuple-element.275.probs, bf16[512,768]{1,0:T(8,128)(2,1)S(1)} %get-tuple-element.246.low.first_low, ...), custom_call_target="tpu_custom_call" | custom-call | flops 70000001024 | bytes 120000000 | tf_op jit(solution)/shard_map/attention_back/pallas_call | solution.py:48
  110.5 3.4 %collective-permute-done.24.got = bf16[960,768]{1,0:T(8,128)(2,1)S(1)} collective-permute-done((bf16[960,768]{1,0:T(8,128)(2,1)S(1)}, bf16[960,768]{1,0:T(8,128)(2,1)S(1)}, u32[]{:S(2)}, u32[]{:S(2)}) %collective-permute-start.24) | collective-permute-done | bytes 1474592 | tf_op jit(solution)/shard_map/ppermute | solution.py:690
  113.9 1.1 next_stage.11
  115.0 1.6 collective-permute-start.27
  117.2 2.7 %collective-permute-start.26 = (bf16[96,768]{1,0:T(8,128)(2,1)S(1)}, bf16[96,768]{1,0:T(8,128)(2,1)S(1)}, u32[]{:S(2)}, u32[]{:S(2)}) collective-permute-start(bf16[96,768]{1,0:T(8,128)(2,1)S(1)} %get-tuple-element.285), channel_id=1, source_target_pairs={{0,16},{1,9},{2,18},{3,11},{4,20},{5,13},{6,22},{7,15},{8,24},{9,1... | collective-permute-start | bytes 442376 | tf_op jit(solution)/shard_map/ppermute | solution.py:690
  119.9 5.4 %attention_back.7 = (bf16[576,768]{1,0:T(8,128)(2,1)S(1)}, f32[8,576]{1,0:T(8,128)S(1)}, f32[512,768]{1,0:T(8,128)S(1)}) custom-call(bf16[576,512]{1,0:T(8,128)(2,1)S(1)} %copy-done.33, bf16[3,512,512]{2,1,0:T(8,128)(2,1)S(1)} %copy-done.27, bf16[512,768]{1,0:T(8,128)(2,1)S(1)} %get-tuple-element.246.low.first_low, bf16[512,768]{1,0:T(8,128)(2,1)S(1)} %copy-done.23, ...), custom_call_target="tpu_custom_call" | custom-call | flops 70000001024 | bytes 120000000 | tf_op jit(solution)/shard_map/attention_back/pallas_call | solution.py:48
  125.3 1.2 collective-permute-done.27.got
  126.5 1.2 first_stage.5
  127.7 1.6 collective-permute-start.28
  129.3 2.6 %collective-permute-start.29 = (bf16[96,768]{1,0:T(8,128)(2,1)S(1)}, bf16[96,768]{1,0:T(8,128)(2,1)S(1)}, u32[]{:S(2)}, u32[]{:S(2)}) collective-permute-start(bf16[96,768]{1,0:T(8,128)(2,1)S(1)} %add_convert_fusion.1), channel_id=1, source_target_pairs={{0,16},{1,9},{2,18},{3,11},{4,20},{5,13},{6,22},{7,15},{8,24},{9,1... | collective-permute-start | bytes 442376 | tf_op jit(solution)/shard_map/ppermute | solution.py:690
  132.8 1.6 collective-permute-start.32
  134.4 8.2 %collective-permute-done.29 = bf16[96,768]{1,0:T(8,128)(2,1)S(1)} collective-permute-done((bf16[96,768]{1,0:T(8,128)(2,1)S(1)}, bf16[96,768]{1,0:T(8,128)(2,1)S(1)}, u32[]{:S(2)}, u32[]{:S(2)}) %collective-permute-start.29) | collective-permute-done | bytes 147488 | tf_op jit(solution)/shard_map/ppermute | solution.py:690
  145.4 1.0 collective-permute-done.32.got
  147.1 1.7 collective-permute-start.34
  148.8 10.6 %collective-permute-done.31 = bf16[192,768]{1,0:T(8,128)(2,1)S(1)} collective-permute-done((bf16[192,768]{1,0:T(8,128)(2,1)S(1)}, bf16[192,768]{1,0:T(8,128)(2,1)S(1)}, u32[]{:S(2)}, u32[]{:S(2)}) %collective-permute-start.31) | collective-permute-done | bytes 294944 | tf_op jit(solution)/shard_map/ppermute | solution.py:690
  160.3 1.7 collective-permute-start.36
  162.6 9.0 %collective-permute-done.33.got = bf16[176,768]{1,0:T(8,128)(2,1)S(1)} collective-permute-done((bf16[176,768]{1,0:T(8,128)(2,1)S(1)}, bf16[176,768]{1,0:T(8,128)(2,1)S(1)}, u32[]{:S(2)}, u32[]{:S(2)}) %collective-permute-start.33) | collective-permute-done | bytes 270368 | tf_op jit(solution)/shard_map/ppermute | solution.py:690
  172.3 1.7 collective-permute-start.39
  174.1 6.8 %collective-permute-done.35 = bf16[104,768]{1,0:T(8,128)(2,1)S(1)} collective-permute-done((bf16[104,768]{1,0:T(8,128)(2,1)S(1)}, bf16[104,768]{1,0:T(8,128)(2,1)S(1)}, u32[]{:S(2)}, u32[]{:S(2)}) %collective-permute-start.35) | collective-permute-done | bytes 159776 | tf_op jit(solution)/shard_map/ppermute | solution.py:690
  181.0 3.0 %collective-permute-done.39 = bf16[240,768]{1,0:T(8,128)(2,1)S(1)} collective-permute-done((bf16[240,768]{1,0:T(8,128)(2,1)S(1)}, bf16[240,768]{1,0:T(8,128)(2,1)S(1)}, u32[]{:S(2)}, u32[]{:S(2)}) %collective-permute-start.39) | collective-permute-done | bytes 368672 | tf_op jit(solution)/shard_map/ppermute | solution.py:690
  184.7 2.0 finish.3
  186.6 2.9 %collective-permute-done.37 = bf16[72,768]{1,0:T(8,128)(2,1)S(1)} collective-permute-done((bf16[72,768]{1,0:T(8,128)(2,1)S(1)}, bf16[72,768]{1,0:T(8,128)(2,1)S(1)}, u32[]{:S(2)}, u32[]{:S(2)}) %collective-permute-start.37) | collective-permute-done | bytes 110624 | tf_op jit(solution)/shard_map/ppermute | solution.py:690
  190.2 1.4 collective-permute-done.41
  193.0 2.5 %collective-permute-done.40 = bf16[144,768]{1,0:T(8,128)(2,1)S(1)} collective-permute-done((bf16[144,768]{1,0:T(8,128)(2,1)S(1)}, bf16[144,768]{1,0:T(8,128)(2,1)S(1)}, u32[]{:S(2)}, u32[]{:S(2)}) %collective-permute-start.40) | collective-permute-done | bytes 221216 | tf_op jit(solution)/shard_map/ppermute | solution.py:690
  196.2 1.1 pad_maximum_fusion.3.mine
  197.4 1.5 fusion.3
  200.8 2.2 %finish.4 = (f32[768,768]{1,0:T(8,128)}, f32[192,768]{1,0:T(8,128)}) custom-call(s32[34]{0:T(128)S(1)} %copy-done.11, bf16[480,768]{1,0:T(8,128)(2,1)S(1)} %pad_maximum_fusion.mine, bf16[480,768]{1,0:T(8,128)(2,1)S(1)} %collective-permute-done.43.theirs), custom_call_target="tpu_custom_call" | custom-call | flops 1000 | bytes 1000 | tf_op jit(solution)/shard_map/finish/pallas_call | solution.py:659
  203.0 5.8 %collective-permute-done.42.theirs = bf16[288,768]{1,0:T(8,128)(2,1)} collective-permute-done((bf16[288,768]{1,0:T(8,128)(2,1)S(1)}, bf16[288,768]{1,0:T(8,128)(2,1)}, u32[]{:S(2)}, u32[]{:S(2)}) %collective-permute-start.42) | collective-permute-done | bytes 442400 | tf_op jit(solution)/shard_map/ppermute | solution.py:690
  208.8 2.8 %finish.5 = (f32[192,768]{1,0:T(8,128)}, f32[192,768]{1,0:T(8,128)}, f32[192,768]{1,0:T(8,128)}) custom-call(s32[34]{0:T(128)S(1)} %copy-done.11, bf16[288,768]{1,0:T(8,128)(2,1)S(1)} %pad_maximum_fusion.3.mine, bf16[288,768]{1,0:T(8,128)(2,1)} %collective-permute-done.42.theirs), custom_call_target="tpu_custom_call" | custom-call | flops 1000 | bytes 1000 | tf_op jit(solution)/shard_map/finish/pallas_call | solution.py:659
  (165 shorter events, 25.8 us)
Async XLA Ops:
  4.0 13.7 %copy-start.23 = (bf16[512,768]{1,0:T(8,128)(2,1)S(1)}, bf16[512,768]{1,0:T(8,128)(2,1)}, u32[]{:S(2)}) copy-start(bf16[512,768]{1,0:T(8,128)(2,1)} %tok.7) | copy-start | bytes 2359300
  4.0 11.6 %collective-permute-start = (bf16[208,768]{1,0:T(8,128)(2,1)}, bf16[208,768]{1,0:T(8,128)(2,1)S(1)}, u32[]{:S(2)}, u32[]{:S(2)}) collective-permute-start(bf16[208,768]{1,0:T(8,128)(2,1)} %pack_near.1.near), channel_id=1, source_target_pairs={{0,2},{1,3},{2,0},{3,1},{4,6},{5,7},{6,4},{7,5},{8,10},{9,11},{10,... | collective-permute-start | bytes 958472 | tf_op jit(solution)/shard_map/ppermute | solution.py:690
  10.3 17.3 %collective-permute-start.3 = (bf16[784,768]{1,0:T(8,128)(2,1)}, bf16[784,768]{1,0:T(8,128)(2,1)S(1)}, u32[]{:S(2)}, u32[]{:S(2)}) collective-permute-start(bf16[784,768]{1,0:T(8,128)(2,1)} %get-tuple-element.185.refs_1_.weights), channel_id=1, source_target_pairs={{0,1},{1,0},{2,3},{3,2},{4,5},{5,4},{6,7},{7,6},{8,9},{9,8},{10,11... | collective-permute-start | bytes 3612680 | tf_op jit(solution)/shard_map/ppermute | solution.py:690
  10.4 24.8 %collective-permute-start.5 = (bf16[384,768]{1,0:T(8,128)(2,1)}, bf16[384,768]{1,0:T(8,128)(2,1)S(1)}, u32[]{:S(2)}, u32[]{:S(2)}) collective-permute-start(bf16[384,768]{1,0:T(8,128)(2,1)} %get-tuple-element.190), channel_id=1, source_target_pairs={{0,2},{1,3},{2,0},{3,1},{4,6},{5,7},{6,4},{7,5},{8,10},{9,11},{10,... | collective-permute-start | bytes 1769480 | tf_op jit(solution)/shard_map/ppermute | solution.py:690
  15.6 8.8 %collective-permute-start.1 = (bf16[192,768]{1,0:T(8,128)(2,1)S(1)}, bf16[192,768]{1,0:T(8,128)(2,1)S(1)}, u32[]{:S(2)}, u32[]{:S(2)}) collective-permute-start(bf16[192,768]{1,0:T(8,128)(2,1)S(1)} %slice.84.refs_0_), channel_id=1, source_target_pairs={{0,4},{1,9},{2,6},{3,11},{4,0},{5,13},{6,2},{7,15},{8,12},{9,1},{1... | collective-permute-start | bytes 884744 | tf_op jit(solution)/shard_map/ppermute | solution.py:690
  19.0 7.1 %copy-start.38 = (bf16[384,768]{1,0:T(8,128)(2,1)S(1)}, bf16[384,768]{1,0:T(8,128)(2,1)}, u32[]{:S(2)}) copy-start(bf16[384,768]{1,0:T(8,128)(2,1)} %get-tuple-element.195) | copy-start | bytes 1769476
  24.4 9.9 %collective-permute-start.2 = (bf16[384,768]{1,0:T(8,128)(2,1)S(1)}, bf16[384,768]{1,0:T(8,128)(2,1)S(1)}, u32[]{:S(2)}, u32[]{:S(2)}) collective-permute-start(bf16[384,768]{1,0:T(8,128)(2,1)S(1)} %pad_maximum_fusion.1), channel_id=1, source_target_pairs={{0,8},{1,5},{2,10},{3,7},{4,12},{5,1},{6,14},{7,3},{8,0},{9,13},{1... | collective-permute-start | bytes 1769480 | tf_op jit(solution)/shard_map/ppermute | solution.py:690
  26.1 8.3 %copy-start.10 = (s32[34]{0:T(128)S(1)}, s32[34]{0:T(128)}, u32[]{:S(2)}) copy-start(s32[34]{0:T(128)} %broadcast_select_fusion.plan) | copy-start | bytes 412
  26.1 15.3 %collective-permute-start.6 = (bf16[384,768]{1,0:T(8,128)(2,1)S(1)}, bf16[384,768]{1,0:T(8,128)(2,1)S(1)}, u32[]{:S(2)}, u32[]{:S(2)}) collective-permute-start(bf16[384,768]{1,0:T(8,128)(2,1)S(1)} %copy-done.38), channel_id=1, source_target_pairs={{0,2},{1,3},{2,0},{3,1},{4,6},{5,7},{6,4},{7,5},{8,10},{9,11},{10,... | collective-permute-start | bytes 1769480 | tf_op jit(solution)/shard_map/ppermute | solution.py:690
  27.6 4.2 %copy-start.14 = (bf16[784,768]{1,0:T(8,128)(2,1)}, bf16[784,768]{1,0:T(8,128)(2,1)S(1)}, u32[]{:S(2)}) copy-start(bf16[784,768]{1,0:T(8,128)(2,1)S(1)} %collective-permute-done.3.refs_1_.weights) | copy-start | bytes 3612676
  35.2 6.2 %copy-start.2 = (bf16[784,768]{1,0:T(8,128)(2,1)}, bf16[784,768]{1,0:T(8,128)(2,1)S(1)}, u32[]{:S(2)}) copy-start(bf16[784,768]{1,0:T(8,128)(2,1)S(1)} %join.3.refs_1_.weights) | copy-start | bytes 3612676
  35.2 8.9 %collective-permute-start.4 = (bf16[784,768]{1,0:T(8,128)(2,1)S(1)}, bf16[784,768]{1,0:T(8,128)(2,1)S(1)}, u32[]{:S(2)}, u32[]{:S(2)}) collective-permute-start(bf16[784,768]{1,0:T(8,128)(2,1)S(1)} %join.3.refs_1_.weights), channel_id=1, source_target_pairs={{0,1},{1,0},{2,3},{3,2},{4,5},{5,4},{6,7},{7,6},{8,9},{9,8},{10,11... | collective-permute-start | bytes 3612680 | tf_op jit(solution)/shard_map/ppermute | solution.py:690
  35.3 8.8 %copy-start.4 = (bf16[768,768]{1,0:T(8,128)(2,1)S(1)}, bf16[768,768]{1,0:T(8,128)(2,1)}, u32[]{:S(2)}) copy-start(bf16[768,768]{1,0:T(8,128)(2,1)} %refs_4_.3) | copy-start | bytes 3538948
  35.3 8.9 %copy-start.24 = (f32[8,768]{1,0:T(8,128)S(1)}, f32[8,768]{1,0:T(8,128)}, u32[]{:S(2)}) copy-start(f32[8,768]{1,0:T(8,128)} %get-tuple-element.198.refs_3_.refs_5_.refs_8_) | copy-start | bytes 73732
  35.3 13.7 %collective-permute-start.7 = (bf16[192,768]{1,0:T(8,128)(2,1)S(1)}, bf16[192,768]{1,0:T(8,128)(2,1)S(1)}, u32[]{:S(2)}, u32[]{:S(2)}) collective-permute-start(bf16[192,768]{1,0:T(8,128)(2,1)S(1)} %get-tuple-element.353.refs_0_), channel_id=1, source_target_pairs={{0,4},{1,5},{2,6},{3,7},{4,0},{5,1},{6,2},{7,3},{8,12},{9,13},{10,... | collective-permute-start | bytes 884744 | tf_op jit(solution)/shard_map/ppermute | solution.py:690
  35.5 14.1 %collective-permute-start.8 = (bf16[192,768]{1,0:T(8,128)(2,1)S(1)}, bf16[192,768]{1,0:T(8,128)(2,1)S(1)}, u32[]{:S(2)}, u32[]{:S(2)}) collective-permute-start(bf16[192,768]{1,0:T(8,128)(2,1)S(1)} %get-tuple-element.353.refs_0_), channel_id=1, source_target_pairs={{0,8},{1,9},{2,10},{3,11},{4,12},{5,13},{6,14},{7,15},{8,0},{9,1},... | collective-permute-start | bytes 884744 | tf_op jit(solution)/shard_map/ppermute | solution.py:690
  42.2 12.0 %collective-permute-start.10 = (bf16[192,768]{1,0:T(8,128)(2,1)S(1)}, bf16[192,768]{1,0:T(8,128)(2,1)S(1)}, u32[]{:S(2)}, u32[]{:S(2)}) collective-permute-start(bf16[192,768]{1,0:T(8,128)(2,1)S(1)} %get-tuple-element.351.refs_0_), channel_id=1, source_target_pairs={{0,4},{1,5},{2,6},{3,7},{4,0},{5,1},{6,2},{7,3},{8,12},{9,13},{10,... | collective-permute-start | bytes 884744 | tf_op jit(solution)/shard_map/ppermute | solution.py:690
  43.7 10.5 %collective-permute-start.11 = (bf16[192,768]{1,0:T(8,128)(2,1)S(1)}, bf16[192,768]{1,0:T(8,128)(2,1)S(1)}, u32[]{:S(2)}, u32[]{:S(2)}) collective-permute-start(bf16[192,768]{1,0:T(8,128)(2,1)S(1)} %get-tuple-element.351.refs_0_), channel_id=1, source_target_pairs={{0,8},{1,9},{2,10},{3,11},{4,12},{5,13},{6,14},{7,15},{8,0},{9,1},... | collective-permute-start | bytes 884744 | tf_op jit(solution)/shard_map/ppermute | solution.py:690
  44.1 4.9 %copy-start.16 = (bf16[784,768]{1,0:T(8,128)(2,1)}, bf16[784,768]{1,0:T(8,128)(2,1)S(1)}, u32[]{:S(2)}) copy-start(bf16[784,768]{1,0:T(8,128)(2,1)S(1)} %collective-permute-done.4.refs_1_.weights) | copy-start | bytes 3612676
  44.1 8.1 %collective-permute-start.12 = (bf16[768,768]{1,0:T(8,128)(2,1)S(1)}, bf16[768,768]{1,0:T(8,128)(2,1)S(1)}, u32[]{:S(2)}, u32[]{:S(2)}) collective-permute-start(bf16[768,768]{1,0:T(8,128)(2,1)S(1)} %copy-done.4), channel_id=1, source_target_pairs={{0,1},{1,0},{2,3},{3,2},{4,5},{5,4},{6,7},{7,6},{8,9},{9,8},{10,11... | collective-permute-start | bytes 3538952 | tf_op jit(solution)/shard_map/ppermute | solution.py:690
  44.2 4.9 %copy-start.6 = (bf16[768,768]{1,0:T(8,128)(2,1)S(1)}, bf16[768,768]{1,0:T(8,128)(2,1)}, u32[]{:S(2)}) copy-start(bf16[768,768]{1,0:T(8,128)(2,1)} %refs_5_.3) | copy-start | bytes 3538948
  49.1 3.2 %collective-permute-start.13 = (bf16[768,768]{1,0:T(8,128)(2,1)S(1)}, bf16[768,768]{1,0:T(8,128)(2,1)S(1)}, u32[]{:S(2)}, u32[]{:S(2)}) collective-permute-start(bf16[768,768]{1,0:T(8,128)(2,1)S(1)} %copy-done.6), channel_id=1, source_target_pairs={{0,1},{1,0},{2,3},{3,2},{4,5},{5,4},{6,7},{7,6},{8,9},{9,8},{10,11... | collective-permute-start | bytes 3538952 | tf_op jit(solution)/shard_map/ppermute | solution.py:690
  50.4 6.9 %collective-permute-start.9 = (bf16[768,768]{1,0:T(8,128)(2,1)S(1)}, bf16[768,768]{1,0:T(8,128)(2,1)S(1)}, u32[]{:S(2)}, u32[]{:S(2)}) collective-permute-start(bf16[768,768]{1,0:T(8,128)(2,1)S(1)} %join.4.refs_1_.refs_4_), channel_id=1, source_target_pairs={{0,1},{1,0},{2,3},{3,2},{4,5},{5,4},{6,7},{7,6},{8,9},{9,8},{10,11... | collective-permute-start | bytes 3538952 | tf_op jit(solution)/shard_map/ppermute | solution.py:690
  54.9 3.0 %collective-permute-start.14 = (bf16[768,768]{1,0:T(8,128)(2,1)S(1)}, bf16[768,768]{1,0:T(8,128)(2,1)S(1)}, u32[]{:S(2)}, u32[]{:S(2)}) collective-permute-start(bf16[768,768]{1,0:T(8,128)(2,1)S(1)} %join.5.refs_2_.refs_5_), channel_id=1, source_target_pairs={{0,1},{1,0},{2,3},{3,2},{4,5},{5,4},{6,7},{7,6},{8,9},{9,8},{10,11... | collective-permute-start | bytes 3538952 | tf_op jit(solution)/shard_map/ppermute | solution.py:690
  62.9 5.2 %collective-permute-start.15 = (bf16[768,768]{1,0:T(8,128)(2,1)S(1)}, bf16[768,768]{1,0:T(8,128)(2,1)S(1)}, u32[]{:S(2)}, u32[]{:S(2)}) collective-permute-start(bf16[768,768]{1,0:T(8,128)(2,1)S(1)} %get-tuple-element.230), channel_id=1, source_target_pairs={{0,1},{1,0},{2,3},{3,2},{4,5},{5,4},{6,7},{7,6},{8,9},{9,8},{10,11... | collective-permute-start | bytes 3538952 | tf_op jit(solution)/shard_map/ppermute | solution.py:690
  64.7 3.3 %collective-permute-start.16 = (bf16[768,768]{1,0:T(8,128)(2,1)S(1)}, bf16[768,768]{1,0:T(8,128)(2,1)S(1)}, u32[]{:S(2)}, u32[]{:S(2)}) collective-permute-start(bf16[768,768]{1,0:T(8,128)(2,1)S(1)} %get-tuple-element.232), channel_id=1, source_target_pairs={{0,1},{1,0},{2,3},{3,2},{4,5},{5,4},{6,7},{7,6},{8,9},{9,8},{10,11... | collective-permute-start | bytes 3538952 | tf_op jit(solution)/shard_map/ppermute | solution.py:690
  67.7 6.1 %collective-permute-start.17 = (bf16[768,768]{1,0:T(8,128)(2,1)S(1)}, bf16[768,768]{1,0:T(8,128)(2,1)S(1)}, u32[]{:S(2)}, u32[]{:S(2)}) collective-permute-start(bf16[768,768]{1,0:T(8,128)(2,1)S(1)} %get-tuple-element.236), channel_id=1, source_target_pairs={{0,1},{1,0},{2,3},{3,2},{4,5},{5,4},{6,7},{7,6},{8,9},{9,8},{10,11... | collective-permute-start | bytes 3538952 | tf_op jit(solution)/shard_map/ppermute | solution.py:690
  69.5 16.3 %collective-permute-start.18 = (bf16[768,768]{1,0:T(8,128)(2,1)S(1)}, bf16[768,768]{1,0:T(8,128)(2,1)S(1)}, u32[]{:S(2)}, u32[]{:S(2)}) collective-permute-start(bf16[768,768]{1,0:T(8,128)(2,1)S(1)} %get-tuple-element.239), channel_id=1, source_target_pairs={{0,2},{1,5},{2,0},{3,7},{4,6},{5,1},{6,4},{7,3},{8,10},{9,13},{10,... | collective-permute-start | bytes 3538952 | tf_op jit(solution)/shard_map/ppermute | solution.py:690
  71.1 3.7 %copy-start.19 = (bf16[768,768]{1,0:T(8,128)(2,1)S(1)}, bf16[768,768]{1,0:T(8,128)(2,1)}, u32[]{:S(2)}) copy-start(bf16[768,768]{1,0:T(8,128)(2,1)} %copy-done.18) | copy-start | bytes 3538948
  71.1 3.7 %copy-start.21 = (bf16[768,768]{1,0:T(8,128)(2,1)S(1)}, bf16[768,768]{1,0:T(8,128)(2,1)}, u32[]{:S(2)}) copy-start(bf16[768,768]{1,0:T(8,128)(2,1)} %copy-done.20) | copy-start | bytes 3538948
  77.5 15.3 %collective-permute-start.20 = (bf16[768,768]{1,0:T(8,128)(2,1)S(1)}, bf16[768,768]{1,0:T(8,128)(2,1)S(1)}, u32[]{:S(2)}, u32[]{:S(2)}) collective-permute-start(bf16[768,768]{1,0:T(8,128)(2,1)S(1)} %get-tuple-element.263), channel_id=1, source_target_pairs={{0,1},{1,0},{2,3},{3,2},{4,5},{5,4},{6,7},{7,6},{8,9},{9,8},{10,11... | collective-permute-start | bytes 3538952 | tf_op jit(solution)/shard_map/ppermute | solution.py:690
  82.1 10.7 %collective-permute-start.21 = (bf16[2,192,768]{2,1,0:T(8,128)(2,1)S(1)}, bf16[2,192,768]{2,1,0:T(8,128)(2,1)S(1)}, u32[]{:S(2)}, u32[]{:S(2)}) collective-permute-start(bf16[2,192,768]{2,1,0:T(8,128)(2,1)S(1)} %get-tuple-element.264), channel_id=1, source_target_pairs={{0,1},{1,0},{2,3},{3,2},{4,5},{5,4},{6,7},{7,6},{8,9},{9,8},{10,11... | collective-permute-start | bytes 1769480 | tf_op jit(solution)/shard_map/ppermute | solution.py:690
  86.7 9.9 %collective-permute-start.19 = (bf16[384,768]{1,0:T(8,128)(2,1)S(1)}, bf16[384,768]{1,0:T(8,128)(2,1)S(1)}, u32[]{:S(2)}, u32[]{:S(2)}) collective-permute-start(bf16[384,768]{1,0:T(8,128)(2,1)S(1)} %get-tuple-element.257), channel_id=1, source_target_pairs={{0,4},{1,3},{2,6},{3,1},{4,0},{5,7},{6,2},{7,5},{8,12},{9,11},{10,... | collective-permute-start | bytes 1769480 | tf_op jit(solution)/shard_map/ppermute | solution.py:690
  87.0 5.8 %copy-start.9 = (bf16[768,768]{1,0:T(8,128)(2,1)S(1)}, bf16[768,768]{1,0:T(8,128)(2,1)}, u32[]{:S(2)}) copy-start(bf16[768,768]{1,0:T(8,128)(2,1)} %copy-done.8) | copy-start | bytes 3538948
  92.4 12.3 %collective-permute-start.22 = (bf16[576,768]{1,0:T(8,128)(2,1)S(1)}, bf16[576,768]{1,0:T(8,128)(2,1)S(1)}, u32[]{:S(2)}, u32[]{:S(2)}) collective-permute-start(bf16[576,768]{1,0:T(8,128)(2,1)S(1)} %get-tuple-element.265), channel_id=1, source_target_pairs={{0,1},{1,0},{2,3},{3,2},{4,5},{5,4},{6,7},{7,6},{8,9},{9,8},{10,11... | collective-permute-start | bytes 2654216 | tf_op jit(solution)/shard_map/ppermute | solution.py:690
  92.8 6.5 %copy-start.31 = (bf16[576,512]{1,0:T(8,128)(2,1)S(1)}, bf16[576,512]{1,0:T(8,128)(2,1)}, u32[]{:S(2)}) copy-start(bf16[576,512]{1,0:T(8,128)(2,1)} %copy-done.30) | copy-start | bytes 1769476
  94.4 4.9 %copy-start.3 = (bf16[784,768]{1,0:T(8,128)(2,1)S(1)}, bf16[784,768]{1,0:T(8,128)(2,1)}, u32[]{:S(2)}) copy-start(bf16[784,768]{1,0:T(8,128)(2,1)} %copy-done.2) | copy-start | bytes 3612676
  94.4 19.4 %collective-permute-start.24 = (bf16[960,768]{1,0:T(8,128)(2,1)S(1)}, bf16[960,768]{1,0:T(8,128)(2,1)S(1)}, u32[]{:S(2)}, u32[]{:S(2)}) collective-permute-start(bf16[960,768]{1,0:T(8,128)(2,1)S(1)} %get-tuple-element.267), channel_id=1, source_target_pairs={{0,2},{1,5},{2,0},{3,7},{4,6},{5,1},{6,4},{7,3},{8,10},{9,13},{10,... | collective-permute-start | bytes 4423688 | tf_op jit(solution)/shard_map/ppermute | solution.py:690
  97.7 18.9 %collective-permute-start.23 = (bf16[192,768]{1,0:T(8,128)(2,1)S(1)}, bf16[192,768]{1,0:T(8,128)(2,1)S(1)}, u32[]{:S(2)}, u32[]{:S(2)}) collective-permute-start(bf16[192,768]{1,0:T(8,128)(2,1)S(1)} %get-tuple-element.269), channel_id=1, source_target_pairs={{0,8},{1,17},{2,10},{3,19},{4,12},{5,21},{6,14},{7,23},{8,0},{9,25... | collective-permute-start | bytes 884744 | tf_op jit(solution)/shard_map/ppermute | solution.py:690
  99.3 5.4 %copy-start.15 = (bf16[784,768]{1,0:T(8,128)(2,1)S(1)}, bf16[784,768]{1,0:T(8,128)(2,1)}, u32[]{:S(2)}) copy-start(bf16[784,768]{1,0:T(8,128)(2,1)} %copy-done.14) | copy-start | bytes 3612676
  99.3 5.4 %copy-start.29 = (bf16[576,512]{1,0:T(8,128)(2,1)S(1)}, bf16[576,512]{1,0:T(8,128)(2,1)}, u32[]{:S(2)}) copy-start(bf16[576,512]{1,0:T(8,128)(2,1)} %copy-done.28) | copy-start | bytes 1769476
  110.1 15.2 %collective-permute-start.25 = (bf16[576,768]{1,0:T(8,128)(2,1)S(1)}, bf16[576,768]{1,0:T(8,128)(2,1)S(1)}, u32[]{:S(2)}, u32[]{:S(2)}) collective-permute-start(bf16[576,768]{1,0:T(8,128)(2,1)S(1)} %get-tuple-element.281), channel_id=1, source_target_pairs={{0,1},{1,0},{2,3},{3,2},{4,5},{5,4},{6,7},{7,6},{8,9},{9,8},{10,11... | collective-permute-start | bytes 2654216 | tf_op jit(solution)/shard_map/ppermute | solution.py:690
  113.9 6.0 %copy-start.13 = (bf16[784,768]{1,0:T(8,128)(2,1)S(1)}, bf16[784,768]{1,0:T(8,128)(2,1)}, u32[]{:S(2)}) copy-start(bf16[784,768]{1,0:T(8,128)(2,1)} %get-tuple-element.185.refs_1_.weights) | copy-start | bytes 3612676
  113.9 6.0 %copy-start.27 = (bf16[3,512,512]{2,1,0:T(8,128)(2,1)S(1)}, bf16[3,512,512]{2,1,0:T(8,128)(2,1)}, u32[]{:S(2)}) copy-start(bf16[3,512,512]{2,1,0:T(8,128)(2,1)} %copy-done.26) | copy-start | bytes 4718596
  113.9 6.0 %copy-start.33 = (bf16[576,512]{1,0:T(8,128)(2,1)S(1)}, bf16[576,512]{1,0:T(8,128)(2,1)}, u32[]{:S(2)}) copy-start(bf16[576,512]{1,0:T(8,128)(2,1)} %copy-done.32) | copy-start | bytes 1769476
  115.0 11.5 %collective-permute-start.27 = (bf16[480,768]{1,0:T(8,128)(2,1)S(1)}, bf16[480,768]{1,0:T(8,128)(2,1)S(1)}, u32[]{:S(2)}, u32[]{:S(2)}) collective-permute-start(bf16[480,768]{1,0:T(8,128)(2,1)S(1)} %get-tuple-element.283), channel_id=1, source_target_pairs={{0,4},{1,3},{2,6},{3,1},{4,0},{5,7},{6,2},{7,5},{8,12},{9,11},{10,... | collective-permute-start | bytes 2211848 | tf_op jit(solution)/shard_map/ppermute | solution.py:690
  117.2 8.1 %collective-permute-start.26 = (bf16[96,768]{1,0:T(8,128)(2,1)S(1)}, bf16[96,768]{1,0:T(8,128)(2,1)S(1)}, u32[]{:S(2)}, u32[]{:S(2)}) collective-permute-start(bf16[96,768]{1,0:T(8,128)(2,1)S(1)} %get-tuple-element.285), channel_id=1, source_target_pairs={{0,16},{1,9},{2,18},{3,11},{4,20},{5,13},{6,22},{7,15},{8,24},{9,1... | collective-permute-start | bytes 442376 | tf_op jit(solution)/shard_map/ppermute | solution.py:690
  127.7 14.9 %collective-permute-start.28 = (bf16[608,768]{1,0:T(8,128)(2,1)S(1)}, bf16[608,768]{1,0:T(8,128)(2,1)S(1)}, u32[]{:S(2)}, u32[]{:S(2)}) collective-permute-start(bf16[608,768]{1,0:T(8,128)(2,1)S(1)} %get-tuple-element.303), channel_id=1, source_target_pairs={{0,2},{1,5},{2,0},{3,7},{4,6},{5,1},{6,4},{7,3},{8,10},{9,13},{10,... | collective-permute-start | bytes 2801672 | tf_op jit(solution)/shard_map/ppermute | solution.py:690
  129.3 13.2 %collective-permute-start.29 = (bf16[96,768]{1,0:T(8,128)(2,1)S(1)}, bf16[96,768]{1,0:T(8,128)(2,1)S(1)}, u32[]{:S(2)}, u32[]{:S(2)}) collective-permute-start(bf16[96,768]{1,0:T(8,128)(2,1)S(1)} %add_convert_fusion.1), channel_id=1, source_target_pairs={{0,16},{1,9},{2,18},{3,11},{4,20},{5,13},{6,22},{7,15},{8,24},{9,1... | collective-permute-start | bytes 442376 | tf_op jit(solution)/shard_map/ppermute | solution.py:690
  132.8 13.6 %collective-permute-start.32 = (bf16[240,768]{1,0:T(8,128)(2,1)S(1)}, bf16[240,768]{1,0:T(8,128)(2,1)S(1)}, u32[]{:S(2)}, u32[]{:S(2)}) collective-permute-start(bf16[240,768]{1,0:T(8,128)(2,1)S(1)} %get-tuple-element.306), channel_id=1, source_target_pairs={{0,8},{1,17},{2,10},{3,19},{4,12},{5,21},{6,14},{7,23},{8,0},{9,25... | collective-permute-start | bytes 1105928 | tf_op jit(solution)/shard_map/ppermute | solution.py:690
  143.5 15.9 %collective-permute-start.30 = (bf16[320,768]{1,0:T(8,128)(2,1)S(1)}, bf16[320,768]{1,0:T(8,128)(2,1)S(1)}, u32[]{:S(2)}, u32[]{:S(2)}) collective-permute-start(bf16[320,768]{1,0:T(8,128)(2,1)S(1)} %get-tuple-element.311), channel_id=1, source_target_pairs={{0,4},{1,3},{2,6},{3,1},{4,0},{5,7},{6,2},{7,5},{8,12},{9,11},{10,... | collective-permute-start | bytes 1474568 | tf_op jit(solution)/shard_map/ppermute | solution.py:690
  144.4 14.9 %collective-permute-start.31 = (bf16[192,768]{1,0:T(8,128)(2,1)S(1)}, bf16[192,768]{1,0:T(8,128)(2,1)S(1)}, u32[]{:S(2)}, u32[]{:S(2)}) collective-permute-start(bf16[192,768]{1,0:T(8,128)(2,1)S(1)} %pad_maximum_fusion.5), channel_id=1, source_target_pairs={{0,8},{1,17},{2,10},{3,19},{4,12},{5,21},{6,14},{7,23},{8,0},{9,25... | collective-permute-start | bytes 884744 | tf_op jit(solution)/shard_map/ppermute | solution.py:690
  147.1 13.1 %collective-permute-start.34 = (bf16[120,768]{1,0:T(8,128)(2,1)S(1)}, bf16[120,768]{1,0:T(8,128)(2,1)S(1)}, u32[]{:S(2)}, u32[]{:S(2)}) collective-permute-start(bf16[120,768]{1,0:T(8,128)(2,1)S(1)} %get-tuple-element.314), channel_id=1, source_target_pairs={{0,16},{1,9},{2,18},{3,11},{4,20},{5,13},{6,22},{7,15},{8,24},{9,1... | collective-permute-start | bytes 552968 | tf_op jit(solution)/shard_map/ppermute | solution.py:690
  160.2 11.4 %collective-permute-start.33 = (bf16[176,768]{1,0:T(8,128)(2,1)S(1)}, bf16[176,768]{1,0:T(8,128)(2,1)S(1)}, u32[]{:S(2)}, u32[]{:S(2)}) collective-permute-start(bf16[176,768]{1,0:T(8,128)(2,1)S(1)} %get-tuple-element.319), channel_id=1, source_target_pairs={{0,8},{1,17},{2,10},{3,19},{4,12},{5,21},{6,14},{7,23},{8,0},{9,25... | collective-permute-start | bytes 811016 | tf_op jit(solution)/shard_map/ppermute | solution.py:690
  160.3 12.0 %collective-permute-start.36 = (bf16[120,768]{1,0:T(8,128)(2,1)S(1)}, bf16[120,768]{1,0:T(8,128)(2,1)S(1)}, u32[]{:S(2)}, u32[]{:S(2)}) collective-permute-start(bf16[120,768]{1,0:T(8,128)(2,1)S(1)} %add_convert_fusion), channel_id=1, source_target_pairs={{0,16},{1,9},{2,18},{3,11},{4,20},{5,13},{6,22},{7,15},{8,24},{9,1... | collective-permute-start | bytes 552968 | tf_op jit(solution)/shard_map/ppermute | solution.py:690
  162.0 22.7 %collective-permute-start.38 = (bf16[384,768]{1,0:T(8,128)(2,1)S(1)}, bf16[384,768]{1,0:T(8,128)(2,1)S(1)}, u32[]{:S(2)}, u32[]{:S(2)}) collective-permute-start(bf16[384,768]{1,0:T(8,128)(2,1)S(1)} %pad_maximum_fusion.2.mine), channel_id=1, source_target_pairs={{0,4},{1,5},{2,6},{3,7},{4,0},{5,1},{6,2},{7,3},{8,12},{9,13},{10,... | collective-permute-start | bytes 1769480 | tf_op jit(solution)/shard_map/ppermute | solution.py:690
  172.2 8.7 %collective-permute-start.35 = (bf16[104,768]{1,0:T(8,128)(2,1)S(1)}, bf16[104,768]{1,0:T(8,128)(2,1)S(1)}, u32[]{:S(2)}, u32[]{:S(2)}) collective-permute-start(bf16[104,768]{1,0:T(8,128)(2,1)S(1)} %get-tuple-element.325), channel_id=1, source_target_pairs={{0,16},{1,9},{2,18},{3,11},{4,20},{5,13},{6,22},{7,15},{8,24},{9,1... | collective-permute-start | bytes 479240 | tf_op jit(solution)/shard_map/ppermute | solution.py:690
  172.3 11.7 %collective-permute-start.39 = (bf16[240,768]{1,0:T(8,128)(2,1)S(1)}, bf16[240,768]{1,0:T(8,128)(2,1)S(1)}, u32[]{:S(2)}, u32[]{:S(2)}) collective-permute-start(bf16[240,768]{1,0:T(8,128)(2,1)S(1)} %pad_maximum_fusion.4), channel_id=1, source_target_pairs={{0,8},{1,17},{2,10},{3,19},{4,12},{5,21},{6,14},{7,23},{8,0},{9,25... | collective-permute-start | bytes 1105928 | tf_op jit(solution)/shard_map/ppermute | solution.py:690
  180.9 8.6 %copy-start.34 = (bf16[72,768]{1,0:T(8,128)(2,1)}, bf16[72,768]{1,0:T(8,128)(2,1)S(1)}, u32[]{:S(2)}) copy-start(bf16[72,768]{1,0:T(8,128)(2,1)S(1)} %add_convert_fusion.2) | copy-start | bytes 331780
  180.9 8.6 %collective-permute-start.37 = (bf16[72,768]{1,0:T(8,128)(2,1)S(1)}, bf16[72,768]{1,0:T(8,128)(2,1)S(1)}, u32[]{:S(2)}, u32[]{:S(2)}) collective-permute-start(bf16[72,768]{1,0:T(8,128)(2,1)S(1)} %add_convert_fusion.2), channel_id=1, source_target_pairs={{0,16},{1,9},{2,18},{3,11},{4,20},{5,13},{6,22},{7,15},{8,24},{9,1... | collective-permute-start | bytes 331784 | tf_op jit(solution)/shard_map/ppermute | solution.py:690
  184.0 16.8 %collective-permute-start.43 = (bf16[480,768]{1,0:T(8,128)(2,1)S(1)}, bf16[480,768]{1,0:T(8,128)(2,1)S(1)}, u32[]{:S(2)}, u32[]{:S(2)}) collective-permute-start(bf16[480,768]{1,0:T(8,128)(2,1)S(1)} %pad_maximum_fusion.mine), channel_id=1, source_target_pairs={{0,4},{1,5},{2,6},{3,7},{4,0},{5,1},{6,2},{7,3},{8,12},{9,13},{10,... | collective-permute-start | bytes 2211848 | tf_op jit(solution)/shard_map/ppermute | solution.py:690
  189.5 6.0 %collective-permute-start.40 = (bf16[144,768]{1,0:T(8,128)(2,1)S(1)}, bf16[144,768]{1,0:T(8,128)(2,1)S(1)}, u32[]{:S(2)}, u32[]{:S(2)}) collective-permute-start(bf16[144,768]{1,0:T(8,128)(2,1)S(1)} %pad_maximum_fusion.6), channel_id=1, source_target_pairs={{0,8},{1,17},{2,10},{3,19},{4,12},{5,21},{6,14},{7,23},{8,0},{9,25... | collective-permute-start | bytes 663560 | tf_op jit(solution)/shard_map/ppermute | solution.py:690
  190.1 1.4 collective-permute-start.41
  197.3 11.5 %collective-permute-start.42 = (bf16[288,768]{1,0:T(8,128)(2,1)S(1)}, bf16[288,768]{1,0:T(8,128)(2,1)}, u32[]{:S(2)}, u32[]{:S(2)}) collective-permute-start(bf16[288,768]{1,0:T(8,128)(2,1)S(1)} %pad_maximum_fusion.3.mine), channel_id=1, source_target_pairs={{0,4},{1,5},{2,6},{3,7},{4,0},{5,1},{6,2},{7,3},{8,12},{9,13},{10,... | collective-permute-start | bytes 1327112 | tf_op jit(solution)/shard_map/ppermute | solution.py:690
  (19 other events, 39.2 us)

commit v3 on v2

--- a/solution.py
+++ b/solution.py
@@ -380,7 +380,10 @@
     def grad_rows(r):
         grads[r, :] = dot(normed_low[:, r], grad_up, 0, 0).astype(BF)
 
-    by_halves(grads.shape[0], grad_rows)
+    if last:
+        by_halves(grads.shape[0], grad_rows)
+    else:
+        grad_rows(slice(None))
     part[...] = grad_in[...] + dot(grad_up, up[...], 1, 1)
     if last:
         small[...] = jnp.zeros_like(small)

time: 212 us -> 212 us (level)
  transfers between devices with their start and end apart: 44 -> 44, of which waited for: 17 -> 18; matrix products, arithmetic and copies ran while one was open for 3% -> 3% of each run, Pallas kernels for 37% -> 36%
where the time goes in v3:
time: 212 us; the launch traced here: 211 us
  Pallas kernels  87.8 us (41%)
  waiting for transfers between devices  68.9 us (33%)
  starting transfers between devices  39.7 us (19%)
  local copies, waits for them, and re-layouts  8.18 us (4%)
  other arithmetic  4.64 us (2%)
    pallas_call x34, Pallas kernels, run(): pl.pallas_call(kernel, in_specs=specs, out_specs=[pl.BlockSpec(memory_spa...  75.2 us
    ppermute x44, waiting for transfers between devices, swap(): return lax.ppermute(value, ('dp', 'tensor'), pairs)  68.9 us
    ppermute x44, starting transfers between devices, swap(): return lax.ppermute(value, ('dp', 'tensor'), pairs)  39.7 us
    pallas_call x3, Pallas kernels, finish(): pl.pallas_call(functools.partial(finish_kernel, sizes), grid_spec=pltpu.P...  6.9 us
    unnamed x78, local copies, waits for them, and re-layouts  5.68 us
  transfers between devices with their start and end apart: 44, of which 18 were waited for; matrix products, arithmetic and copies ran while one was open for 3% of the time, Pallas kernels for 36%

profile of v3, /device:TPU:0, one launch (start us, length us, event | category | flops | bytes accessed | tf_op | source)
XLA Modules:
  0.0 211.1 jit_solution(9555444025644612450)
XLA Ops:
  1.6 2.4 %pack_near.1.near = bf16[208,768]{1,0:T(8,128)(2,1)} custom-call(s32[34]{0:T(128)} %broadcast_select_fusion.plan, bf16[192,768]{1,0:T(8,128)(2,1)} %bitcast.59, bf16[192,768]{1,0:T(8,128)(2,1)} %bitcast.61, bf16[192,768]{1,0:T(8,128)(2,1)} %bitcast.63, bf16[192,768]{1,0:T(8,128)(2,1)} %wo.3, bf16[192]{0:T(256)(128)(2,1)} %bq.1, bf16[192]{0:T(256)(128)(2,1)} %bv.1, ...), custom_call_target="tpu_custom_call" | custom-call | tf_op jit(solution)/shard_map/pack_near/pallas_call | solution.py:86
  4.0 3.0 %collective-permute-start = (bf16[208,768]{1,0:T(8,128)(2,1)}, bf16[208,768]{1,0:T(8,128)(2,1)S(1)}, u32[]{:S(2)}, u32[]{:S(2)}) collective-permute-start(bf16[208,768]{1,0:T(8,128)(2,1)} %pack_near.1.near), channel_id=1, source_target_pairs={{0,2},{1,3},{2,0},{3,1},{4,6},{5,7},{6,4},{7,5},{8,10},{9,11},{10,... | collective-permute-start | bytes 958472 | tf_op jit(solution)/shard_map/ppermute | solution.py:693
  7.0 3.3 %pack_weights.1 = (bf16[784,768]{1,0:T(8,128)(2,1)}, bf16[384,768]{1,0:T(8,128)(2,1)}, bf16[384,768]{1,0:T(8,128)(2,1)}, f32[8,768]{1,0:T(8,128)}) custom-call(s32[34]{0:T(128)} %broadcast_select_fusion.plan, bf16[192,768]{1,0:T(8,128)(2,1)} %bitcast.60, bf16[192,768]{1,0:T(8,128)(2,1)} %bitcast.62, bf16[192,768]{1,0:T(8,128)(2,1)} %bitcast.64, ...), custom_call_target="tpu_custom_call" | custom-call | tf_op jit(solution)/shard_map/pack_weights/pallas_call | solution.py:155
  10.7 4.9 %collective-permute-done = bf16[208,768]{1,0:T(8,128)(2,1)S(1)} collective-permute-done((bf16[208,768]{1,0:T(8,128)(2,1)}, bf16[208,768]{1,0:T(8,128)(2,1)S(1)}, u32[]{:S(2)}, u32[]{:S(2)}) %collective-permute-start) | collective-permute-done | bytes 319520 | tf_op jit(solution)/shard_map/ppermute | solution.py:693
  15.6 2.1 collective-permute-start.1
  17.7 1.3 copy-done.12
  19.0 4.2 %attention.3 = (bf16[576,512]{1,0:T(8,128)(2,1)S(1)}, bf16[3,512,512]{2,1,0:T(8,128)(2,1)S(1)}, bf16[192,512]{1,0:T(8,128)(2,1)S(1)}, f32[1,768]{1,0:T(1,128)S(1)}, f32[512,768]{1,0:T(8,128)S(1)}) custom-call(bf16[512,768]{1,0:T(8,128)(2,1)S(1)} %copy-done.23, bf16[784,768]{1,0:T(8,128)(2,1)S(1)} %copy-done.12), custom_call_target="tpu_custom_call" | custom-call | flops 49999998976 | bytes 80000000 | tf_op jit(solution)/shard_map/attention/pallas_call | solution.py:48
  23.2 1.1 copy-done.26
  24.4 1.6 collective-permute-start.2
  26.1 1.5 collective-permute-start.6
  27.6 4.2 %attention.4 = (bf16[576,512]{1,0:T(8,128)(2,1)S(1)}, bf16[3,512,512]{2,1,0:T(8,128)(2,1)S(1)}, bf16[192,512]{1,0:T(8,128)(2,1)S(1)}, f32[1,768]{1,0:T(1,128)S(1)}, f32[512,768]{1,0:T(8,128)S(1)}) custom-call(bf16[512,768]{1,0:T(8,128)(2,1)S(1)} %copy-done.23, bf16[784,768]{1,0:T(8,128)(2,1)S(1)} %collective-permute-done.3.refs_1_.weights, ...), custom_call_target="tpu_custom_call" | custom-call | flops 49999998976 | bytes 80000000 | tf_op jit(solution)/shard_map/attention/pallas_call | solution.py:48
  31.9 2.5 %collective-permute-done.2 = bf16[384,768]{1,0:T(8,128)(2,1)S(1)} collective-permute-done((bf16[384,768]{1,0:T(8,128)(2,1)S(1)}, bf16[384,768]{1,0:T(8,128)(2,1)S(1)}, u32[]{:S(2)}, u32[]{:S(2)}) %collective-permute-start.2) | collective-permute-done | bytes 589856 | tf_op jit(solution)/shard_map/ppermute | solution.py:693
  35.5 2.0 collective-permute-start.8
  37.5 3.8 %attention.5 = (bf16[576,512]{1,0:T(8,128)(2,1)S(1)}, bf16[3,512,512]{2,1,0:T(8,128)(2,1)S(1)}, bf16[192,512]{1,0:T(8,128)(2,1)S(1)}, f32[1,768]{1,0:T(1,128)S(1)}, f32[512,768]{1,0:T(8,128)S(1)}) custom-call(bf16[512,768]{1,0:T(8,128)(2,1)S(1)} %copy-done.23, bf16[784,768]{1,0:T(8,128)(2,1)S(1)} %join.3.refs_1_.weights, ...), custom_call_target="tpu_custom_call" | custom-call | flops 49999998976 | bytes 80000000 | tf_op jit(solution)/shard_map/attention/pallas_call | solution.py:48
  42.2 1.5 collective-permute-start.10
  44.2 4.8 %attention_last.1 = (bf16[576,512]{1,0:T(8,128)(2,1)S(1)}, bf16[3,512,512]{2,1,0:T(8,128)(2,1)S(1)}, bf16[192,512]{1,0:T(8,128)(2,1)S(1)}, f32[1,768]{1,0:T(1,12...) custom-call(bf16[512,768]{1,0:T(8,128)(2,1)S(1)} %copy-done.23, ...), custom_call_target="tpu_custom_call" | custom-call | flops 49999998976 | bytes 80000000 | tf_op jit(solution)/shard_map/attention_last/pallas_call | solution.py:48
  50.5 1.8 feed.3
  52.3 1.8 feed.4
  55.4 1.8 feed.5
  57.9 3.6 %feed_last.1 = (bf16[512,768]{1,0:T(8,128)(2,1)S(1)}, bf16[512,768]{1,0:T(8,128)(2,1)S(1)}, f32[512,768]{1,0:T(8,128)S(1)}, bf16[512,768]{1,0:T(8,128)(2,1)S(1)}...) custom-call(bf16[512,768]{1,0:T(8,128)(2,1)S(1)} %get-tuple-element.199.refs_0_.refs_2_, ...), custom_call_target="tpu_custom_call" | custom-call | flops 49999998976 | bytes 80000000 | tf_op jit(solution)/shard_map/feed_last/pallas_call | solution.py:48
  61.5 1.4 down_grad.2
  63.3 1.4 down_grad.3
  65.0 2.1 feed_back.3
  67.7 1.4 first_stage.3
  69.1 1.6 collective-permute-start.18
  70.6 2.1 feed_back.4
  73.8 2.1 feed_back.5
  76.0 3.9 %feed_back_last.1 = (bf16[768,768]{1,0:T(8,128)(2,1)S(1)}, f32[1,768]{1,0:T(1,128)S(1)}, f32[512,768]{1,0:T(8,128)S(1)}, bf16[512,768]{1,0:T(8,128)(2,1)S(1)}, f32[8,768]{1,0:T(8,128)S(1)}) custom-call(bf16[512,768]{1,0:T(8,128)(2,1)S(1)} %get-tuple-element.220.refs_0_, bf16[512,768]{1,0:T(8,128)(2,1)S(1)} %get-tuple-element.231.refs_2_.refs_1_, ...), custom_call_target="tpu_custom_call" | custom-call | flops 49999998976 | bytes 100000000 | tf_op jit(solution)/shard_map/feed_back_last/pallas_call | solution.py:48
  81.2 4.1 %collective-permute-done.18.got = bf16[768,768]{1,0:T(8,128)(2,1)S(1)} collective-permute-done((bf16[768,768]{1,0:T(8,128)(2,1)S(1)}, bf16[768,768]{1,0:T(8,128)(2,1)S(1)}, u32[]{:S(2)}, u32[]{:S(2)}) %collective-permute-start.18) | collective-permute-done | bytes 1179680 | tf_op jit(solution)/shard_map/ppermute | solution.py:693
  86.6 5.4 %attention_back.4 = (bf16[576,768]{1,0:T(8,128)(2,1)S(1)}, f32[8,576]{1,0:T(8,128)S(1)}, f32[512,768]{1,0:T(8,128)S(1)}) custom-call(bf16[576,512]{1,0:T(8,128)(2,1)S(1)} %get-tuple-element.247.qkv, bf16[3,512,512]{2,1,0:T(8,128)(2,1)S(1)} %get-tuple-element.248.probs, bf16[512,768]{1,0:T(8,128)(2,1)S(1)} %get-tuple-element.246.low.first_low, ...), custom_call_target="tpu_custom_call" | custom-call | flops 70000001024 | bytes 120000000 | tf_op jit(solution)/shard_map/attention_back/pallas_call | solution.py:48
  92.5 1.6 first_stage.4
  94.1 1.6 collective-permute-start.24
  97.0 1.6 collective-permute-start.23
  98.7 5.4 %attention_back.5 = (bf16[576,768]{1,0:T(8,128)(2,1)S(1)}, f32[8,576]{1,0:T(8,128)S(1)}, f32[512,768]{1,0:T(8,128)S(1)}) custom-call(bf16[576,512]{1,0:T(8,128)(2,1)S(1)} %copy-done.31, bf16[3,512,512]{2,1,0:T(8,128)(2,1)S(1)} %get-tuple-element.219.probs, bf16[512,768]{1,0:T(8,128)(2,1)S(1)} %get-tuple-element.246.low.first_low, ...), custom_call_target="tpu_custom_call" | custom-call | flops 70000001024 | bytes 120000000 | tf_op jit(solution)/shard_map/attention_back/pallas_call | solution.py:48
  104.1 5.4 %attention_back.6 = (bf16[576,768]{1,0:T(8,128)(2,1)S(1)}, f32[8,576]{1,0:T(8,128)S(1)}, f32[512,768]{1,0:T(8,128)S(1)}) custom-call(bf16[576,512]{1,0:T(8,128)(2,1)S(1)} %copy-done.29, bf16[3,512,512]{2,1,0:T(8,128)(2,1)S(1)} %get-tuple-element.275.probs, bf16[512,768]{1,0:T(8,128)(2,1)S(1)} %get-tuple-element.246.low.first_low, ...), custom_call_target="tpu_custom_call" | custom-call | flops 70000001024 | bytes 120000000 | tf_op jit(solution)/shard_map/attention_back/pallas_call | solution.py:48
  109.8 3.7 %collective-permute-done.24.got = bf16[960,768]{1,0:T(8,128)(2,1)S(1)} collective-permute-done((bf16[960,768]{1,0:T(8,128)(2,1)S(1)}, bf16[960,768]{1,0:T(8,128)(2,1)S(1)}, u32[]{:S(2)}, u32[]{:S(2)}) %collective-permute-start.24) | collective-permute-done | bytes 1474592 | tf_op jit(solution)/shard_map/ppermute | solution.py:693
  113.5 1.1 next_stage.11
  114.6 1.5 collective-permute-start.27
  116.8 2.7 %collective-permute-start.26 = (bf16[96,768]{1,0:T(8,128)(2,1)S(1)}, bf16[96,768]{1,0:T(8,128)(2,1)S(1)}, u32[]{:S(2)}, u32[]{:S(2)}) collective-permute-start(bf16[96,768]{1,0:T(8,128)(2,1)S(1)} %get-tuple-element.285), channel_id=1, source_target_pairs={{0,16},{1,9},{2,18},{3,11},{4,20},{5,13},{6,22},{7,15},{8,24},{9,1... | collective-permute-start | bytes 442376 | tf_op jit(solution)/shard_map/ppermute | solution.py:693
  119.4 5.4 %attention_back.7 = (bf16[576,768]{1,0:T(8,128)(2,1)S(1)}, f32[8,576]{1,0:T(8,128)S(1)}, f32[512,768]{1,0:T(8,128)S(1)}) custom-call(bf16[576,512]{1,0:T(8,128)(2,1)S(1)} %copy-done.33, bf16[3,512,512]{2,1,0:T(8,128)(2,1)S(1)} %copy-done.27, bf16[512,768]{1,0:T(8,128)(2,1)S(1)} %get-tuple-element.246.low.first_low, bf16[512,768]{1,0:T(8,128)(2,1)S(1)} %copy-done.23, ...), custom_call_target="tpu_custom_call" | custom-call | flops 70000001024 | bytes 120000000 | tf_op jit(solution)/shard_map/attention_back/pallas_call | solution.py:48
  124.9 1.2 collective-permute-done.27.got
  126.1 1.2 first_stage.5
  127.3 1.6 collective-permute-start.28
  128.9 2.6 %collective-permute-start.29 = (bf16[96,768]{1,0:T(8,128)(2,1)S(1)}, bf16[96,768]{1,0:T(8,128)(2,1)S(1)}, u32[]{:S(2)}, u32[]{:S(2)}) collective-permute-start(bf16[96,768]{1,0:T(8,128)(2,1)S(1)} %add_convert_fusion.1), channel_id=1, source_target_pairs={{0,16},{1,9},{2,18},{3,11},{4,20},{5,13},{6,22},{7,15},{8,24},{9,1... | collective-permute-start | bytes 442376 | tf_op jit(solution)/shard_map/ppermute | solution.py:693
  131.5 1.1 next_stage.13
  132.6 1.6 collective-permute-start.32
  134.2 7.9 %collective-permute-done.29 = bf16[96,768]{1,0:T(8,128)(2,1)S(1)} collective-permute-done((bf16[96,768]{1,0:T(8,128)(2,1)S(1)}, bf16[96,768]{1,0:T(8,128)(2,1)S(1)}, u32[]{:S(2)}, u32[]{:S(2)}) %collective-permute-start.29) | collective-permute-done | bytes 147488 | tf_op jit(solution)/shard_map/ppermute | solution.py:693
  145.0 1.5 collective-permute-done.32.got
  147.2 1.4 collective-permute-start.34
  148.6 10.2 %collective-permute-done.31 = bf16[192,768]{1,0:T(8,128)(2,1)S(1)} collective-permute-done((bf16[192,768]{1,0:T(8,128)(2,1)S(1)}, bf16[192,768]{1,0:T(8,128)(2,1)S(1)}, u32[]{:S(2)}, u32[]{:S(2)}) %collective-permute-start.31) | collective-permute-done | bytes 294944 | tf_op jit(solution)/shard_map/ppermute | solution.py:693
  159.7 2.1 collective-permute-start.36
  162.4 8.9 %collective-permute-done.33.got = bf16[176,768]{1,0:T(8,128)(2,1)S(1)} collective-permute-done((bf16[176,768]{1,0:T(8,128)(2,1)S(1)}, bf16[176,768]{1,0:T(8,128)(2,1)S(1)}, u32[]{:S(2)}, u32[]{:S(2)}) %collective-permute-start.33) | collective-permute-done | bytes 270368 | tf_op jit(solution)/shard_map/ppermute | solution.py:693
  172.1 1.8 collective-permute-start.39
  173.9 6.7 %collective-permute-done.35 = bf16[104,768]{1,0:T(8,128)(2,1)S(1)} collective-permute-done((bf16[104,768]{1,0:T(8,128)(2,1)S(1)}, bf16[104,768]{1,0:T(8,128)(2,1)S(1)}, u32[]{:S(2)}, u32[]{:S(2)}) %collective-permute-start.35) | collective-permute-done | bytes 159776 | tf_op jit(solution)/shard_map/ppermute | solution.py:693
  180.7 2.8 %collective-permute-done.39 = bf16[240,768]{1,0:T(8,128)(2,1)S(1)} collective-permute-done((bf16[240,768]{1,0:T(8,128)(2,1)S(1)}, bf16[240,768]{1,0:T(8,128)(2,1)S(1)}, u32[]{:S(2)}, u32[]{:S(2)}) %collective-permute-start.39) | collective-permute-done | bytes 368672 | tf_op jit(solution)/shard_map/ppermute | solution.py:693
  183.7 2.0 finish.3
  185.6 3.9 %collective-permute-done.37 = bf16[72,768]{1,0:T(8,128)(2,1)S(1)} collective-permute-done((bf16[72,768]{1,0:T(8,128)(2,1)S(1)}, bf16[72,768]{1,0:T(8,128)(2,1)S(1)}, u32[]{:S(2)}, u32[]{:S(2)}) %collective-permute-start.37) | collective-permute-done | bytes 110624 | tf_op jit(solution)/shard_map/ppermute | solution.py:693
  190.2 1.4 collective-permute-done.41
  193.0 2.5 %collective-permute-done.40 = bf16[144,768]{1,0:T(8,128)(2,1)S(1)} collective-permute-done((bf16[144,768]{1,0:T(8,128)(2,1)S(1)}, bf16[144,768]{1,0:T(8,128)(2,1)S(1)}, u32[]{:S(2)}, u32[]{:S(2)}) %collective-permute-start.40) | collective-permute-done | bytes 221216 | tf_op jit(solution)/shard_map/ppermute | solution.py:693
  196.3 1.1 pad_maximum_fusion.3.mine
  197.5 1.5 fusion.3
  200.9 2.2 %finish.4 = (f32[768,768]{1,0:T(8,128)}, f32[192,768]{1,0:T(8,128)}) custom-call(s32[34]{0:T(128)S(1)} %copy-done.11, bf16[480,768]{1,0:T(8,128)(2,1)S(1)} %pad_maximum_fusion.mine, bf16[480,768]{1,0:T(8,128)(2,1)S(1)} %collective-permute-done.43.theirs), custom_call_target="tpu_custom_call" | custom-call | flops 1000 | bytes 1000 | tf_op jit(solution)/shard_map/finish/pallas_call | solution.py:662
  203.0 5.1 %collective-permute-done.42.theirs = bf16[288,768]{1,0:T(8,128)(2,1)} collective-permute-done((bf16[288,768]{1,0:T(8,128)(2,1)S(1)}, bf16[288,768]{1,0:T(8,128)(2,1)}, u32[]{:S(2)}, u32[]{:S(2)}) %collective-permute-start.42) | collective-permute-done | bytes 442400 | tf_op jit(solution)/shard_map/ppermute | solution.py:693
  208.2 2.8 %finish.5 = (f32[192,768]{1,0:T(8,128)}, f32[192,768]{1,0:T(8,128)}, f32[192,768]{1,0:T(8,128)}) custom-call(s32[34]{0:T(128)S(1)} %copy-done.11, bf16[288,768]{1,0:T(8,128)(2,1)S(1)} %pad_maximum_fusion.3.mine, bf16[288,768]{1,0:T(8,128)(2,1)} %collective-permute-done.42.theirs), custom_call_target="tpu_custom_call" | custom-call | flops 1000 | bytes 1000 | tf_op jit(solution)/shard_map/finish/pallas_call | solution.py:662
  (165 shorter events, 25.5 us)
Async XLA Ops:
  4.0 13.7 %copy-start.23 = (bf16[512,768]{1,0:T(8,128)(2,1)S(1)}, bf16[512,768]{1,0:T(8,128)(2,1)}, u32[]{:S(2)}) copy-start(bf16[512,768]{1,0:T(8,128)(2,1)} %tok.7) | copy-start | bytes 2359300
  4.0 11.6 %collective-permute-start = (bf16[208,768]{1,0:T(8,128)(2,1)}, bf16[208,768]{1,0:T(8,128)(2,1)S(1)}, u32[]{:S(2)}, u32[]{:S(2)}) collective-permute-start(bf16[208,768]{1,0:T(8,128)(2,1)} %pack_near.1.near), channel_id=1, source_target_pairs={{0,2},{1,3},{2,0},{3,1},{4,6},{5,7},{6,4},{7,5},{8,10},{9,11},{10,... | collective-permute-start | bytes 958472 | tf_op jit(solution)/shard_map/ppermute | solution.py:693
  10.3 17.3 %collective-permute-start.3 = (bf16[784,768]{1,0:T(8,128)(2,1)}, bf16[784,768]{1,0:T(8,128)(2,1)S(1)}, u32[]{:S(2)}, u32[]{:S(2)}) collective-permute-start(bf16[784,768]{1,0:T(8,128)(2,1)} %get-tuple-element.185.refs_1_.weights), channel_id=1, source_target_pairs={{0,1},{1,0},{2,3},{3,2},{4,5},{5,4},{6,7},{7,6},{8,9},{9,8},{10,11... | collective-permute-start | bytes 3612680 | tf_op jit(solution)/shard_map/ppermute | solution.py:693
  10.4 24.8 %collective-permute-start.5 = (bf16[384,768]{1,0:T(8,128)(2,1)}, bf16[384,768]{1,0:T(8,128)(2,1)S(1)}, u32[]{:S(2)}, u32[]{:S(2)}) collective-permute-start(bf16[384,768]{1,0:T(8,128)(2,1)} %get-tuple-element.190), channel_id=1, source_target_pairs={{0,2},{1,3},{2,0},{3,1},{4,6},{5,7},{6,4},{7,5},{8,10},{9,11},{10,... | collective-permute-start | bytes 1769480 | tf_op jit(solution)/shard_map/ppermute | solution.py:693
  15.6 8.8 %collective-permute-start.1 = (bf16[192,768]{1,0:T(8,128)(2,1)S(1)}, bf16[192,768]{1,0:T(8,128)(2,1)S(1)}, u32[]{:S(2)}, u32[]{:S(2)}) collective-permute-start(bf16[192,768]{1,0:T(8,128)(2,1)S(1)} %slice.84.refs_0_), channel_id=1, source_target_pairs={{0,4},{1,9},{2,6},{3,11},{4,0},{5,13},{6,2},{7,15},{8,12},{9,1},{1... | collective-permute-start | bytes 884744 | tf_op jit(solution)/shard_map/ppermute | solution.py:693
  19.0 7.1 %copy-start.38 = (bf16[384,768]{1,0:T(8,128)(2,1)S(1)}, bf16[384,768]{1,0:T(8,128)(2,1)}, u32[]{:S(2)}) copy-start(bf16[384,768]{1,0:T(8,128)(2,1)} %get-tuple-element.195) | copy-start | bytes 1769476
  24.4 3.2 %copy-start.32 = (bf16[576,512]{1,0:T(8,128)(2,1)}, bf16[576,512]{1,0:T(8,128)(2,1)S(1)}, u32[]{:S(2)}) copy-start(bf16[576,512]{1,0:T(8,128)(2,1)S(1)} %get-tuple-element.272.qkv) | copy-start | bytes 1769476
  24.4 9.9 %collective-permute-start.2 = (bf16[384,768]{1,0:T(8,128)(2,1)S(1)}, bf16[384,768]{1,0:T(8,128)(2,1)S(1)}, u32[]{:S(2)}, u32[]{:S(2)}) collective-permute-start(bf16[384,768]{1,0:T(8,128)(2,1)S(1)} %pad_maximum_fusion.1), channel_id=1, source_target_pairs={{0,8},{1,5},{2,10},{3,7},{4,12},{5,1},{6,14},{7,3},{8,0},{9,13},{1... | collective-permute-start | bytes 1769480 | tf_op jit(solution)/shard_map/ppermute | solution.py:693
  26.1 8.3 %copy-start.10 = (s32[34]{0:T(128)S(1)}, s32[34]{0:T(128)}, u32[]{:S(2)}) copy-start(s32[34]{0:T(128)} %broadcast_select_fusion.plan) | copy-start | bytes 412
  26.1 15.3 %collective-permute-start.6 = (bf16[384,768]{1,0:T(8,128)(2,1)S(1)}, bf16[384,768]{1,0:T(8,128)(2,1)S(1)}, u32[]{:S(2)}, u32[]{:S(2)}) collective-permute-start(bf16[384,768]{1,0:T(8,128)(2,1)S(1)} %copy-done.38), channel_id=1, source_target_pairs={{0,2},{1,3},{2,0},{3,1},{4,6},{5,7},{6,4},{7,5},{8,10},{9,11},{10,... | collective-permute-start | bytes 1769480 | tf_op jit(solution)/shard_map/ppermute | solution.py:693
  27.6 4.2 %copy-start.14 = (bf16[784,768]{1,0:T(8,128)(2,1)}, bf16[784,768]{1,0:T(8,128)(2,1)S(1)}, u32[]{:S(2)}) copy-start(bf16[784,768]{1,0:T(8,128)(2,1)S(1)} %collective-permute-done.3.refs_1_.weights) | copy-start | bytes 3612676
  31.9 3.3 %copy-start.28 = (bf16[576,512]{1,0:T(8,128)(2,1)}, bf16[576,512]{1,0:T(8,128)(2,1)S(1)}, u32[]{:S(2)}) copy-start(bf16[576,512]{1,0:T(8,128)(2,1)S(1)} %get-tuple-element.274.qkv) | copy-start | bytes 1769476
  35.2 6.2 %copy-start.2 = (bf16[784,768]{1,0:T(8,128)(2,1)}, bf16[784,768]{1,0:T(8,128)(2,1)S(1)}, u32[]{:S(2)}) copy-start(bf16[784,768]{1,0:T(8,128)(2,1)S(1)} %join.3.refs_1_.weights) | copy-start | bytes 3612676
  35.2 8.9 %collective-permute-start.4 = (bf16[784,768]{1,0:T(8,128)(2,1)S(1)}, bf16[784,768]{1,0:T(8,128)(2,1)S(1)}, u32[]{:S(2)}, u32[]{:S(2)}) collective-permute-start(bf16[784,768]{1,0:T(8,128)(2,1)S(1)} %join.3.refs_1_.weights), channel_id=1, source_target_pairs={{0,1},{1,0},{2,3},{3,2},{4,5},{5,4},{6,7},{7,6},{8,9},{9,8},{10,11... | collective-permute-start | bytes 3612680 | tf_op jit(solution)/shard_map/ppermute | solution.py:693
  35.3 8.8 %copy-start.4 = (bf16[768,768]{1,0:T(8,128)(2,1)S(1)}, bf16[768,768]{1,0:T(8,128)(2,1)}, u32[]{:S(2)}) copy-start(bf16[768,768]{1,0:T(8,128)(2,1)} %refs_4_.3) | copy-start | bytes 3538948
  35.3 8.9 %copy-start.24 = (f32[8,768]{1,0:T(8,128)S(1)}, f32[8,768]{1,0:T(8,128)}, u32[]{:S(2)}) copy-start(f32[8,768]{1,0:T(8,128)} %get-tuple-element.198.refs_3_.refs_5_.refs_8_) | copy-start | bytes 73732
  35.3 13.7 %collective-permute-start.7 = (bf16[192,768]{1,0:T(8,128)(2,1)S(1)}, bf16[192,768]{1,0:T(8,128)(2,1)S(1)}, u32[]{:S(2)}, u32[]{:S(2)}) collective-permute-start(bf16[192,768]{1,0:T(8,128)(2,1)S(1)} %get-tuple-element.353.refs_0_), channel_id=1, source_target_pairs={{0,4},{1,5},{2,6},{3,7},{4,0},{5,1},{6,2},{7,3},{8,12},{9,13},{10,... | collective-permute-start | bytes 884744 | tf_op jit(solution)/shard_map/ppermute | solution.py:693
  35.5 14.1 %collective-permute-start.8 = (bf16[192,768]{1,0:T(8,128)(2,1)S(1)}, bf16[192,768]{1,0:T(8,128)(2,1)S(1)}, u32[]{:S(2)}, u32[]{:S(2)}) collective-permute-start(bf16[192,768]{1,0:T(8,128)(2,1)S(1)} %get-tuple-element.353.refs_0_), channel_id=1, source_target_pairs={{0,8},{1,9},{2,10},{3,11},{4,12},{5,13},{6,14},{7,15},{8,0},{9,1},... | collective-permute-start | bytes 884744 | tf_op jit(solution)/shard_map/ppermute | solution.py:693
  42.2 12.0 %collective-permute-start.10 = (bf16[192,768]{1,0:T(8,128)(2,1)S(1)}, bf16[192,768]{1,0:T(8,128)(2,1)S(1)}, u32[]{:S(2)}, u32[]{:S(2)}) collective-permute-start(bf16[192,768]{1,0:T(8,128)(2,1)S(1)} %get-tuple-element.351.refs_0_), channel_id=1, source_target_pairs={{0,4},{1,5},{2,6},{3,7},{4,0},{5,1},{6,2},{7,3},{8,12},{9,13},{10,... | collective-permute-start | bytes 884744 | tf_op jit(solution)/shard_map/ppermute | solution.py:693
  43.7 10.5 %collective-permute-start.11 = (bf16[192,768]{1,0:T(8,128)(2,1)S(1)}, bf16[192,768]{1,0:T(8,128)(2,1)S(1)}, u32[]{:S(2)}, u32[]{:S(2)}) collective-permute-start(bf16[192,768]{1,0:T(8,128)(2,1)S(1)} %get-tuple-element.351.refs_0_), channel_id=1, source_target_pairs={{0,8},{1,9},{2,10},{3,11},{4,12},{5,13},{6,14},{7,15},{8,0},{9,1},... | collective-permute-start | bytes 884744 | tf_op jit(solution)/shard_map/ppermute | solution.py:693
  44.1 4.9 %copy-start.16 = (bf16[784,768]{1,0:T(8,128)(2,1)}, bf16[784,768]{1,0:T(8,128)(2,1)S(1)}, u32[]{:S(2)}) copy-start(bf16[784,768]{1,0:T(8,128)(2,1)S(1)} %collective-permute-done.4.refs_1_.weights) | copy-start | bytes 3612676
  44.1 8.1 %collective-permute-start.12 = (bf16[768,768]{1,0:T(8,128)(2,1)S(1)}, bf16[768,768]{1,0:T(8,128)(2,1)S(1)}, u32[]{:S(2)}, u32[]{:S(2)}) collective-permute-start(bf16[768,768]{1,0:T(8,128)(2,1)S(1)} %copy-done.4), channel_id=1, source_target_pairs={{0,1},{1,0},{2,3},{3,2},{4,5},{5,4},{6,7},{7,6},{8,9},{9,8},{10,11... | collective-permute-start | bytes 3538952 | tf_op jit(solution)/shard_map/ppermute | solution.py:693
  44.2 4.9 %copy-start.6 = (bf16[768,768]{1,0:T(8,128)(2,1)S(1)}, bf16[768,768]{1,0:T(8,128)(2,1)}, u32[]{:S(2)}) copy-start(bf16[768,768]{1,0:T(8,128)(2,1)} %refs_5_.3) | copy-start | bytes 3538948
  49.1 3.2 %collective-permute-start.13 = (bf16[768,768]{1,0:T(8,128)(2,1)S(1)}, bf16[768,768]{1,0:T(8,128)(2,1)S(1)}, u32[]{:S(2)}, u32[]{:S(2)}) collective-permute-start(bf16[768,768]{1,0:T(8,128)(2,1)S(1)} %copy-done.6), channel_id=1, source_target_pairs={{0,1},{1,0},{2,3},{3,2},{4,5},{5,4},{6,7},{7,6},{8,9},{9,8},{10,11... | collective-permute-start | bytes 3538952 | tf_op jit(solution)/shard_map/ppermute | solution.py:693
  50.4 6.9 %collective-permute-start.9 = (bf16[768,768]{1,0:T(8,128)(2,1)S(1)}, bf16[768,768]{1,0:T(8,128)(2,1)S(1)}, u32[]{:S(2)}, u32[]{:S(2)}) collective-permute-start(bf16[768,768]{1,0:T(8,128)(2,1)S(1)} %join.4.refs_1_.refs_4_), channel_id=1, source_target_pairs={{0,1},{1,0},{2,3},{3,2},{4,5},{5,4},{6,7},{7,6},{8,9},{9,8},{10,11... | collective-permute-start | bytes 3538952 | tf_op jit(solution)/shard_map/ppermute | solution.py:693
  54.9 3.0 %collective-permute-start.14 = (bf16[768,768]{1,0:T(8,128)(2,1)S(1)}, bf16[768,768]{1,0:T(8,128)(2,1)S(1)}, u32[]{:S(2)}, u32[]{:S(2)}) collective-permute-start(bf16[768,768]{1,0:T(8,128)(2,1)S(1)} %join.5.refs_2_.refs_5_), channel_id=1, source_target_pairs={{0,1},{1,0},{2,3},{3,2},{4,5},{5,4},{6,7},{7,6},{8,9},{9,8},{10,11... | collective-permute-start | bytes 3538952 | tf_op jit(solution)/shard_map/ppermute | solution.py:693
  62.9 4.6 %collective-permute-start.15 = (bf16[768,768]{1,0:T(8,128)(2,1)S(1)}, bf16[768,768]{1,0:T(8,128)(2,1)S(1)}, u32[]{:S(2)}, u32[]{:S(2)}) collective-permute-start(bf16[768,768]{1,0:T(8,128)(2,1)S(1)} %get-tuple-element.230), channel_id=1, source_target_pairs={{0,1},{1,0},{2,3},{3,2},{4,5},{5,4},{6,7},{7,6},{8,9},{9,8},{10,11... | collective-permute-start | bytes 3538952 | tf_op jit(solution)/shard_map/ppermute | solution.py:693
  64.7 2.9 %collective-permute-start.16 = (bf16[768,768]{1,0:T(8,128)(2,1)S(1)}, bf16[768,768]{1,0:T(8,128)(2,1)S(1)}, u32[]{:S(2)}, u32[]{:S(2)}) collective-permute-start(bf16[768,768]{1,0:T(8,128)(2,1)S(1)} %get-tuple-element.232), channel_id=1, source_target_pairs={{0,1},{1,0},{2,3},{3,2},{4,5},{5,4},{6,7},{7,6},{8,9},{9,8},{10,11... | collective-permute-start | bytes 3538952 | tf_op jit(solution)/shard_map/ppermute | solution.py:693
  67.0 5.7 %collective-permute-start.17 = (bf16[768,768]{1,0:T(8,128)(2,1)S(1)}, bf16[768,768]{1,0:T(8,128)(2,1)S(1)}, u32[]{:S(2)}, u32[]{:S(2)}) collective-permute-start(bf16[768,768]{1,0:T(8,128)(2,1)S(1)} %get-tuple-element.236), channel_id=1, source_target_pairs={{0,1},{1,0},{2,3},{3,2},{4,5},{5,4},{6,7},{7,6},{8,9},{9,8},{10,11... | collective-permute-start | bytes 3538952 | tf_op jit(solution)/shard_map/ppermute | solution.py:693
  69.1 16.3 %collective-permute-start.18 = (bf16[768,768]{1,0:T(8,128)(2,1)S(1)}, bf16[768,768]{1,0:T(8,128)(2,1)S(1)}, u32[]{:S(2)}, u32[]{:S(2)}) collective-permute-start(bf16[768,768]{1,0:T(8,128)(2,1)S(1)} %get-tuple-element.239), channel_id=1, source_target_pairs={{0,2},{1,5},{2,0},{3,7},{4,6},{5,1},{6,4},{7,3},{8,10},{9,13},{10,... | collective-permute-start | bytes 3538952 | tf_op jit(solution)/shard_map/ppermute | solution.py:693
  75.9 16.6 %collective-permute-start.20 = (bf16[768,768]{1,0:T(8,128)(2,1)S(1)}, bf16[768,768]{1,0:T(8,128)(2,1)S(1)}, u32[]{:S(2)}, u32[]{:S(2)}) collective-permute-start(bf16[768,768]{1,0:T(8,128)(2,1)S(1)} %get-tuple-element.263), channel_id=1, source_target_pairs={{0,1},{1,0},{2,3},{3,2},{4,5},{5,4},{6,7},{7,6},{8,9},{9,8},{10,11... | collective-permute-start | bytes 3538952 | tf_op jit(solution)/shard_map/ppermute | solution.py:693
  80.7 11.7 %collective-permute-start.21 = (bf16[2,192,768]{2,1,0:T(8,128)(2,1)S(1)}, bf16[2,192,768]{2,1,0:T(8,128)(2,1)S(1)}, u32[]{:S(2)}, u32[]{:S(2)}) collective-permute-start(bf16[2,192,768]{2,1,0:T(8,128)(2,1)S(1)} %get-tuple-element.264), channel_id=1, source_target_pairs={{0,1},{1,0},{2,3},{3,2},{4,5},{5,4},{6,7},{7,6},{8,9},{9,8},{10,11... | collective-permute-start | bytes 1769480 | tf_op jit(solution)/shard_map/ppermute | solution.py:693
  86.3 9.9 %collective-permute-start.19 = (bf16[384,768]{1,0:T(8,128)(2,1)S(1)}, bf16[384,768]{1,0:T(8,128)(2,1)S(1)}, u32[]{:S(2)}, u32[]{:S(2)}) collective-permute-start(bf16[384,768]{1,0:T(8,128)(2,1)S(1)} %get-tuple-element.257), channel_id=1, source_target_pairs={{0,4},{1,3},{2,6},{3,1},{4,0},{5,7},{6,2},{7,5},{8,12},{9,11},{10,... | collective-permute-start | bytes 1769480 | tf_op jit(solution)/shard_map/ppermute | solution.py:693
  86.6 5.8 %copy-start.9 = (bf16[768,768]{1,0:T(8,128)(2,1)S(1)}, bf16[768,768]{1,0:T(8,128)(2,1)}, u32[]{:S(2)}) copy-start(bf16[768,768]{1,0:T(8,128)(2,1)} %copy-done.8) | copy-start | bytes 3538948
  92.0 12.1 %collective-permute-start.22 = (bf16[576,768]{1,0:T(8,128)(2,1)S(1)}, bf16[576,768]{1,0:T(8,128)(2,1)S(1)}, u32[]{:S(2)}, u32[]{:S(2)}) collective-permute-start(bf16[576,768]{1,0:T(8,128)(2,1)S(1)} %get-tuple-element.265), channel_id=1, source_target_pairs={{0,1},{1,0},{2,3},{3,2},{4,5},{5,4},{6,7},{7,6},{8,9},{9,8},{10,11... | collective-permute-start | bytes 2654216 | tf_op jit(solution)/shard_map/ppermute | solution.py:693
  92.4 6.2 %copy-start.31 = (bf16[576,512]{1,0:T(8,128)(2,1)S(1)}, bf16[576,512]{1,0:T(8,128)(2,1)}, u32[]{:S(2)}) copy-start(bf16[576,512]{1,0:T(8,128)(2,1)} %copy-done.30) | copy-start | bytes 1769476
  94.0 4.6 %copy-start.3 = (bf16[784,768]{1,0:T(8,128)(2,1)S(1)}, bf16[784,768]{1,0:T(8,128)(2,1)}, u32[]{:S(2)}) copy-start(bf16[784,768]{1,0:T(8,128)(2,1)} %copy-done.2) | copy-start | bytes 3612676
  94.1 19.4 %collective-permute-start.24 = (bf16[960,768]{1,0:T(8,128)(2,1)S(1)}, bf16[960,768]{1,0:T(8,128)(2,1)S(1)}, u32[]{:S(2)}, u32[]{:S(2)}) collective-permute-start(bf16[960,768]{1,0:T(8,128)(2,1)S(1)} %get-tuple-element.267), channel_id=1, source_target_pairs={{0,2},{1,5},{2,0},{3,7},{4,6},{5,1},{6,4},{7,3},{8,10},{9,13},{10,... | collective-permute-start | bytes 4423688 | tf_op jit(solution)/shard_map/ppermute | solution.py:693
  97.0 19.1 %collective-permute-start.23 = (bf16[192,768]{1,0:T(8,128)(2,1)S(1)}, bf16[192,768]{1,0:T(8,128)(2,1)S(1)}, u32[]{:S(2)}, u32[]{:S(2)}) collective-permute-start(bf16[192,768]{1,0:T(8,128)(2,1)S(1)} %get-tuple-element.269), channel_id=1, source_target_pairs={{0,8},{1,17},{2,10},{3,19},{4,12},{5,21},{6,14},{7,23},{8,0},{9,25... | collective-permute-start | bytes 884744 | tf_op jit(solution)/shard_map/ppermute | solution.py:693
  98.7 5.4 %copy-start.15 = (bf16[784,768]{1,0:T(8,128)(2,1)S(1)}, bf16[784,768]{1,0:T(8,128)(2,1)}, u32[]{:S(2)}) copy-start(bf16[784,768]{1,0:T(8,128)(2,1)} %copy-done.14) | copy-start | bytes 3612676
  98.7 5.4 %copy-start.29 = (bf16[576,512]{1,0:T(8,128)(2,1)S(1)}, bf16[576,512]{1,0:T(8,128)(2,1)}, u32[]{:S(2)}) copy-start(bf16[576,512]{1,0:T(8,128)(2,1)} %copy-done.28) | copy-start | bytes 1769476
  109.5 15.4 %collective-permute-start.25 = (bf16[576,768]{1,0:T(8,128)(2,1)S(1)}, bf16[576,768]{1,0:T(8,128)(2,1)S(1)}, u32[]{:S(2)}, u32[]{:S(2)}) collective-permute-start(bf16[576,768]{1,0:T(8,128)(2,1)S(1)} %get-tuple-element.281), channel_id=1, source_target_pairs={{0,1},{1,0},{2,3},{3,2},{4,5},{5,4},{6,7},{7,6},{8,9},{9,8},{10,11... | collective-permute-start | bytes 2654216 | tf_op jit(solution)/shard_map/ppermute | solution.py:693
  113.5 5.9 %copy-start.13 = (bf16[784,768]{1,0:T(8,128)(2,1)S(1)}, bf16[784,768]{1,0:T(8,128)(2,1)}, u32[]{:S(2)}) copy-start(bf16[784,768]{1,0:T(8,128)(2,1)} %get-tuple-element.185.refs_1_.weights) | copy-start | bytes 3612676
  113.5 5.9 %copy-start.27 = (bf16[3,512,512]{2,1,0:T(8,128)(2,1)S(1)}, bf16[3,512,512]{2,1,0:T(8,128)(2,1)}, u32[]{:S(2)}) copy-start(bf16[3,512,512]{2,1,0:T(8,128)(2,1)} %copy-done.26) | copy-start | bytes 4718596
  113.5 5.9 %copy-start.33 = (bf16[576,512]{1,0:T(8,128)(2,1)S(1)}, bf16[576,512]{1,0:T(8,128)(2,1)}, u32[]{:S(2)}) copy-start(bf16[576,512]{1,0:T(8,128)(2,1)} %copy-done.32) | copy-start | bytes 1769476
  114.6 11.5 %collective-permute-start.27 = (bf16[480,768]{1,0:T(8,128)(2,1)S(1)}, bf16[480,768]{1,0:T(8,128)(2,1)S(1)}, u32[]{:S(2)}, u32[]{:S(2)}) collective-permute-start(bf16[480,768]{1,0:T(8,128)(2,1)S(1)} %get-tuple-element.283), channel_id=1, source_target_pairs={{0,4},{1,3},{2,6},{3,1},{4,0},{5,7},{6,2},{7,5},{8,12},{9,11},{10,... | collective-permute-start | bytes 2211848 | tf_op jit(solution)/shard_map/ppermute | solution.py:693
  116.8 8.1 %collective-permute-start.26 = (bf16[96,768]{1,0:T(8,128)(2,1)S(1)}, bf16[96,768]{1,0:T(8,128)(2,1)S(1)}, u32[]{:S(2)}, u32[]{:S(2)}) collective-permute-start(bf16[96,768]{1,0:T(8,128)(2,1)S(1)} %get-tuple-element.285), channel_id=1, source_target_pairs={{0,16},{1,9},{2,18},{3,11},{4,20},{5,13},{6,22},{7,15},{8,24},{9,1... | collective-permute-start | bytes 442376 | tf_op jit(solution)/shard_map/ppermute | solution.py:693
  127.3 14.8 %collective-permute-start.28 = (bf16[608,768]{1,0:T(8,128)(2,1)S(1)}, bf16[608,768]{1,0:T(8,128)(2,1)S(1)}, u32[]{:S(2)}, u32[]{:S(2)}) collective-permute-start(bf16[608,768]{1,0:T(8,128)(2,1)S(1)} %get-tuple-element.303), channel_id=1, source_target_pairs={{0,2},{1,5},{2,0},{3,7},{4,6},{5,1},{6,4},{7,3},{8,10},{9,13},{10,... | collective-permute-start | bytes 2801672 | tf_op jit(solution)/shard_map/ppermute | solution.py:693
  128.9 13.3 %collective-permute-start.29 = (bf16[96,768]{1,0:T(8,128)(2,1)S(1)}, bf16[96,768]{1,0:T(8,128)(2,1)S(1)}, u32[]{:S(2)}, u32[]{:S(2)}) collective-permute-start(bf16[96,768]{1,0:T(8,128)(2,1)S(1)} %add_convert_fusion.1), channel_id=1, source_target_pairs={{0,16},{1,9},{2,18},{3,11},{4,20},{5,13},{6,22},{7,15},{8,24},{9,1... | collective-permute-start | bytes 442376 | tf_op jit(solution)/shard_map/ppermute | solution.py:693
  132.6 13.9 %collective-permute-start.32 = (bf16[240,768]{1,0:T(8,128)(2,1)S(1)}, bf16[240,768]{1,0:T(8,128)(2,1)S(1)}, u32[]{:S(2)}, u32[]{:S(2)}) collective-permute-start(bf16[240,768]{1,0:T(8,128)(2,1)S(1)} %get-tuple-element.306), channel_id=1, source_target_pairs={{0,8},{1,17},{2,10},{3,19},{4,12},{5,21},{6,14},{7,23},{8,0},{9,25... | collective-permute-start | bytes 1105928 | tf_op jit(solution)/shard_map/ppermute | solution.py:693
  143.1 15.8 %collective-permute-start.30 = (bf16[320,768]{1,0:T(8,128)(2,1)S(1)}, bf16[320,768]{1,0:T(8,128)(2,1)S(1)}, u32[]{:S(2)}, u32[]{:S(2)}) collective-permute-start(bf16[320,768]{1,0:T(8,128)(2,1)S(1)} %get-tuple-element.311), channel_id=1, source_target_pairs={{0,4},{1,3},{2,6},{3,1},{4,0},{5,7},{6,2},{7,5},{8,12},{9,11},{10,... | collective-permute-start | bytes 1474568 | tf_op jit(solution)/shard_map/ppermute | solution.py:693
  144.0 14.8 %collective-permute-start.31 = (bf16[192,768]{1,0:T(8,128)(2,1)S(1)}, bf16[192,768]{1,0:T(8,128)(2,1)S(1)}, u32[]{:S(2)}, u32[]{:S(2)}) collective-permute-start(bf16[192,768]{1,0:T(8,128)(2,1)S(1)} %pad_maximum_fusion.5), channel_id=1, source_target_pairs={{0,8},{1,17},{2,10},{3,19},{4,12},{5,21},{6,14},{7,23},{8,0},{9,25... | collective-permute-start | bytes 884744 | tf_op jit(solution)/shard_map/ppermute | solution.py:693
  147.2 12.5 %collective-permute-start.34 = (bf16[120,768]{1,0:T(8,128)(2,1)S(1)}, bf16[120,768]{1,0:T(8,128)(2,1)S(1)}, u32[]{:S(2)}, u32[]{:S(2)}) collective-permute-start(bf16[120,768]{1,0:T(8,128)(2,1)S(1)} %get-tuple-element.314), channel_id=1, source_target_pairs={{0,16},{1,9},{2,18},{3,11},{4,20},{5,13},{6,22},{7,15},{8,24},{9,1... | collective-permute-start | bytes 552968 | tf_op jit(solution)/shard_map/ppermute | solution.py:693
  159.6 11.7 %collective-permute-start.33 = (bf16[176,768]{1,0:T(8,128)(2,1)S(1)}, bf16[176,768]{1,0:T(8,128)(2,1)S(1)}, u32[]{:S(2)}, u32[]{:S(2)}) collective-permute-start(bf16[176,768]{1,0:T(8,128)(2,1)S(1)} %get-tuple-element.319), channel_id=1, source_target_pairs={{0,8},{1,17},{2,10},{3,19},{4,12},{5,21},{6,14},{7,23},{8,0},{9,25... | collective-permute-start | bytes 811016 | tf_op jit(solution)/shard_map/ppermute | solution.py:693
  159.7 12.3 %collective-permute-start.36 = (bf16[120,768]{1,0:T(8,128)(2,1)S(1)}, bf16[120,768]{1,0:T(8,128)(2,1)S(1)}, u32[]{:S(2)}, u32[]{:S(2)}) collective-permute-start(bf16[120,768]{1,0:T(8,128)(2,1)S(1)} %add_convert_fusion), channel_id=1, source_target_pairs={{0,16},{1,9},{2,18},{3,11},{4,20},{5,13},{6,22},{7,15},{8,24},{9,1... | collective-permute-start | bytes 552968 | tf_op jit(solution)/shard_map/ppermute | solution.py:693
  161.8 21.9 %collective-permute-start.38 = (bf16[384,768]{1,0:T(8,128)(2,1)S(1)}, bf16[384,768]{1,0:T(8,128)(2,1)S(1)}, u32[]{:S(2)}, u32[]{:S(2)}) collective-permute-start(bf16[384,768]{1,0:T(8,128)(2,1)S(1)} %pad_maximum_fusion.2.mine), channel_id=1, source_target_pairs={{0,4},{1,5},{2,6},{3,7},{4,0},{5,1},{6,2},{7,3},{8,12},{9,13},{10,... | collective-permute-start | bytes 1769480 | tf_op jit(solution)/shard_map/ppermute | solution.py:693
  171.9 8.6 %collective-permute-start.35 = (bf16[104,768]{1,0:T(8,128)(2,1)S(1)}, bf16[104,768]{1,0:T(8,128)(2,1)S(1)}, u32[]{:S(2)}, u32[]{:S(2)}) collective-permute-start(bf16[104,768]{1,0:T(8,128)(2,1)S(1)} %get-tuple-element.325), channel_id=1, source_target_pairs={{0,16},{1,9},{2,18},{3,11},{4,20},{5,13},{6,22},{7,15},{8,24},{9,1... | collective-permute-start | bytes 479240 | tf_op jit(solution)/shard_map/ppermute | solution.py:693
  172.1 11.4 %collective-permute-start.39 = (bf16[240,768]{1,0:T(8,128)(2,1)S(1)}, bf16[240,768]{1,0:T(8,128)(2,1)S(1)}, u32[]{:S(2)}, u32[]{:S(2)}) collective-permute-start(bf16[240,768]{1,0:T(8,128)(2,1)S(1)} %pad_maximum_fusion.4), channel_id=1, source_target_pairs={{0,8},{1,17},{2,10},{3,19},{4,12},{5,21},{6,14},{7,23},{8,0},{9,25... | collective-permute-start | bytes 1105928 | tf_op jit(solution)/shard_map/ppermute | solution.py:693
  180.6 9.0 %copy-start.34 = (bf16[72,768]{1,0:T(8,128)(2,1)}, bf16[72,768]{1,0:T(8,128)(2,1)S(1)}, u32[]{:S(2)}) copy-start(bf16[72,768]{1,0:T(8,128)(2,1)S(1)} %add_convert_fusion.2) | copy-start | bytes 331780
  180.6 9.0 %collective-permute-start.37 = (bf16[72,768]{1,0:T(8,128)(2,1)S(1)}, bf16[72,768]{1,0:T(8,128)(2,1)S(1)}, u32[]{:S(2)}, u32[]{:S(2)}) collective-permute-start(bf16[72,768]{1,0:T(8,128)(2,1)S(1)} %add_convert_fusion.2), channel_id=1, source_target_pairs={{0,16},{1,9},{2,18},{3,11},{4,20},{5,13},{6,22},{7,15},{8,24},{9,1... | collective-permute-start | bytes 331784 | tf_op jit(solution)/shard_map/ppermute | solution.py:693
  183.5 17.4 %collective-permute-start.43 = (bf16[480,768]{1,0:T(8,128)(2,1)S(1)}, bf16[480,768]{1,0:T(8,128)(2,1)S(1)}, u32[]{:S(2)}, u32[]{:S(2)}) collective-permute-start(bf16[480,768]{1,0:T(8,128)(2,1)S(1)} %pad_maximum_fusion.mine), channel_id=1, source_target_pairs={{0,4},{1,5},{2,6},{3,7},{4,0},{5,1},{6,2},{7,3},{8,12},{9,13},{10,... | collective-permute-start | bytes 2211848 | tf_op jit(solution)/shard_map/ppermute | solution.py:693
  189.6 6.0 %collective-permute-start.40 = (bf16[144,768]{1,0:T(8,128)(2,1)S(1)}, bf16[144,768]{1,0:T(8,128)(2,1)S(1)}, u32[]{:S(2)}, u32[]{:S(2)}) collective-permute-start(bf16[144,768]{1,0:T(8,128)(2,1)S(1)} %pad_maximum_fusion.6), channel_id=1, source_target_pairs={{0,8},{1,17},{2,10},{3,19},{4,12},{5,21},{6,14},{7,23},{8,0},{9,25... | collective-permute-start | bytes 663560 | tf_op jit(solution)/shard_map/ppermute | solution.py:693
  190.2 1.4 collective-permute-start.41
  197.4 10.8 %collective-permute-start.42 = (bf16[288,768]{1,0:T(8,128)(2,1)S(1)}, bf16[288,768]{1,0:T(8,128)(2,1)}, u32[]{:S(2)}, u32[]{:S(2)}) collective-permute-start(bf16[288,768]{1,0:T(8,128)(2,1)S(1)} %pad_maximum_fusion.3.mine), channel_id=1, source_target_pairs={{0,4},{1,5},{2,6},{3,7},{4,0},{5,1},{6,2},{7,3},{8,12},{9,13},{10,... | collective-permute-start | bytes 1327112 | tf_op jit(solution)/shard_map/ppermute | solution.py:693
  (19 other events, 36.8 us)
